TPU v7x, 512 devices: a whole 4x8x8 slice. The times are simulated.
512 devices in a mesh: dp: 32 (over z, y_lo), seq: 16 (over x, y_hi, core).
Axes of the slice: x: 4, y: 8 (y_hi: 2, y_lo: 4; y = y_hi * 4 + y_lo), z: 8, core: 2. Of those that a mesh axis runs over, the one named last changes fastest.
Arguments:
- bases: int32 [32, 24576], P('dp', 'seq'), may hold values from 0 to 3
- embed_weight: bfloat16 [15, 4, 768], P(None, None, 'dp'), may hold values from -1.5 to 1.5
- embed_bias: bfloat16 [768], P('dp'), may hold values from -3 to 3
- norm_gain: bfloat16 [768], P('dp'), may hold values from 0.5 to 1.5
- proj_weight: bfloat16 [768, 896], P('dp'), may hold values from -0.21875 to 0.21875
- proj_bias: bfloat16 [896], P('dp'), may hold values from -3 to 3
- cotangent: bfloat16 [32, 12288, 896], P('dp', 'seq'), may hold values from -6 to 6
Outputs:
- pooled: bfloat16 [32, 12288, 896], P('dp', 'seq')
- grad_embed_weight: float32 [15, 4, 768], P(None, None, 'dp')
- grad_embed_bias: float32 [768], P('dp')
- grad_norm_gain: float32 [768], P('dp')
- grad_proj_weight: float32 [768, 896], P('dp')
- grad_proj_bias: float32 [896], P('dp')
All inputs are finite; a program needn't handle non-finite values.
Results may differ from a plain program's by a relative error of at most 0.0065.
Values may be sent and summed in bfloat16 or wider, within the bound.
No kernel may reach another device: no remote copies, remote signals or barrier semaphores. Data moves between devices by JAX's collectives and lax.ppermute only.
A program may use at most 64 MiB of HBM per device.

v0:
```python
import jax
import jax.numpy as jnp
from jax import lax
from jax.sharding import PartitionSpec as P


def with_halo(x, sides, width):
    for axis, dim in sides:
        devices, length = (lax.axis_size(axis), x.shape[dim])
        up = [(i, (i + 1) % devices) for i in range(devices - 1)]
        down = [(j, i) for i, j in up]
        last = lax.slice_in_dim(x, length - width, length, axis=dim)
        leading = lax.slice_in_dim(x, 0, width, axis=dim)
        before = lax.ppermute(last, axis, up)
        after = lax.ppermute(leading, axis, down)
        x = jnp.concatenate([before, x, after], axis=dim)
    return x


def local(bases, embed_weight, embed_bias, norm_gain, proj_weight, proj_bias, cotangent):
    kernel_width = embed_weight.shape[0]
    row_count = bases.shape[1]
    codes = bases + 1
    padded = with_halo(codes, (("seq", 1),), kernel_width // 2)[0]
    full_embed, full_bias, full_gain, full_proj, full_proj_bias = (
        lax.all_gather(embed_weight, "dp", axis=2, tiled=True),
        lax.all_gather(embed_bias, "dp", axis=0, tiled=True),
        lax.all_gather(norm_gain, "dp", axis=0, tiled=True),
        lax.all_gather(proj_weight, "dp", axis=0, tiled=True),
        lax.all_gather(proj_bias, "dp", axis=0, tiled=True),
    )
    letters = jnp.arange(1, 5, dtype=jnp.int32)
    features = jnp.concatenate(
        [
            (padded[k : k + row_count, None] == letters).astype(jnp.bfloat16)
            for k in range(kernel_width)
        ],
        axis=1,
    )
    flat_weight = full_embed.reshape(kernel_width * 4, -1)
    embedded = (
        jnp.dot(features, flat_weight, preferred_element_type=jnp.float32)
        + full_bias.astype(jnp.float32)
    ).astype(jnp.bfloat16)
    values = embedded.astype(jnp.float32)
    inverse = lax.rsqrt(jnp.mean(values * values, axis=1, keepdims=True) + 1e-06)
    scaled = values * inverse
    normed = scaled * full_gain.astype(jnp.float32)
    activated = jax.nn.gelu(normed, approximate=True).astype(jnp.bfloat16)
    product = jnp.dot(activated, full_proj, preferred_element_type=jnp.float32)
    mixed = product + full_proj_bias.astype(jnp.float32)
    pooled = jnp.mean(mixed.reshape(row_count // 2, 2, -1), axis=1).astype(jnp.bfloat16)
    scale_factor = 0.5 / (row_count * lax.axis_size("seq") * lax.axis_size("dp"))
    grad_mixed = (jnp.repeat(cotangent[0].astype(jnp.float32), 2, axis=0) * scale_factor).astype(
        jnp.bfloat16
    )
    grad_proj_weight = lax.dot_general(
        activated, grad_mixed, (((0,), (0,)), ((), ())), preferred_element_type=jnp.float32
    )
    grad_proj_bias = jnp.sum(grad_mixed.astype(jnp.float32), axis=0)
    grad_activated = lax.dot_general(
        grad_mixed, full_proj, (((1,), (1,)), ((), ())), preferred_element_type=jnp.float32
    )
    _, pullback = jax.vjp(lambda v: jax.nn.gelu(v, approximate=True), normed)
    grad_normed = pullback(grad_activated)[0]
    grad_norm_gain = jnp.sum(grad_normed * scaled, axis=0)
    weighted = grad_normed * full_gain.astype(jnp.float32)
    grad_embedded = (
        inverse * (weighted - scaled * jnp.mean(weighted * scaled, axis=1, keepdims=True))
    ).astype(jnp.bfloat16)
    grad_embed_weight = lax.dot_general(
        features, grad_embedded, (((0,), (0,)), ((), ())), preferred_element_type=jnp.float32
    ).reshape(kernel_width, 4, -1)
    grad_embed_bias = jnp.sum(grad_embedded.astype(jnp.float32), axis=0)
    whole = lax.psum(
        (grad_embed_weight, grad_embed_bias, grad_norm_gain, grad_proj_weight, grad_proj_bias),
        "seq",
    )
    results = (
        lax.psum_scatter(whole[0], "dp", scatter_dimension=2, tiled=True),
        lax.psum_scatter(whole[1], "dp", scatter_dimension=0, tiled=True),
        lax.psum_scatter(whole[2], "dp", scatter_dimension=0, tiled=True),
        lax.psum_scatter(whole[3], "dp", scatter_dimension=0, tiled=True),
        lax.psum_scatter(whole[4], "dp", scatter_dimension=0, tiled=True),
    )
    return (pooled[None], results[0], results[1], results[2], results[3], results[4])


def solution(mesh):
    placed = (
        P("dp", "seq"),
        P(None, None, "dp"),
        P("dp"),
        P("dp"),
        P("dp", None),
        P("dp"),
        P("dp", "seq", None),
    )
    return jax.shard_map(
        local,
        mesh=mesh,
        in_specs=placed,
        out_specs=(
            P("dp", "seq", None),
            P(None, None, "dp"),
            P("dp"),
            P("dp"),
            P("dp", None),
            P("dp"),
        ),
        check_vma=False,
    )
```

profile of v0, /device:TPU:1, one launch (start us, length us, event | category | flops | bytes accessed | tf_op | source)
XLA Modules:
  0.0 875.5 jit_solution(2991489569043815438)
XLA Ops:
  8.7 8.8 %collective-permute-start.1 = (s32[1,7]{1,0:T(1,128)S(1)}, s32[1,7]{1,0:T(1,128)S(1)}, u32[]{:S(2)}, u32[]{:S(2)}) collective-permute-start(s32[1,7]{1,0:T(1,128)S(1)} %get-tuple-element.39), channel_id=1, source_target_pairs={{1,0},{2,1},{3,2},{4,3},{5,4},{6,5},{7,6},{8,7},{9,8},{10,9},{11,1... | collective-permute-start | bytes 92 | tf_op jit(solution)/shard_map/ppermute | solution.py:15
  17.5 2.0 collective-permute-start
  19.5 1.4 fusion.57
  24.7 75.1 %all-reduce.10 = (bf16[896]{0:T(1024)(128)(2,1)}, bf16[768]{0:T(1024)(128)(2,1)S(1)}, bf16[768]{0:T(1024)(128)(2,1)S(1)}) all-reduce(bf16[896]{0:T(1024)(128)(2,1)S(1)} %dynamic-update-slice.2, bf16[768]{0:T(1024)(128)(2,1)S(1)} %dynamic-update-slice, bf16[768]{0:T(1024)(128)(2,1)S(1)} %dynamic-update-slice.1), channel_id=1, replica_groups=mesh['dp'=32,'seq'=16] {'dp'}, use_global_device_ids=true, to_apply=%add.2 | all-reduce | flops 2432 | bytes 9728
  100.7 69.9 %all_gather.15 = bf16[15,4,768]{0,1,2:T(4,128)(2,1)S(1)} all-gather(bf16[15,4,24]{0,1,2:T(4,128)(2,1)S(1)} %copy.16), channel_id=1, replica_groups=mesh['dp'=32,'seq'=16] {'dp'}, dimensions={2}, use_global_device_ids=true | all-gather | bytes 95040 | tf_op jit(solution)/shard_map/all_gather | solution.py:26
  171.8 1.7 fusion.50
  173.4 3.0 broadcast_in_dim.4
  176.4 6.8 convert_element_type.87
  183.7 5.0 broadcast_compare_fusion
  188.7 6.3 concatenate.27
  195.0 1.8 fusion.17
  196.9 1.4 copy-done
  198.3 6.7 fusion.51
  206.9 8.5 fusion.16
  215.4 1.5 convert_reduce_fusion
  218.2 126.2 %all-reduce.8 = (f32[768]{0:T(1024)S(1)}, f32[768]{0:T(1024)S(1)}, f32[896]{0:T(1024)S(1)}) all-reduce(f32[768]{0:T(1024)S(1)} %get-tuple-element.32, f32[768]{0:T(1024)S(1)} %get-tuple-element.6, f32[896]{0:T(1024)S(1)} %broadcast_reduce_fusion), channel_id=3, replica_groups=mesh['dp'=32,'seq'=16] {'dp'}, use_global_device_ids=true, to_apply=%region_7.0.clone | all-reduce | flops 2432 | bytes 19456
  344.6 6.7 convolution_add_fusion
  351.3 7.6 reshape.112
  359.3 9.1 %reduce_sum.55 = f32[768,896]{1,0:T(8,128)S(1)} reduce(f32[768,2,896]{2,1,0:T(2,128)} %reshape.112, f32[]{:T(128)} %constant.4.clone.1), dimensions={1}, to_apply=%region_1.0 | reduce | flops 688128 | bytes 8257540 | tf_op jit(solution)/shard_map/reduce_sum | solution.py:52
  369.7 1.4 reduce-scatter.6.cloned.1.call-done
  371.1 302.5 %all-reduce.16.cloned.1.call-done = f32[15,4,768]{2,1,0:T(4,128)} async-done(((f32[15,4,768]{2,1,0:T(4,128)}), f32[15,4,768]{2,1,0:T(4,128)}) %all-reduce.16.cloned.1.call-update) | async-done | bytes 184336
  674.6 94.5 %all-reduce.9 = (f32[15,4,24]{2,1,0:T(4,128)}, f32[24]{0:T(128)}, f32[24]{0:T(128)}, f32[28]{0:T(128)}) all-reduce(f32[15,4,24]{2,1,0:T(4,128)S(1)} %constant_dynamic-slice_fusion, f32[24]{0:T(128)S(1)} %dynamic-slice.6, f32[24]{0:T(128)S(1)} %dynamic-slice.8, f32[28]{0:T(128)S(1)} %dynamic-slice.12), channel_id=1, replica_groups=mesh['dp'=32,'seq'=16] {'seq'}, use_global_device_ids=true, to_apply=%region_3.0 | all-reduce | flops 1516 | bytes 12128 | tf_op jit(solution)/shard_map/psum | solution.py:75
  769.0 98.4 %all-reduce.14.cloned.1.call-done = f32[24,896]{1,0:T(8,128)} async-done(((f32[24,896]{1,0:T(8,128)}), f32[24,896]{1,0:T(8,128)}) %all-reduce.14.cloned.1.call-update) | async-done | bytes 86032 | tf_op jit(solution)/shard_map/psum | solution.py:75
  867.4 1.5 copy.42
  (46 shorter events, 11.1 us)
Async XLA Ops:
  7.2 199.7 %all-gather.2.cloned.1.call-start = ((), (), s32[]{:S(2)}) async-start(), calls=%async_computation.1 | async-start | bytes 1419264 | tf_op jit(solution)/shard_map/all_gather | solution.py:29
  7.9 363.2 %reduce-scatter.6.cloned.1.call-start = ((), (), s32[]{:S(2)}) async-start(), calls=%async_computation.4 | async-start | bytes 2838528
  8.7 174.5 %collective-permute-start.1 = (s32[1,7]{1,0:T(1,128)S(1)}, s32[1,7]{1,0:T(1,128)S(1)}, u32[]{:S(2)}, u32[]{:S(2)}) collective-permute-start(s32[1,7]{1,0:T(1,128)S(1)} %get-tuple-element.39), channel_id=1, source_target_pairs={{1,0},{2,1},{3,2},{4,3},{5,4},{6,5},{7,6},{8,7},{9,8},{10,9},{11,1... | collective-permute-start | bytes 92 | tf_op jit(solution)/shard_map/ppermute | solution.py:15
  17.5 165.7 %collective-permute-start = (s32[1,7]{1,0:T(1,128)S(1)}, s32[1,7]{1,0:T(1,128)S(1)}, u32[]{:S(2)}, u32[]{:S(2)}) collective-permute-start(s32[1,7]{1,0:T(1,128)S(1)} %get-tuple-element.40), channel_id=1, source_target_pairs={{0,1},{1,2},{2,3},{3,4},{4,5},{5,6},{6,7},{7,8},{8,9},{9,10},{10,1... | collective-permute-start | bytes 92 | tf_op jit(solution)/shard_map/ppermute | solution.py:14
  196.8 1.4 copy-start
  198.3 8.3 copy-start.3
  205.0 468.6 %all-reduce.16.cloned.1.call-start = ((), (), s32[]{:S(2)}) async-start(), calls=%async_computation.3 | async-start | bytes 368640
  206.8 8.5 copy-start.1
  215.3 1.5 copy-start.2
  359.0 508.4 %all-reduce.14.cloned.1.call-start = ((), (), s32[]{:S(2)}) async-start(), calls=%async_computation.2 | async-start | bytes 172032 | tf_op jit(solution)/shard_map/psum | solution.py:75
Sparse Core Ops, SparseCore 0:
  10.1 141.4 all-gather.1
  205.1 165.9 reduce-scatter.5
  374.0 299.5 all-reduce.15
  676.7 190.7 all-reduce.13
where the time goes:
time: 877 us; the launch traced here: 875 us
  waiting for transfers between devices  403 us (46%)
  blocking collectives  366 us (42%)
  local copies, waits for them, and re-layouts  34.5 us (4%)
  matrix products  24.3 us (3%)
  other arithmetic  20 us (2%)
  between operations  16.5 us (2%)
  starting transfers between devices  11.3 us (1%)
    unnamed x6, waiting for transfers between devices  305 us
    unnamed x2, blocking collectives  201 us
    psum x1, waiting for transfers between devices, local(): lax.psum((grad_embed_weight, grad_embed_bias, grad_norm_gain, grad_proj_w...  98.4 us
    psum x1, blocking collectives, local(): lax.psum((grad_embed_weight, grad_embed_bias, grad_norm_gain, grad_proj_w...  94.5 us
    all_gather x1, blocking collectives, local(): lax.all_gather(embed_weight, 'dp', axis=2, tiled=True)  69.9 us
  transfers between devices with their start and end apart: 6, of which 3 were waited for; matrix products, arithmetic and copies ran while one was open for 9% of the time, Pallas kernels for 0%

commit v1 on v0

v1 whole, which is shorter than its diff:
```python
import functools

import jax
import jax.numpy as jnp
from jax import lax
from jax.experimental import pallas as pl
from jax.experimental.pallas import tpu as pltpu
from jax.sharding import PartitionSpec as P

F32, BF16 = jnp.float32, jnp.bfloat16
LANES = 128
GELU_A = 0.7978845608028654
GELU_B = 0.044715
EPSILON = 1e-06


def dot(a, b, contract, precision=None):
    return lax.dot_general(a, b, ((contract[:1], contract[1:]), ((), ())), precision=precision, preferred_element_type=F32)


def iota(shape, dim):
    return lax.broadcasted_iota(jnp.int32, shape, dim)


def step_kernel(dims, core_ref, before_ref, bases_ref, after_ref, own_ref, other_ref, cot_ref,
                pooled_ref, mine_ref, theirs_ref,
                w_ref, code_ref, perm_ref, feat_ref, we_ref, wide_ref, emb_ref, ga_ref, s_ref, ge_ref, gew_ref):
    kw, shards, d0, d1, rows, tile, chunk = dims
    half = w_ref.shape[1] // 2
    pairs, pair_tile = rows // 2, tile // 2
    reach = kw // 2
    taps = kw * 4
    core = core_ref[0]
    per = d1 // shards
    block = d0 // shards

    @pl.when(core == 0)
    def _():
        w_ref[:, :half] = own_ref[...]
        w_ref[:, half:] = other_ref[...]

    @pl.when(core != 0)
    def _():
        w_ref[:, :half] = other_ref[...]
        w_ref[:, half:] = own_ref[...]

    code_ref[:, :LANES] = before_ref[...].astype(F32)
    code_ref[:, LANES:LANES + rows] = (bases_ref[...] + 1).astype(F32)
    code_ref[:, LANES + rows:] = after_ref[...].astype(F32)

    wide = w_ref[:, d1:].astype(F32)
    wide_ref[...] = wide
    we_ref[...] = wide.T.astype(BF16)
    gain = we_ref[pl.ds(64 - 8, 8), :].astype(F32)[5:6, :]

    column = iota((LANES, d1), 1)
    owner = (column * 2341) >> 16
    spread = (iota((LANES, d1), 0) == column - owner * per + 64).astype(F32)
    owned = owner[:shards] == iota((shards, d1), 0)
    pieces = wide_ref[pl.ds(0, shards, stride=block), :]
    bias = jnp.sum(jnp.where(owned, dot(pieces.astype(BF16), spread.astype(BF16), (1, 0)), 0.0), axis=0, keepdims=True)

    source, place = iota((tile, tile), 0), iota((tile, tile), 1)
    perm_ref[...] = (source == jnp.where(place < pair_tile, 2 * place, 2 * (place - pair_tile) + 1)).astype(BF16)
    repeat = ((iota((LANES, 16), 0) >> 2) == iota((LANES, 16), 1)).astype(BF16)
    letter = (iota((LANES, tile), 0) & 3) + 1
    line = iota((LANES, tile), 0)
    for t in range(rows // tile):
        window = code_ref[:, t * tile:t * tile + tile + 2 * LANES]
        start = LANES - reach
        shifted = jnp.concatenate([window[:, start + k:start + k + tile] for k in range(kw)] + [jnp.zeros((1, tile), F32)], axis=0)
        spreaded = dot(repeat, shifted.astype(BF16), (1, 0))
        hot = ((spreaded == letter.astype(F32)) & (line < taps)) | (line == taps)
        ordered = dot(hot.astype(F32).astype(BF16), perm_ref[...], (1, 0))
        feat_ref[:, t * tile:(t + 1) * tile] = ordered.astype(BF16)

    for t in range(rows // tile):
        at = t * tile
        emb_ref[at:at + tile, :] = dot(feat_ref[:, at:at + tile], we_ref[...], (0, 0)).astype(BF16)
        half_at = t * pair_tile
        ga_ref[half_at:half_at + pair_tile, :] = dot(cot_ref[half_at:half_at + pair_tile, :], w_ref[:, :d1], (1, 1))

        def side(start, grad):
            values = emb_ref[pl.ds(start, chunk), :].astype(F32)
            inverse = lax.rsqrt(jnp.sum(values * values, axis=1, keepdims=True) * (1.0 / d0) + EPSILON)
            scaled = values * inverse
            normed = scaled * gain
            square = normed * normed
            tanh = jnp.tanh(normed * (GELU_A + (GELU_A * GELU_B) * square))
            gate = 0.5 + 0.5 * tanh
            activated = normed * gate
            slope = gate + (activated * (1.0 - tanh)) * (GELU_A + (3.0 * GELU_A * GELU_B) * square)
            grad_normed = grad * slope
            toward_gain = grad_normed * scaled
            weighted = grad_normed * gain
            shared = jnp.sum(toward_gain * gain, axis=1, keepdims=True) * (1.0 / d0)
            ge_ref[pl.ds(start, chunk), :] = (inverse * (weighted - scaled * shared)).astype(BF16)
            return activated, toward_gain

        def body(i, total):
            first = pl.multiple_of(at + i * chunk, chunk)
            second = pl.multiple_of(at + pair_tile + i * chunk, chunk)
            pair_at = pl.multiple_of(half_at + i * chunk, chunk)
            grad = ga_ref[pl.ds(pair_at, chunk), :]
            act_even, gain_even = side(first, grad)
            act_odd, gain_odd = side(second, grad)
            s_ref[pl.ds(pair_at, chunk), :] = (act_even + act_odd).astype(BF16)
            both = gain_even + gain_odd
            for r in range(0, chunk, 8):
                total = total + both[r:r + 8]
            return total

        start_total = jnp.zeros((8, d0), F32)
        gain_total = lax.fori_loop(0, pair_tile // chunk, body, start_total)
        pooled_ref[half_at:half_at + pair_tile, :] = (
            0.5 * dot(s_ref[half_at:half_at + pair_tile, :], w_ref[:, :d1], (1, 0)) + bias).astype(BF16)
        part = dot(feat_ref[:, at:at + tile], ge_ref[at:at + tile, :], (1, 0))
        is_gain = iota((LANES, d0), 0) == taps + 1
        part = jnp.where(is_gain, jnp.sum(gain_total, axis=0, keepdims=True), part)
        if t == 0:
            gew_ref[...] = part
        else:
            gew_ref[...] += part

    wide_ref[...] = gew_ref[...].T
    sums = 2.0 * jnp.sum(cot_ref[...].astype(F32), axis=0, keepdims=True)
    pieces = dot(jnp.where(owned, sums, 0.0), spread, (1, 1), lax.Precision.HIGHEST)
    wide_ref[pl.ds(0, shards, stride=block), :] = wide_ref[pl.ds(0, shards, stride=block), :] + pieces

    def halves(first_ref, second_ref):
        first_ref[...] = dot(s_ref[...], cot_ref[:, :half], (0, 0)).astype(first_ref.dtype)
        second_ref[:, :d1 - half] = dot(s_ref[...], cot_ref[:, half:], (0, 0)).astype(second_ref.dtype)
        second_ref[:, d1 - half:] = wide_ref[...].astype(second_ref.dtype)

    @pl.when(core == 0)
    def _():
        halves(mine_ref, theirs_ref)

    @pl.when(core != 0)
    def _():
        halves(theirs_ref, mine_ref)


def train_step(core, before, bases, after, own, other, cot, kw, shards):
    d0, half = own.shape
    pairs, d1 = cot.shape
    rows = 2 * pairs
    width = 2 * half
    tile, chunk = 512, 16
    dims = (kw, shards, d0, d1, rows, tile, chunk)
    vmem = pl.BlockSpec(memory_space=pltpu.VMEM)
    return pl.pallas_call(
        functools.partial(step_kernel, dims),
        out_shape=(
            jax.ShapeDtypeStruct((pairs, d1), BF16),
            jax.ShapeDtypeStruct((d0, half), F32),
            jax.ShapeDtypeStruct((d0, half), BF16),
        ),
        in_specs=[pl.BlockSpec(memory_space=pltpu.SMEM)] + [vmem] * 6,
        out_specs=(vmem, vmem, vmem),
        scratch_shapes=[
            pltpu.VMEM((d0, width), BF16),
            pltpu.VMEM((1, rows + 2 * LANES), F32),
            pltpu.VMEM((tile, tile), BF16),
            pltpu.VMEM((LANES, rows), BF16),
            pltpu.VMEM((LANES, d0), BF16),
            pltpu.VMEM((d0, LANES), F32),
            pltpu.VMEM((rows, d0), BF16),
            pltpu.VMEM((pairs, d0), F32),
            pltpu.VMEM((pairs, d0), BF16),
            pltpu.VMEM((rows, d0), BF16),
            pltpu.VMEM((LANES, d0), F32),
        ],
        compiler_params=pltpu.CompilerParams(vmem_limit_bytes=50 << 20),
        name="train_step",
    )(core, before, bases, after, own, other, cot)


def pack_kernel(core_ref, embed_ref, embed_bias_ref, gain_ref, proj_ref, proj_bias_ref, out_ref, rows_ref, block_ref):
    kw, block, d1 = embed_ref.shape[0], proj_ref.shape[0], proj_ref.shape[1]
    copies, _, half = out_ref.shape
    taps, per = kw * 4, proj_bias_ref.shape[1]
    rows_ref[...] = jnp.zeros_like(rows_ref)
    for k in range(kw):
        rows_ref[4 * k:4 * k + 4, :block] = embed_ref[k].astype(F32)
    rows_ref[taps:taps + 1, :block] = embed_bias_ref[...].astype(F32)
    rows_ref[taps + 1:taps + 2, :block] = gain_ref[...].astype(F32)
    block_ref[...] = rows_ref[...].T[:block]
    block_ref[:1, 64:64 + per] = proj_bias_ref[...].astype(F32)
    edge = d1 - half

    @pl.when(core_ref[0] == 0)
    def _():
        for i in range(copies):
            out_ref[i] = proj_ref[:, :half]

    @pl.when(core_ref[0] != 0)
    def _():
        for i in range(copies):
            out_ref[i, :, :edge] = proj_ref[:, half:]
            out_ref[i, :, edge:] = block_ref[...].astype(BF16)


def sum_kernel(scale, in_ref, out_ref):
    total = in_ref[0].astype(F32)
    for i in range(1, in_ref.shape[0]):
        total = total + in_ref[i].astype(F32)
    if scale != 1.0:
        total = total * scale
    total = total.astype(out_ref.dtype)
    for i in range(out_ref.shape[0]):
        out_ref[i] = total


def unpack_kernel(core_ref, total_ref, across_ref, embed_ref, embed_bias_ref, gain_ref, proj_ref, proj_bias_ref, rows_ref):
    kw, block, d1 = embed_ref.shape[0], proj_ref.shape[0], proj_ref.shape[1]
    half = total_ref.shape[1]
    taps, per, edge = kw * 4, proj_bias_ref.shape[1], d1 - half

    def place(left_ref, right_ref):
        proj_ref[:, :half] = left_ref[...]
        proj_ref[:, half:] = right_ref[:, :edge]
        rows_ref[:block, :] = right_ref[:, edge:]

    @pl.when(core_ref[0] == 0)
    def _():
        place(total_ref, across_ref)

    @pl.when(core_ref[0] != 0)
    def _():
        place(across_ref, total_ref)

    proj_bias_ref[...] = rows_ref[:1, 64:64 + per]
    rows_ref[block:, :] = jnp.zeros((LANES - block, LANES), F32)
    rows_ref[...] = rows_ref[...].T
    for k in range(kw):
        embed_ref[k] = rows_ref[4 * k:4 * k + 4, :block]
    embed_bias_ref[...] = rows_ref[taps:taps + 1, :block]
    gain_ref[...] = rows_ref[taps + 1:taps + 2, :block]


VMEM = pl.BlockSpec(memory_space=pltpu.VMEM)
SMEM = pl.BlockSpec(memory_space=pltpu.SMEM)


def local(bases, embed_weight, embed_bias, norm_gain, proj_weight, proj_bias, cotangent):
    kw = embed_weight.shape[0]
    shards, members = lax.axis_size("dp"), lax.axis_size("seq")
    block, d1 = proj_weight.shape
    per = proj_bias.shape[0]
    half = (d1 + LANES) // 2
    core = (lax.axis_index("seq") & 1).astype(jnp.int32).reshape(1)
    swap = [(i, i ^ 1) for i in range(members)]

    codes = bases + 1
    before = lax.ppermute(codes[:, -LANES:], "seq", [(i, i + 1) for i in range(members - 1)])
    after = lax.ppermute(codes[:, :LANES], "seq", [(i + 1, i) for i in range(members - 1)])

    piece = pl.pallas_call(
        pack_kernel,
        out_shape=jax.ShapeDtypeStruct((shards, block, half), BF16),
        in_specs=[SMEM] + [VMEM] * 5,
        out_specs=VMEM,
        scratch_shapes=[pltpu.VMEM((LANES, LANES), F32), pltpu.VMEM((block, LANES), F32)],
        name="pack",
    )(core, embed_weight, embed_bias[None], norm_gain[None], proj_weight, proj_bias[None])
    own = lax.all_to_all(piece, "dp", 0, 0, tiled=True).reshape(shards * block, half)
    other = lax.ppermute(own, "seq", swap)

    pooled, mine, theirs = train_step(core, before, bases, after, own, other, cotangent[0], kw, shards)

    came = lax.ppermute(theirs, "seq", swap)
    summed = (mine + came.astype(F32)).astype(BF16).reshape(shards, block, half)
    parts = lax.all_to_all(summed, "dp", 0, 0, tiled=True)

    def add_up(parts, scale, copies, kind):
        return pl.pallas_call(
            functools.partial(sum_kernel, scale),
            out_shape=jax.ShapeDtypeStruct((copies, block, half), kind),
            in_specs=[VMEM],
            out_specs=VMEM,
            name="add_up",
        )(parts)

    groups = [[i for i in range(members) if i % 2 == c] for c in range(2)]
    spread = lax.all_to_all(add_up(parts, 1.0, members // 2, BF16), "seq", 0, 0, axis_index_groups=groups, tiled=True)
    total = add_up(spread, 0.25 / (cotangent.shape[1] * members * shards), 1, F32)[0]
    across = lax.ppermute(total, "seq", swap)
    grad_embed, grad_embed_bias, grad_gain, grad_proj, grad_proj_bias = pl.pallas_call(
        unpack_kernel,
        out_shape=(
            jax.ShapeDtypeStruct(embed_weight.shape, F32),
            jax.ShapeDtypeStruct((1, block), F32),
            jax.ShapeDtypeStruct((1, block), F32),
            jax.ShapeDtypeStruct((block, d1), F32),
            jax.ShapeDtypeStruct((1, per), F32),
        ),
        in_specs=[SMEM, VMEM, VMEM],
        out_specs=(VMEM,) * 5,
        scratch_shapes=[pltpu.VMEM((LANES, LANES), F32)],
        name="unpack",
    )(core, total, across)
    return (pooled[None], grad_embed, grad_embed_bias[0], grad_gain[0], grad_proj, grad_proj_bias[0])


def solution(mesh):
    placed = (
        P("dp", "seq"),
        P(None, None, "dp"),
        P("dp"),
        P("dp"),
        P("dp", None),
        P("dp"),
        P("dp", "seq", None),
    )
    return jax.shard_map(
        local,
        mesh=mesh,
        in_specs=placed,
        out_specs=(
            P("dp", "seq", None),
            P(None, None, "dp"),
            P("dp"),
            P("dp"),
            P("dp", None),
            P("dp"),
        ),
        check_vma=False,
    )
```

time: 877 us -> 138 us (0.16)
  waiting for transfers between devices: 403 us -> 4.01 us
  blocking collectives: 366 us -> 80 us
  local copies, waits for them, and re-layouts: 34.5 us -> 0.63 us
  Pallas kernels: 0 us -> 28.1 us
  matrix products: 24.3 us -> 0 us
  other arithmetic: 20 us -> 1.67 us
  between operations: 16.5 us -> 0.74 us
  starting transfers between devices: 11.3 us -> 22 us
    unnamed x6 -> x0, waiting for transfers between devices: 305 us -> none
    unnamed x2 -> x0, blocking collectives: 201 us -> none
    psum x1 -> x0, waiting for transfers between devices: 98.4 us -> none  [local(): lax.psum((grad_embed_weight, grad_embed_bias, grad_norm_gain, grad_proj_w...]
    psum x1 -> x0, blocking collectives: 94.5 us -> none  [local(): lax.psum((grad_embed_weight, grad_embed_bias, grad_norm_gain, grad_proj_w...]
    all_to_all x0 -> x3, blocking collectives: none -> 80 us  [the longest x1 34.6 us: local(): lax.all_to_all(piece, 'dp', 0, 0, tiled=True).reshape(shards * block, half)]
    all_gather x1 -> x0, blocking collectives: 69.9 us -> none  [local(): lax.all_gather(embed_weight, 'dp', axis=2, tiled=True)]
    pallas_call x0 -> x5, Pallas kernels: none -> 28.1 us  [the longest x1 21.1 us: train_step(): pl.pallas_call(functools.partial(step_kernel, dims), out_shape=(jax.Shape...]
    dot_general x5 -> x0, matrix products: 24.3 us -> none  [the longest x1 8.46 us: local(): lax.dot_general(grad_mixed, full_proj, (((1,), (1,)), ((), ())), preferre...]
  transfers between devices with their start and end apart: 6 -> 5, of which waited for: 3 -> 3; matrix products, arithmetic and copies ran while one was open for 9% -> 0% of each run, Pallas kernels for 0% -> 0%
where the time goes in v1:
time: 138 us; the launch traced here: 137 us
  blocking collectives  80 us (58%)
  Pallas kernels  28.1 us (20%)
  starting transfers between devices  22 us (16%)
  waiting for transfers between devices  4.01 us (3%)
  other arithmetic  1.67 us (1%)
    all_to_all x1, blocking collectives, local(): lax.all_to_all(piece, 'dp', 0, 0, tiled=True).reshape(shards * block, half)  34.6 us
    all_to_all x1, blocking collectives, local(): parts = lax.all_to_all(summed, 'dp', 0, 0, tiled=True)  26.9 us
    pallas_call x1, Pallas kernels, train_step(): pl.pallas_call(functools.partial(step_kernel, dims), out_shape=(jax.Shape...  21.1 us
    all_to_all x1, blocking collectives, local(): lax.all_to_all(add_up(parts, 1.0, members // 2, BF16), 'seq', 0, 0, axis_...  18.5 us
    ppermute x1, starting transfers between devices, local(): lax.ppermute(codes[:, -LANES:], 'seq', [(i, i + 1) for i in range(members...  7.55 us
    ppermute x1, starting transfers between devices, local(): across = lax.ppermute(total, 'seq', swap)  5.95 us
    ppermute x1, starting transfers between devices, local(): other = lax.ppermute(own, 'seq', swap)  4.71 us
    pallas_call x2, Pallas kernels, add_up(): pl.pallas_call(functools.partial(sum_kernel, scale), out_shape=jax.ShapeD...  3.49 us
  transfers between devices with their start and end apart: 5, of which 3 were waited for; matrix products, arithmetic and copies ran while one was open for 0% of the time, Pallas kernels for 0%

profile of v1, /device:TPU:1, one launch (start us, length us, event | category | flops | bytes accessed | tf_op | source)
XLA Modules:
  0.0 137.2 jit_solution(11874116034953712142)
XLA Ops:
  0.6 0.0 copy-start.1
  0.6 0.0 copy-start
  0.7 2.0 %pack.1 = bf16[32,24,512]{2,1,0:T(8,128)(2,1)} custom-call(s32[1]{0:T(128)} %bitcast.core_ref, bf16[15,4,24]{2,1,0:T(4,128)(2,1)} %embed_ref.1, bf16[1,24]{1,0:T(2,128)(2,1)} %bitcast.18, bf16[1,24]{1,0:T(2,128)(2,1)} %bitcast.19, bf16[24,896]{1,0:T(8,128)(2,1)} %proj_ref.1, bf16[1,28]{1,0:T(2,128)(2,1)} %bitcast.20), custom_call_target="tpu_custom_call" | custom-call | tf_op jit(solution)/shard_map/pack/pallas_call | solution.py:259
  2.6 34.6 %all_to_all.15 = bf16[32,24,512]{2,1,0:T(8,128)(2,1)S(1)} all-to-all(bf16[32,24,512]{2,1,0:T(8,128)(2,1)} %pack.1), channel_id=1, replica_groups=mesh['dp'=32,'seq'=16] {'dp'}, dimensions={0} | all-to-all | bytes 1572864 | tf_op jit(solution)/shard_map/all_to_all | solution.py:267
  37.2 4.7 %collective-permute-start.2 = (bf16[768,512]{1,0:T(8,128)(2,1)S(1)}, bf16[768,512]{1,0:T(8,128)(2,1)S(1)}, u32[]{:S(2)}, u32[]{:S(2)}) collective-permute-start(bf16[768,512]{1,0:T(8,128)(2,1)S(1)} %bitcast.12), channel_id=1, source_target_pairs={{0,1},{1,0},{2,3},{3,2},{4,5},{5,4},{6,7},{7,6},{8,9},{9,8},{10,11... | collective-permute-start | bytes 2359304 | tf_op jit(solution)/shard_map/ppermute | solution.py:268
  42.0 0.0 copy-done.1
  42.0 1.9 %collective-permute-start.1 = (s32[1,128]{1,0:T(1,128)S(1)}, s32[1,128]{1,0:T(1,128)S(1)}, u32[]{:S(2)}, u32[]{:S(2)}) collective-permute-start(s32[1,128]{1,0:T(1,128)S(1)} %get-tuple-element.22), channel_id=1, source_target_pairs={{1,0},{2,1},{3,2},{4,3},{5,4},{6,5},{7,6},{8,7},{9,8},{10,9},{11,1... | collective-permute-start | bytes 1544 | tf_op jit(solution)/shard_map/ppermute | solution.py:257
  43.9 7.5 %collective-permute-start = (s32[1,128]{1,0:T(1,128)S(1)}, s32[1,128]{1,0:T(1,128)S(1)}, u32[]{:S(2)}, u32[]{:S(2)}) collective-permute-start(s32[1,128]{1,0:T(1,128)S(1)} %get-tuple-element.23), channel_id=1, source_target_pairs={{0,1},{1,2},{2,3},{3,4},{4,5},{5,6},{6,7},{7,8},{8,9},{9,10},{10,1... | collective-permute-start | bytes 1544 | tf_op jit(solution)/shard_map/ppermute | solution.py:256
  51.5 0.0 collective-permute-done.1.after_ref
  51.5 0.7 collective-permute-done.before_ref
  52.2 0.0 collective-permute-done.2.other_ref
  52.2 0.0 copy-done
  52.2 21.1 %train_step.1 = (bf16[768,896]{1,0:T(8,128)(2,1)}, f32[768,512]{1,0:T(8,128)}, bf16[768,512]{1,0:T(8,128)(2,1)S(1)}) custom-call(s32[1]{0:T(128)} %bitcast.core_ref, s32[1,128]{1,0:T(1,128)S(1)} %collective-permute-done.before_ref, s32[1,1536]{1,0:T(1,128)S(1)} %copy-done.1, s32[1,128]{1,0:T(1,128)S(1)} %collective-permute-done.1.after_ref, ...), custom_call_target="tpu_custom_call" | custom-call | tf_op jit(solution)/shard_map/train_step/pallas_call | solution.py:152
  73.3 1.9 %collective-permute-start.3 = (bf16[768,512]{1,0:T(8,128)(2,1)S(1)}, bf16[768,512]{1,0:T(8,128)(2,1)S(1)}, u32[]{:S(2)}, u32[]{:S(2)}) collective-permute-start(bf16[768,512]{1,0:T(8,128)(2,1)S(1)} %get-tuple-element.16), channel_id=1, source_target_pairs={{0,1},{1,0},{2,3},{3,2},{4,5},{5,4},{6,7},{7,6},{8,9},{9,8},{10,11... | collective-permute-start | bytes 2359304 | tf_op jit(solution)/shard_map/ppermute | solution.py:272
  75.2 2.3 %collective-permute-done.3 = bf16[768,512]{1,0:T(8,128)(2,1)S(1)} collective-permute-done((bf16[768,512]{1,0:T(8,128)(2,1)S(1)}, bf16[768,512]{1,0:T(8,128)(2,1)S(1)}, u32[]{:S(2)}, u32[]{:S(2)}) %collective-permute-start.3) | collective-permute-done | bytes 786464 | tf_op jit(solution)/shard_map/ppermute | solution.py:272
  77.4 1.7 %add_convert_fusion = bf16[768,512]{1,0:T(8,128)(2,1)S(1)} fusion(f32[768,512]{1,0:T(8,128)} %get-tuple-element.15, bf16[768,512]{1,0:T(8,128)(2,1)S(1)} %collective-permute-done.3), kind=kLoop, calls=%fused_computation | loop fusion | flops 1179648 | bytes 3145728 | tf_op jit(solution)/shard_map/convert_element_type | solution.py:273
  79.1 26.9 %all_to_all.16.in_ref = bf16[32,24,512]{2,1,0:T(8,128)(2,1)} all-to-all(bf16[32,24,512]{2,1,0:T(8,128)(2,1)S(1)} %bitcast.15), channel_id=1, replica_groups=mesh['dp'=32,'seq'=16] {'dp'}, dimensions={0} | all-to-all | bytes 1572864 | tf_op jit(solution)/shard_map/all_to_all | solution.py:274
  106.0 1.9 %add_up.2 = bf16[8,24,512]{2,1,0:T(8,128)(2,1)} custom-call(bf16[32,24,512]{2,1,0:T(8,128)(2,1)} %all_to_all.16.in_ref), custom_call_target="tpu_custom_call" | custom-call | tf_op jit(solution)/shard_map/add_up/pallas_call | solution.py:277
  108.0 18.5 %all_to_all.17.in_ref = bf16[8,24,512]{2,1,0:T(8,128)(2,1)} all-to-all(bf16[8,24,512]{2,1,0:T(8,128)(2,1)} %add_up.2), channel_id=1, replica_groups={{0,2,4,6,8,10,12,14},{1,3,5,7,9,11,13,15},{16,18,20,22,24,26,28,30},{17..., dimensions={0} | all-to-all | bytes 393216 | tf_op jit(solution)/shard_map/all_to_all | solution.py:286
  126.4 1.6 %add_up.3 = f32[1,24,512]{2,1,0:T(8,128)} custom-call(bf16[8,24,512]{2,1,0:T(8,128)(2,1)} %all_to_all.17.in_ref), custom_call_target="tpu_custom_call" | custom-call | tf_op jit(solution)/shard_map/add_up/pallas_call | solution.py:277
  128.0 6.0 %collective-permute-start.4 = (f32[24,512]{1,0:T(8,128)}, f32[24,512]{1,0:T(8,128)S(1)}, u32[]{:S(2)}, u32[]{:S(2)}) collective-permute-start(f32[24,512]{1,0:T(8,128)} %bitcast.16), channel_id=1, source_target_pairs={{0,1},{1,0},{2,3},{3,2},{4,5},{5,4},{6,7},{7,6},{8,9},{9,8},{10,11... | collective-permute-start | bytes 147464 | tf_op jit(solution)/shard_map/ppermute | solution.py:288
  133.9 1.1 collective-permute-done.4.across_ref
  135.0 0.6 copy-done.2
  135.6 1.6 %unpack.1 = (f32[15,4,24]{2,1,0:T(4,128)}, f32[1,24]{1,0:T(1,128)}, f32[1,24]{1,0:T(1,128)}, f32[24,896]{1,0:T(8,128)}, f32[1,28]{1,0:T(1,128)}) custom-call(s32[1]{0:T(128)} %bitcast.core_ref, f32[24,512]{1,0:T(8,128)} %bitcast.17, f32[24,512]{1,0:T(8,128)} %copy-done.2), custom_call_target="tpu_custom_call" | custom-call | tf_op jit(solution)/shard_map/unpack/pallas_call | solution.py:289
  (3 shorter events, 0.0 us)
Async XLA Ops:
  0.6 41.3 %copy-start.1 = (s32[1,1536]{1,0:T(1,128)S(1)}, s32[1,1536]{1,0:T(1,128)}, u32[]{:S(2)}) copy-start(s32[1,1536]{1,0:T(1,128)} %bases_ref.1) | copy-start | bytes 18436
  0.6 51.5 %copy-start = (bf16[1,768,896]{2,1,0:T(8,128)(2,1)S(1)}, bf16[1,768,896]{2,1,0:T(8,128)(2,1)}, u32[]{:S(2)}) copy-start(bf16[1,768,896]{2,1,0:T(8,128)(2,1)} %param.13) | copy-start | bytes 4128772
  37.2 14.9 %collective-permute-start.2 = (bf16[768,512]{1,0:T(8,128)(2,1)S(1)}, bf16[768,512]{1,0:T(8,128)(2,1)S(1)}, u32[]{:S(2)}, u32[]{:S(2)}) collective-permute-start(bf16[768,512]{1,0:T(8,128)(2,1)S(1)} %bitcast.12), channel_id=1, source_target_pairs={{0,1},{1,0},{2,3},{3,2},{4,5},{5,4},{6,7},{7,6},{8,9},{9,8},{10,11... | collective-permute-start | bytes 2359304 | tf_op jit(solution)/shard_map/ppermute | solution.py:268
  42.0 9.5 %collective-permute-start.1 = (s32[1,128]{1,0:T(1,128)S(1)}, s32[1,128]{1,0:T(1,128)S(1)}, u32[]{:S(2)}, u32[]{:S(2)}) collective-permute-start(s32[1,128]{1,0:T(1,128)S(1)} %get-tuple-element.22), channel_id=1, source_target_pairs={{1,0},{2,1},{3,2},{4,3},{5,4},{6,5},{7,6},{8,7},{9,8},{10,9},{11,1... | collective-permute-start | bytes 1544 | tf_op jit(solution)/shard_map/ppermute | solution.py:257
  43.9 8.3 %collective-permute-start = (s32[1,128]{1,0:T(1,128)S(1)}, s32[1,128]{1,0:T(1,128)S(1)}, u32[]{:S(2)}, u32[]{:S(2)}) collective-permute-start(s32[1,128]{1,0:T(1,128)S(1)} %get-tuple-element.23), channel_id=1, source_target_pairs={{0,1},{1,2},{2,3},{3,4},{4,5},{5,6},{6,7},{7,8},{8,9},{9,10},{10,1... | collective-permute-start | bytes 1544 | tf_op jit(solution)/shard_map/ppermute | solution.py:256
  73.3 4.2 %collective-permute-start.3 = (bf16[768,512]{1,0:T(8,128)(2,1)S(1)}, bf16[768,512]{1,0:T(8,128)(2,1)S(1)}, u32[]{:S(2)}, u32[]{:S(2)}) collective-permute-start(bf16[768,512]{1,0:T(8,128)(2,1)S(1)} %get-tuple-element.16), channel_id=1, source_target_pairs={{0,1},{1,0},{2,3},{3,2},{4,5},{5,4},{6,7},{7,6},{8,9},{9,8},{10,11... | collective-permute-start | bytes 2359304 | tf_op jit(solution)/shard_map/ppermute | solution.py:272
  128.0 7.0 %collective-permute-start.4 = (f32[24,512]{1,0:T(8,128)}, f32[24,512]{1,0:T(8,128)S(1)}, u32[]{:S(2)}, u32[]{:S(2)}) collective-permute-start(f32[24,512]{1,0:T(8,128)} %bitcast.16), channel_id=1, source_target_pairs={{0,1},{1,0},{2,3},{3,2},{4,5},{5,4},{6,7},{7,6},{8,9},{9,8},{10,11... | collective-permute-start | bytes 147464 | tf_op jit(solution)/shard_map/ppermute | solution.py:288
  135.0 0.6 copy-start.2

commit v2 on v1

--- a/solution.py
+++ b/solution.py
@@ -11,6 +11,8 @@
 LANES = 128
 GELU_A = 0.7978845608028654
 GELU_B = 0.044715
+GELU_K = (GELU_A * GELU_B) ** (1 / 3)
+GELU_C = GELU_A / GELU_K
 EPSILON = 1e-06
 
 
@@ -52,6 +54,7 @@
     wide_ref[...] = wide
     we_ref[...] = wide.T.astype(BF16)
     gain = we_ref[pl.ds(64 - 8, 8), :].astype(F32)[5:6, :]
+    gain_y = gain * GELU_K
 
     column = iota((LANES, d1), 1)
     owner = (column * 2341) >> 16
@@ -83,18 +86,16 @@
         def side(start, grad):
             values = emb_ref[pl.ds(start, chunk), :].astype(F32)
             inverse = lax.rsqrt(jnp.sum(values * values, axis=1, keepdims=True) * (1.0 / d0) + EPSILON)
-            scaled = values * inverse
-            normed = scaled * gain
-            square = normed * normed
-            tanh = jnp.tanh(normed * (GELU_A + (GELU_A * GELU_B) * square))
-            gate = 0.5 + 0.5 * tanh
-            activated = normed * gate
-            slope = gate + (activated * (1.0 - tanh)) * (GELU_A + (3.0 * GELU_A * GELU_B) * square)
+            y = (values * inverse) * gain_y
+            square = y * y
+            tanh = jnp.tanh(y * (GELU_C + square))
+            above, below = 1.0 + tanh, 1.0 - tanh
+            activated = y * above
+            slope = above + (activated * below) * (GELU_C + 3.0 * square)
             grad_normed = grad * slope
-            toward_gain = grad_normed * scaled
-            weighted = grad_normed * gain
-            shared = jnp.sum(toward_gain * gain, axis=1, keepdims=True) * (1.0 / d0)
-            ge_ref[pl.ds(start, chunk), :] = (inverse * (weighted - scaled * shared)).astype(BF16)
+            toward_gain = grad_normed * y
+            shared = jnp.sum(toward_gain, axis=1, keepdims=True) * (inverse * inverse * (1.0 / (GELU_K * d0)))
+            ge_ref[pl.ds(start, chunk), :] = (inverse * (grad_normed * gain) - values * shared).astype(BF16)
             return activated, toward_gain
 
         def body(i, total):
@@ -111,25 +112,25 @@
             return total
 
         start_total = jnp.zeros((8, d0), F32)
-        gain_total = lax.fori_loop(0, pair_tile // chunk, body, start_total)
+        gain_total = lax.fori_loop(0, pair_tile // chunk, body, start_total, unroll=True)
         pooled_ref[half_at:half_at + pair_tile, :] = (
-            0.5 * dot(s_ref[half_at:half_at + pair_tile, :], w_ref[:, :d1], (1, 0)) + bias).astype(BF16)
+            (0.25 / GELU_K) * dot(s_ref[half_at:half_at + pair_tile, :], w_ref[:, :d1], (1, 0)) + bias).astype(BF16)
         part = dot(feat_ref[:, at:at + tile], ge_ref[at:at + tile, :], (1, 0))
         is_gain = iota((LANES, d0), 0) == taps + 1
-        part = jnp.where(is_gain, jnp.sum(gain_total, axis=0, keepdims=True), part)
+        part = jnp.where(is_gain, jnp.sum(gain_total, axis=0, keepdims=True) / gain_y, part)
         if t == 0:
             gew_ref[...] = part
         else:
             gew_ref[...] += part
 
     wide_ref[...] = gew_ref[...].T
-    sums = 2.0 * jnp.sum(cot_ref[...].astype(F32), axis=0, keepdims=True)
+    sums = 4.0 * jnp.sum(cot_ref[...].astype(F32), axis=0, keepdims=True)
     pieces = dot(jnp.where(owned, sums, 0.0), spread, (1, 1), lax.Precision.HIGHEST)
     wide_ref[pl.ds(0, shards, stride=block), :] = wide_ref[pl.ds(0, shards, stride=block), :] + pieces
 
     def halves(first_ref, second_ref):
-        first_ref[...] = dot(s_ref[...], cot_ref[:, :half], (0, 0)).astype(first_ref.dtype)
-        second_ref[:, :d1 - half] = dot(s_ref[...], cot_ref[:, half:], (0, 0)).astype(second_ref.dtype)
+        first_ref[...] = (dot(s_ref[...], cot_ref[:, :half], (0, 0)) * (1.0 / GELU_K)).astype(first_ref.dtype)
+        second_ref[:, :d1 - half] = (dot(s_ref[...], cot_ref[:, half:], (0, 0)) * (1.0 / GELU_K)).astype(second_ref.dtype)
         second_ref[:, d1 - half:] = wide_ref[...].astype(second_ref.dtype)
 
     @pl.when(core == 0)
@@ -146,7 +147,7 @@
     pairs, d1 = cot.shape
     rows = 2 * pairs
     width = 2 * half
-    tile, chunk = 512, 16
+    tile, chunk = 512, 32
     dims = (kw, shards, d0, d1, rows, tile, chunk)
     vmem = pl.BlockSpec(memory_space=pltpu.VMEM)
     return pl.pallas_call(
@@ -171,7 +172,7 @@
             pltpu.VMEM((rows, d0), BF16),
             pltpu.VMEM((LANES, d0), F32),
         ],
-        compiler_params=pltpu.CompilerParams(vmem_limit_bytes=50 << 20),
+        compiler_params=pltpu.CompilerParams(vmem_limit_bytes=28 << 20),
         name="train_step",
     )(core, before, bases, after, own, other, cot)
 
@@ -262,6 +263,7 @@
         in_specs=[SMEM] + [VMEM] * 5,
         out_specs=VMEM,
         scratch_shapes=[pltpu.VMEM((LANES, LANES), F32), pltpu.VMEM((block, LANES), F32)],
+        compiler_params=pltpu.CompilerParams(vmem_limit_bytes=4 << 20),
         name="pack",
     )(core, embed_weight, embed_bias[None], norm_gain[None], proj_weight, proj_bias[None])
     own = lax.all_to_all(piece, "dp", 0, 0, tiled=True).reshape(shards * block, half)
@@ -279,12 +281,13 @@
             out_shape=jax.ShapeDtypeStruct((copies, block, half), kind),
             in_specs=[VMEM],
             out_specs=VMEM,
+            compiler_params=pltpu.CompilerParams(vmem_limit_bytes=4 << 20),
             name="add_up",
         )(parts)
 
     groups = [[i for i in range(members) if i % 2 == c] for c in range(2)]
     spread = lax.all_to_all(add_up(parts, 1.0, members // 2, BF16), "seq", 0, 0, axis_index_groups=groups, tiled=True)
-    total = add_up(spread, 0.25 / (cotangent.shape[1] * members * shards), 1, F32)[0]
+    total = add_up(spread, 0.125 / (cotangent.shape[1] * members * shards), 1, F32)[0]
     across = lax.ppermute(total, "seq", swap)
     grad_embed, grad_embed_bias, grad_gain, grad_proj, grad_proj_bias = pl.pallas_call(
         unpack_kernel,
@@ -298,6 +301,7 @@
         in_specs=[SMEM, VMEM, VMEM],
         out_specs=(VMEM,) * 5,
         scratch_shapes=[pltpu.VMEM((LANES, LANES), F32)],
+        compiler_params=pltpu.CompilerParams(vmem_limit_bytes=4 << 20),
         name="unpack",
     )(core, total, across)
     return (pooled[None], grad_embed, grad_embed_bias[0], grad_gain[0], grad_proj, grad_proj_bias[0])

time: 138 us -> 122 us (0.88)
  Pallas kernels: 28.1 us -> 11.4 us
  local copies, waits for them, and re-layouts: 0.63 us -> 3.57 us
  other arithmetic: 1.67 us -> 0.28 us
    pallas_call x1, Pallas kernels: 21.1 us -> 10.4 us  [train_step(): pl.pallas_call(functools.partial(step_kernel, dims), out_shape=(jax.Shape...]
    pallas_call x2, Pallas kernels: 3.49 us -> 0.15 us  [add_up(): pl.pallas_call(functools.partial(sum_kernel, scale), out_shape=jax.ShapeD...]
    unnamed x6 -> x14, local copies, waits for them, and re-layouts: 0.62 us -> 3.57 us
    pallas_call x1, Pallas kernels: 1.96 us -> 0.17 us  [local(): pl.pallas_call(pack_kernel, out_shape=jax.ShapeDtypeStruct((shards, block...]
    convert_element_type x1, other arithmetic: 1.66 us -> 0.27 us  [local(): summed = (mine + came.astype(F32)).astype(BF16).reshape(shards, block, half)]
where the time goes in v2:
time: 122 us; the launch traced here: 121 us
  blocking collectives  79.4 us (65%)
  starting transfers between devices  22 us (18%)
  Pallas kernels  11.4 us (9%)
  waiting for transfers between devices  3.8 us (3%)
  local copies, waits for them, and re-layouts  3.57 us (3%)
    all_to_all x1, blocking collectives, local(): lax.all_to_all(piece, 'dp', 0, 0, tiled=True).reshape(shards * block, half)  34.4 us
    all_to_all x1, blocking collectives, local(): parts = lax.all_to_all(summed, 'dp', 0, 0, tiled=True)  26.8 us
    all_to_all x1, blocking collectives, local(): lax.all_to_all(add_up(parts, 1.0, members // 2, BF16), 'seq', 0, 0, axis_...  18.1 us
    pallas_call x1, Pallas kernels, train_step(): pl.pallas_call(functools.partial(step_kernel, dims), out_shape=(jax.Shape...  10.4 us
    ppermute x1, starting transfers between devices, local(): lax.ppermute(codes[:, -LANES:], 'seq', [(i, i + 1) for i in range(members...  7.55 us
    ppermute x1, starting transfers between devices, local(): across = lax.ppermute(total, 'seq', swap)  5.97 us
    ppermute x1, starting transfers between devices, local(): other = lax.ppermute(own, 'seq', swap)  4.68 us
    unnamed x14, local copies, waits for them, and re-layouts  3.57 us
  transfers between devices with their start and end apart: 5, of which 3 were waited for; matrix products, arithmetic and copies ran while one was open for 0% of the time, Pallas kernels for 0%

profile of v2, /device:TPU:1, one launch (start us, length us, event | category | flops | bytes accessed | tf_op | source)
XLA Modules:
  0.0 121.2 jit_solution(14386335077944512655)
XLA Ops:
  0.6 0.0 copy-start
  0.7 0.9 copy-done.1
  1.5 0.7 copy-done.3
  2.3 0.7 copy-done.4
  2.9 0.7 copy-done.5
  3.6 0.7 copy-done.6
  4.2 0.2 pack.1
  4.4 34.4 %all_to_all.15 = bf16[32,24,512]{2,1,0:T(8,128)(2,1)S(1)} all-to-all(bf16[32,24,512]{2,1,0:T(8,128)(2,1)S(1)} %pack.1), channel_id=1, replica_groups=mesh['dp'=32,'seq'=16] {'dp'}, dimensions={0} | all-to-all | bytes 1572864 | tf_op jit(solution)/shard_map/all_to_all | solution.py:269
  38.8 4.7 %collective-permute-start.2 = (bf16[768,512]{1,0:T(8,128)(2,1)S(1)}, bf16[768,512]{1,0:T(8,128)(2,1)S(1)}, u32[]{:S(2)}, u32[]{:S(2)}) collective-permute-start(bf16[768,512]{1,0:T(8,128)(2,1)S(1)} %bitcast.12), channel_id=1, source_target_pairs={{0,1},{1,0},{2,3},{3,2},{4,5},{5,4},{6,7},{7,6},{8,9},{9,8},{10,11... | collective-permute-start | bytes 2359304 | tf_op jit(solution)/shard_map/ppermute | solution.py:270
  43.6 1.9 %collective-permute-start.1 = (s32[1,128]{1,0:T(1,128)S(1)}, s32[1,128]{1,0:T(1,128)S(1)}, u32[]{:S(2)}, u32[]{:S(2)}) collective-permute-start(s32[1,128]{1,0:T(1,128)S(1)} %get-tuple-element.22), channel_id=1, source_target_pairs={{1,0},{2,1},{3,2},{4,3},{5,4},{6,5},{7,6},{8,7},{9,8},{10,9},{11,1... | collective-permute-start | bytes 1544 | tf_op jit(solution)/shard_map/ppermute | solution.py:258
  45.5 7.5 %collective-permute-start = (s32[1,128]{1,0:T(1,128)S(1)}, s32[1,128]{1,0:T(1,128)S(1)}, u32[]{:S(2)}, u32[]{:S(2)}) collective-permute-start(s32[1,128]{1,0:T(1,128)S(1)} %get-tuple-element.23), channel_id=1, source_target_pairs={{0,1},{1,2},{2,3},{3,4},{4,5},{5,6},{6,7},{7,8},{8,9},{9,10},{10,1... | collective-permute-start | bytes 1544 | tf_op jit(solution)/shard_map/ppermute | solution.py:257
  53.0 0.0 collective-permute-done.1.after_ref
  53.1 0.7 collective-permute-done.before_ref
  53.7 0.0 collective-permute-done.2.other_ref
  53.7 10.4 %train_step.1 = (bf16[768,896]{1,0:T(8,128)(2,1)}, f32[768,512]{1,0:T(8,128)S(1)}, bf16[768,512]{1,0:T(8,128)(2,1)S(1)}) custom-call(s32[1]{0:T(128)} %bitcast.core_ref, s32[1,128]{1,0:T(1,128)S(1)} %collective-permute-done.before_ref, s32[1,1536]{1,0:T(1,128)S(1)} %copy-done.2, s32[1,128]{1,0:T(1,128)S(1)} %collective-permute-done.1.after_ref, ...), custom_call_target="tpu_custom_call" | custom-call | tf_op jit(solution)/shard_map/train_step/pallas_call | solution.py:153
  64.1 1.9 %collective-permute-start.3 = (bf16[768,512]{1,0:T(8,128)(2,1)S(1)}, bf16[768,512]{1,0:T(8,128)(2,1)S(1)}, u32[]{:S(2)}, u32[]{:S(2)}) collective-permute-start(bf16[768,512]{1,0:T(8,128)(2,1)S(1)} %get-tuple-element.16), channel_id=1, source_target_pairs={{0,1},{1,0},{2,3},{3,2},{4,5},{5,4},{6,7},{7,6},{8,9},{9,8},{10,11... | collective-permute-start | bytes 2359304 | tf_op jit(solution)/shard_map/ppermute | solution.py:274
  66.0 2.3 %collective-permute-done.3 = bf16[768,512]{1,0:T(8,128)(2,1)S(1)} collective-permute-done((bf16[768,512]{1,0:T(8,128)(2,1)S(1)}, bf16[768,512]{1,0:T(8,128)(2,1)S(1)}, u32[]{:S(2)}, u32[]{:S(2)}) %collective-permute-start.3) | collective-permute-done | bytes 786464 | tf_op jit(solution)/shard_map/ppermute | solution.py:274
  68.3 0.3 add_convert_fusion
  68.5 26.8 %all_to_all.16.in_ref = bf16[32,24,512]{2,1,0:T(8,128)(2,1)S(1)} all-to-all(bf16[32,24,512]{2,1,0:T(8,128)(2,1)S(1)} %bitcast.20), channel_id=1, replica_groups=mesh['dp'=32,'seq'=16] {'dp'}, dimensions={0} | all-to-all | bytes 1572864 | tf_op jit(solution)/shard_map/all_to_all | solution.py:276
  95.4 0.1 add_up.2
  95.5 18.1 %all_to_all.17.in_ref = bf16[8,24,512]{2,1,0:T(8,128)(2,1)S(1)} all-to-all(bf16[8,24,512]{2,1,0:T(8,128)(2,1)S(1)} %add_up.2), channel_id=1, replica_groups={{0,2,4,6,8,10,12,14},{1,3,5,7,9,11,13,15},{16,18,20,22,24,26,28,30},{17..., dimensions={0} | all-to-all | bytes 393216 | tf_op jit(solution)/shard_map/all_to_all | solution.py:289
  113.6 6.0 %collective-permute-start.4 = (f32[24,512]{1,0:T(8,128)S(1)}, f32[24,512]{1,0:T(8,128)S(1)}, u32[]{:S(2)}, u32[]{:S(2)}) collective-permute-start(f32[24,512]{1,0:T(8,128)S(1)} %bitcast.15), channel_id=1, source_target_pairs={{0,1},{1,0},{2,3},{3,2},{4,5},{5,4},{6,7},{7,6},{8,9},{9,8},{10,11... | collective-permute-start | bytes 147464 | tf_op jit(solution)/shard_map/ppermute | solution.py:291
  119.6 0.9 collective-permute-done.4.across_ref
  120.5 0.7 unpack.1
  (11 shorter events, 0.1 us)
Async XLA Ops:
  0.6 53.1 %copy-start = (bf16[1,768,896]{2,1,0:T(8,128)(2,1)S(1)}, bf16[1,768,896]{2,1,0:T(8,128)(2,1)}, u32[]{:S(2)}) copy-start(bf16[1,768,896]{2,1,0:T(8,128)(2,1)} %param.13) | copy-start | bytes 4128772
  0.6 0.9 copy-start.1
  1.5 0.7 copy-start.3
  2.3 0.7 copy-start.4
  2.9 0.7 copy-start.5
  3.6 0.7 copy-start.6
  4.2 39.3 %copy-start.2 = (s32[1,1536]{1,0:T(1,128)S(1)}, s32[1,1536]{1,0:T(1,128)}, u32[]{:S(2)}) copy-start(s32[1,1536]{1,0:T(1,128)} %bases_ref.1) | copy-start | bytes 18436
  38.8 14.9 %collective-permute-start.2 = (bf16[768,512]{1,0:T(8,128)(2,1)S(1)}, bf16[768,512]{1,0:T(8,128)(2,1)S(1)}, u32[]{:S(2)}, u32[]{:S(2)}) collective-permute-start(bf16[768,512]{1,0:T(8,128)(2,1)S(1)} %bitcast.12), channel_id=1, source_target_pairs={{0,1},{1,0},{2,3},{3,2},{4,5},{5,4},{6,7},{7,6},{8,9},{9,8},{10,11... | collective-permute-start | bytes 2359304 | tf_op jit(solution)/shard_map/ppermute | solution.py:270
  43.6 9.5 %collective-permute-start.1 = (s32[1,128]{1,0:T(1,128)S(1)}, s32[1,128]{1,0:T(1,128)S(1)}, u32[]{:S(2)}, u32[]{:S(2)}) collective-permute-start(s32[1,128]{1,0:T(1,128)S(1)} %get-tuple-element.22), channel_id=1, source_target_pairs={{1,0},{2,1},{3,2},{4,3},{5,4},{6,5},{7,6},{8,7},{9,8},{10,9},{11,1... | collective-permute-start | bytes 1544 | tf_op jit(solution)/shard_map/ppermute | solution.py:258
  45.5 8.3 %collective-permute-start = (s32[1,128]{1,0:T(1,128)S(1)}, s32[1,128]{1,0:T(1,128)S(1)}, u32[]{:S(2)}, u32[]{:S(2)}) collective-permute-start(s32[1,128]{1,0:T(1,128)S(1)} %get-tuple-element.23), channel_id=1, source_target_pairs={{0,1},{1,2},{2,3},{3,4},{4,5},{5,6},{6,7},{7,8},{8,9},{9,10},{10,1... | collective-permute-start | bytes 1544 | tf_op jit(solution)/shard_map/ppermute | solution.py:257
  64.1 4.2 %collective-permute-start.3 = (bf16[768,512]{1,0:T(8,128)(2,1)S(1)}, bf16[768,512]{1,0:T(8,128)(2,1)S(1)}, u32[]{:S(2)}, u32[]{:S(2)}) collective-permute-start(bf16[768,512]{1,0:T(8,128)(2,1)S(1)} %get-tuple-element.16), channel_id=1, source_target_pairs={{0,1},{1,0},{2,3},{3,2},{4,5},{5,4},{6,7},{7,6},{8,9},{9,8},{10,11... | collective-permute-start | bytes 2359304 | tf_op jit(solution)/shard_map/ppermute | solution.py:274
  113.6 6.8 %collective-permute-start.4 = (f32[24,512]{1,0:T(8,128)S(1)}, f32[24,512]{1,0:T(8,128)S(1)}, u32[]{:S(2)}, u32[]{:S(2)}) collective-permute-start(f32[24,512]{1,0:T(8,128)S(1)} %bitcast.15), channel_id=1, source_target_pairs={{0,1},{1,0},{2,3},{3,2},{4,5},{5,4},{6,7},{7,6},{8,9},{9,8},{10,11... | collective-permute-start | bytes 147464 | tf_op jit(solution)/shard_map/ppermute | solution.py:291

commit v3 on v2

--- a/solution.py
+++ b/solution.py
@@ -24,7 +24,7 @@
     return lax.broadcasted_iota(jnp.int32, shape, dim)
 
 
-def step_kernel(dims, core_ref, before_ref, bases_ref, after_ref, own_ref, other_ref, cot_ref,
+def step_kernel(dims, core_ref, inner_ref, bases_ref, outer_ref, own_ref, other_ref, cot_ref,
                 pooled_ref, mine_ref, theirs_ref,
                 w_ref, code_ref, perm_ref, feat_ref, we_ref, wide_ref, emb_ref, ga_ref, s_ref, ge_ref, gew_ref):
     kw, shards, d0, d1, rows, tile, chunk = dims
@@ -40,15 +40,17 @@
     def _():
         w_ref[:, :half] = own_ref[...]
         w_ref[:, half:] = other_ref[...]
+        code_ref[:, :LANES] = outer_ref[...].astype(F32)
+        code_ref[:, LANES + rows:] = inner_ref[...].astype(F32)
 
     @pl.when(core != 0)
     def _():
         w_ref[:, :half] = other_ref[...]
         w_ref[:, half:] = own_ref[...]
-
-    code_ref[:, :LANES] = before_ref[...].astype(F32)
+        code_ref[:, :LANES] = inner_ref[...].astype(F32)
+        code_ref[:, LANES + rows:] = outer_ref[...].astype(F32)
+
     code_ref[:, LANES:LANES + rows] = (bases_ref[...] + 1).astype(F32)
-    code_ref[:, LANES + rows:] = after_ref[...].astype(F32)
 
     wide = w_ref[:, d1:].astype(F32)
     wide_ref[...] = wide
@@ -142,7 +144,7 @@
         halves(theirs_ref, mine_ref)
 
 
-def train_step(core, before, bases, after, own, other, cot, kw, shards):
+def train_step(core, inner, bases, outer, own, other, cot, kw, shards):
     d0, half = own.shape
     pairs, d1 = cot.shape
     rows = 2 * pairs
@@ -174,14 +176,31 @@
         ],
         compiler_params=pltpu.CompilerParams(vmem_limit_bytes=28 << 20),
         name="train_step",
-    )(core, before, bases, after, own, other, cot)
-
-
-def pack_kernel(core_ref, embed_ref, embed_bias_ref, gain_ref, proj_ref, proj_bias_ref, out_ref, rows_ref, block_ref):
+    )(core, inner, bases, outer, own, other, cot)
+
+
+def pack_kernel(core_ref, bases_hbm, embed_hbm, embed_bias_hbm, gain_hbm, proj_hbm, proj_bias_hbm,
+                out_ref, inner_ref, outer_ref,
+                bases_ref, embed_ref, embed_bias_ref, gain_ref, proj_ref, proj_bias_ref, rows_ref, block_ref, sems):
     kw, block, d1 = embed_ref.shape[0], proj_ref.shape[0], proj_ref.shape[1]
     copies, _, half = out_ref.shape
     taps, per = kw * 4, proj_bias_ref.shape[1]
+    fetched = [
+        pltpu.make_async_copy(source, target, sems.at[n])
+        for n, (source, target) in enumerate((
+            (bases_hbm, bases_ref), (embed_hbm, embed_ref), (embed_bias_hbm, embed_bias_ref),
+            (gain_hbm, gain_ref), (proj_hbm, proj_ref), (proj_bias_hbm, proj_bias_ref)))
+    ]
+    for copy in fetched:
+        copy.start()
     rows_ref[...] = jnp.zeros_like(rows_ref)
+    for copy in fetched:
+        copy.wait()
+    first = bases_ref[:, :LANES] + 1
+    last = bases_ref[:, bases_ref.shape[1] - LANES:] + 1
+    even = core_ref[0] == 0
+    inner_ref[...] = jnp.where(even, last, first)
+    outer_ref[...] = jnp.where(even, first, last)
     for k in range(kw):
         rows_ref[4 * k:4 * k + 4, :block] = embed_ref[k].astype(F32)
     rows_ref[taps:taps + 1, :block] = embed_bias_ref[...].astype(F32)
@@ -190,12 +209,12 @@
     block_ref[:1, 64:64 + per] = proj_bias_ref[...].astype(F32)
     edge = d1 - half
 
-    @pl.when(core_ref[0] == 0)
+    @pl.when(even)
     def _():
         for i in range(copies):
             out_ref[i] = proj_ref[:, :half]
 
-    @pl.when(core_ref[0] != 0)
+    @pl.when(jnp.logical_not(even))
     def _():
         for i in range(copies):
             out_ref[i, :, :edge] = proj_ref[:, half:]
@@ -253,23 +272,30 @@
     core = (lax.axis_index("seq") & 1).astype(jnp.int32).reshape(1)
     swap = [(i, i ^ 1) for i in range(members)]
 
-    codes = bases + 1
-    before = lax.ppermute(codes[:, -LANES:], "seq", [(i, i + 1) for i in range(members - 1)])
-    after = lax.ppermute(codes[:, :LANES], "seq", [(i + 1, i) for i in range(members - 1)])
-
-    piece = pl.pallas_call(
+    facing = [(i, i + 1 if i % 2 else i - 1) for i in range(1, members - 1)]
+
+    hbm = pl.BlockSpec(memory_space=pltpu.HBM)
+    gathered = (bases, embed_weight, embed_bias[None], norm_gain[None], proj_weight, proj_bias[None])
+    piece, inner, outer = pl.pallas_call(
         pack_kernel,
-        out_shape=jax.ShapeDtypeStruct((shards, block, half), BF16),
-        in_specs=[SMEM] + [VMEM] * 5,
-        out_specs=VMEM,
-        scratch_shapes=[pltpu.VMEM((LANES, LANES), F32), pltpu.VMEM((block, LANES), F32)],
-        compiler_params=pltpu.CompilerParams(vmem_limit_bytes=4 << 20),
+        out_shape=(
+            jax.ShapeDtypeStruct((shards, block, half), BF16),
+            jax.ShapeDtypeStruct((1, LANES), jnp.int32),
+            jax.ShapeDtypeStruct((1, LANES), jnp.int32),
+        ),
+        in_specs=[SMEM] + [hbm] * 6,
+        out_specs=(VMEM,) * 3,
+        scratch_shapes=[pltpu.VMEM(x.shape, x.dtype) for x in gathered] + [
+            pltpu.VMEM((LANES, LANES), F32), pltpu.VMEM((block, LANES), F32), pltpu.SemaphoreType.DMA((6,))],
+        compiler_params=pltpu.CompilerParams(vmem_limit_bytes=60 << 20),
         name="pack",
-    )(core, embed_weight, embed_bias[None], norm_gain[None], proj_weight, proj_bias[None])
+    )(core, *gathered)
+    inner = lax.ppermute(inner, "seq", swap)
+    outer = lax.ppermute(outer, "seq", facing)
     own = lax.all_to_all(piece, "dp", 0, 0, tiled=True).reshape(shards * block, half)
     other = lax.ppermute(own, "seq", swap)
 
-    pooled, mine, theirs = train_step(core, before, bases, after, own, other, cotangent[0], kw, shards)
+    pooled, mine, theirs = train_step(core, inner, bases, outer, own, other, cotangent[0], kw, shards)
 
     came = lax.ppermute(theirs, "seq", swap)
     summed = (mine + came.astype(F32)).astype(BF16).reshape(shards, block, half)

time: 122 us -> 119 us (0.975)
  local copies, waits for them, and re-layouts: 3.57 us -> 0.02 us
  starting transfers between devices: 22 us -> 18.6 us
  waiting for transfers between devices: 3.8 us -> 6.72 us
  Pallas kernels: 11.4 us -> 13.3 us
    unnamed x14 -> x8, local copies, waits for them, and re-layouts: 3.57 us -> 0.02 us
    ppermute x2, waiting for transfers between devices: 0.69 us -> 3.61 us  [the longest x1 3.61 us: local(): outer = lax.ppermute(outer, 'seq', facing)]
    ppermute x2, starting transfers between devices: 9.47 us -> 7.06 us  [the longest x1 5.14 us: local(): outer = lax.ppermute(outer, 'seq', facing)]
    pallas_call x1, Pallas kernels: 0.17 us -> 2.06 us  [local(): pl.pallas_call(pack_kernel, out_shape=(jax.ShapeDtypeStruct((shards, bloc...]
where the time goes in v3:
time: 119 us; the launch traced here: 118 us
  blocking collectives  78.5 us (66%)
  starting transfers between devices  18.6 us (16%)
  Pallas kernels  13.3 us (11%)
  waiting for transfers between devices  6.72 us (6%)
    all_to_all x1, blocking collectives, local(): lax.all_to_all(piece, 'dp', 0, 0, tiled=True).reshape(shards * block, half)  34.6 us
    all_to_all x1, blocking collectives, local(): parts = lax.all_to_all(summed, 'dp', 0, 0, tiled=True)  26.8 us
    all_to_all x1, blocking collectives, local(): lax.all_to_all(add_up(parts, 1.0, members // 2, BF16), 'seq', 0, 0, axis_...  17.1 us
    pallas_call x1, Pallas kernels, train_step(): pl.pallas_call(functools.partial(step_kernel, dims), out_shape=(jax.Shape...  10.4 us
    ppermute x1, starting transfers between devices, local(): outer = lax.ppermute(outer, 'seq', facing)  5.14 us
    ppermute x1, starting transfers between devices, local(): across = lax.ppermute(total, 'seq', swap)  4.94 us
    ppermute x1, starting transfers between devices, local(): other = lax.ppermute(own, 'seq', swap)  4.72 us
    ppermute x1, waiting for transfers between devices, local(): outer = lax.ppermute(outer, 'seq', facing)  3.61 us
  transfers between devices with their start and end apart: 5, of which 3 were waited for; matrix products, arithmetic and copies ran while one was open for 0% of the time, Pallas kernels for 0%

profile of v3, /device:TPU:1, one launch (start us, length us, event | category | flops | bytes accessed | tf_op | source)
XLA Modules:
  0.0 118.2 jit_solution(13331794290455773141)
XLA Ops:
  0.6 0.0 copy-start.1
  0.6 0.0 copy-start
  0.7 2.1 %pack.1 = (bf16[32,24,512]{2,1,0:T(8,128)(2,1)}, s32[1,128]{1,0:T(1,128)}, s32[1,128]{1,0:T(1,128)}) custom-call(s32[1]{0:T(128)} %bitcast.core_ref, s32[1,1536]{1,0:T(1,128)} %bases_ref.1, bf16[15,4,24]{2,1,0:T(4,128)(2,1)} %embed_hbm.1, bf16[1,24]{1,0:T(2,128)(2,1)} %bitcast.18, bf16[1,24]{1,0:T(2,128)(2,1)} %bitcast.19, bf16[24,896]{1,0:T(8,128)(2,1)} %proj_hbm.1, ...), custom_call_target="tpu_custom_call" | custom-call | tf_op jit(solution)/shard_map/pack/pallas_call | solution.py:279
  2.7 0.0 copy-start.3
  2.7 0.0 copy-start.2
  2.8 34.6 %all_to_all.15 = bf16[32,24,512]{2,1,0:T(8,128)(2,1)S(1)} all-to-all(bf16[32,24,512]{2,1,0:T(8,128)(2,1)} %get-tuple-element.19), channel_id=1, replica_groups=mesh['dp'=32,'seq'=16] {'dp'}, dimensions={0} | all-to-all | bytes 1572864 | tf_op jit(solution)/shard_map/all_to_all | solution.py:295
  37.4 4.7 %collective-permute-start.2 = (bf16[768,512]{1,0:T(8,128)(2,1)S(1)}, bf16[768,512]{1,0:T(8,128)(2,1)S(1)}, u32[]{:S(2)}, u32[]{:S(2)}) collective-permute-start(bf16[768,512]{1,0:T(8,128)(2,1)S(1)} %bitcast.12), channel_id=1, source_target_pairs={{0,1},{1,0},{2,3},{3,2},{4,5},{5,4},{6,7},{7,6},{8,9},{9,8},{10,11... | collective-permute-start | bytes 2359304 | tf_op jit(solution)/shard_map/ppermute | solution.py:296
  42.1 0.0 copy-done.3
  42.1 1.9 %collective-permute-start = (s32[1,128]{1,0:T(1,128)S(1)}, s32[1,128]{1,0:T(1,128)S(1)}, u32[]{:S(2)}, u32[]{:S(2)}) collective-permute-start(s32[1,128]{1,0:T(1,128)S(1)} %copy-done.3), channel_id=1, source_target_pairs={{0,1},{1,0},{2,3},{3,2},{4,5},{5,4},{6,7},{7,6},{8,9},{9,8},{10,11... | collective-permute-start | bytes 1544 | tf_op jit(solution)/shard_map/ppermute | solution.py:293
  44.0 0.0 copy-done.2
  44.1 5.1 %collective-permute-start.1 = (s32[1,128]{1,0:T(1,128)S(1)}, s32[1,128]{1,0:T(1,128)S(1)}, u32[]{:S(2)}, u32[]{:S(2)}) collective-permute-start(s32[1,128]{1,0:T(1,128)S(1)} %copy-done.2), channel_id=1, source_target_pairs={{1,2},{2,1},{3,4},{4,3},{5,6},{6,5},{7,8},{8,7},{9,10},{10,9},{11,... | collective-permute-start | bytes 1544 | tf_op jit(solution)/shard_map/ppermute | solution.py:294
  49.2 0.0 collective-permute-done.inner_ref
  49.2 3.6 %collective-permute-done.1.outer_ref = s32[1,128]{1,0:T(1,128)S(1)} collective-permute-done((s32[1,128]{1,0:T(1,128)S(1)}, s32[1,128]{1,0:T(1,128)S(1)}, u32[]{:S(2)}, u32[]{:S(2)}) %collective-permute-start.1) | collective-permute-done | bytes 544 | tf_op jit(solution)/shard_map/ppermute | solution.py:294
  52.8 0.0 collective-permute-done.2.other_ref
  52.8 10.4 %train_step.1 = (bf16[768,896]{1,0:T(8,128)(2,1)}, f32[768,512]{1,0:T(8,128)S(1)}, bf16[768,512]{1,0:T(8,128)(2,1)S(1)}) custom-call(s32[1]{0:T(128)} %bitcast.core_ref, s32[1,128]{1,0:T(1,128)S(1)} %collective-permute-done.inner_ref, s32[1,1536]{1,0:T(1,128)S(1)} %copy-done.1, s32[1,128]{1,0:T(1,128)S(1)} %collective-permute-done.1.outer_ref, ...), custom_call_target="tpu_custom_call" | custom-call | tf_op jit(solution)/shard_map/train_step/pallas_call | solution.py:155
  63.2 1.9 %collective-permute-start.3 = (bf16[768,512]{1,0:T(8,128)(2,1)S(1)}, bf16[768,512]{1,0:T(8,128)(2,1)S(1)}, u32[]{:S(2)}, u32[]{:S(2)}) collective-permute-start(bf16[768,512]{1,0:T(8,128)(2,1)S(1)} %get-tuple-element.22), channel_id=1, source_target_pairs={{0,1},{1,0},{2,3},{3,2},{4,5},{5,4},{6,7},{7,6},{8,9},{9,8},{10,11... | collective-permute-start | bytes 2359304 | tf_op jit(solution)/shard_map/ppermute | solution.py:300
  65.1 2.3 %collective-permute-done.3 = bf16[768,512]{1,0:T(8,128)(2,1)S(1)} collective-permute-done((bf16[768,512]{1,0:T(8,128)(2,1)S(1)}, bf16[768,512]{1,0:T(8,128)(2,1)S(1)}, u32[]{:S(2)}, u32[]{:S(2)}) %collective-permute-start.3) | collective-permute-done | bytes 786464 | tf_op jit(solution)/shard_map/ppermute | solution.py:300
  67.4 0.3 add_convert_fusion
  67.6 26.8 %all_to_all.16.in_ref = bf16[32,24,512]{2,1,0:T(8,128)(2,1)S(1)} all-to-all(bf16[32,24,512]{2,1,0:T(8,128)(2,1)S(1)} %bitcast.17), channel_id=1, replica_groups=mesh['dp'=32,'seq'=16] {'dp'}, dimensions={0} | all-to-all | bytes 1572864 | tf_op jit(solution)/shard_map/all_to_all | solution.py:302
  94.4 0.1 add_up.2
  94.6 17.1 %all_to_all.17.in_ref = bf16[8,24,512]{2,1,0:T(8,128)(2,1)S(1)} all-to-all(bf16[8,24,512]{2,1,0:T(8,128)(2,1)S(1)} %add_up.2), channel_id=1, replica_groups={{0,2,4,6,8,10,12,14},{1,3,5,7,9,11,13,15},{16,18,20,22,24,26,28,30},{17..., dimensions={0} | all-to-all | bytes 393216 | tf_op jit(solution)/shard_map/all_to_all | solution.py:315
  111.7 4.9 %collective-permute-start.4 = (f32[24,512]{1,0:T(8,128)S(1)}, f32[24,512]{1,0:T(8,128)S(1)}, u32[]{:S(2)}, u32[]{:S(2)}) collective-permute-start(f32[24,512]{1,0:T(8,128)S(1)} %bitcast.15), channel_id=1, source_target_pairs={{0,1},{1,0},{2,3},{3,2},{4,5},{5,4},{6,7},{7,6},{8,9},{9,8},{10,11... | collective-permute-start | bytes 147464 | tf_op jit(solution)/shard_map/ppermute | solution.py:317
  116.6 0.9 collective-permute-done.4.across_ref
  117.5 0.7 unpack.1
  (3 shorter events, 0.0 us)
Async XLA Ops:
  0.6 52.2 %copy-start.1 = (s32[1,1536]{1,0:T(1,128)S(1)}, s32[1,1536]{1,0:T(1,128)}, u32[]{:S(2)}) copy-start(s32[1,1536]{1,0:T(1,128)} %bases_ref.1) | copy-start | bytes 18436
  0.6 52.2 %copy-start = (bf16[1,768,896]{2,1,0:T(8,128)(2,1)S(1)}, bf16[1,768,896]{2,1,0:T(8,128)(2,1)}, u32[]{:S(2)}) copy-start(bf16[1,768,896]{2,1,0:T(8,128)(2,1)} %param.13) | copy-start | bytes 4128772
  2.7 39.4 %copy-start.3 = (s32[1,128]{1,0:T(1,128)S(1)}, s32[1,128]{1,0:T(1,128)}, u32[]{:S(2)}) copy-start(s32[1,128]{1,0:T(1,128)} %get-tuple-element.17) | copy-start | bytes 1540
  2.7 41.3 %copy-start.2 = (s32[1,128]{1,0:T(1,128)S(1)}, s32[1,128]{1,0:T(1,128)}, u32[]{:S(2)}) copy-start(s32[1,128]{1,0:T(1,128)} %get-tuple-element.18) | copy-start | bytes 1540
  37.4 15.4 %collective-permute-start.2 = (bf16[768,512]{1,0:T(8,128)(2,1)S(1)}, bf16[768,512]{1,0:T(8,128)(2,1)S(1)}, u32[]{:S(2)}, u32[]{:S(2)}) collective-permute-start(bf16[768,512]{1,0:T(8,128)(2,1)S(1)} %bitcast.12), channel_id=1, source_target_pairs={{0,1},{1,0},{2,3},{3,2},{4,5},{5,4},{6,7},{7,6},{8,9},{9,8},{10,11... | collective-permute-start | bytes 2359304 | tf_op jit(solution)/shard_map/ppermute | solution.py:296
  42.1 7.1 %collective-permute-start = (s32[1,128]{1,0:T(1,128)S(1)}, s32[1,128]{1,0:T(1,128)S(1)}, u32[]{:S(2)}, u32[]{:S(2)}) collective-permute-start(s32[1,128]{1,0:T(1,128)S(1)} %copy-done.3), channel_id=1, source_target_pairs={{0,1},{1,0},{2,3},{3,2},{4,5},{5,4},{6,7},{7,6},{8,9},{9,8},{10,11... | collective-permute-start | bytes 1544 | tf_op jit(solution)/shard_map/ppermute | solution.py:293
  44.1 8.8 %collective-permute-start.1 = (s32[1,128]{1,0:T(1,128)S(1)}, s32[1,128]{1,0:T(1,128)S(1)}, u32[]{:S(2)}, u32[]{:S(2)}) collective-permute-start(s32[1,128]{1,0:T(1,128)S(1)} %copy-done.2), channel_id=1, source_target_pairs={{1,2},{2,1},{3,4},{4,3},{5,6},{6,5},{7,8},{8,7},{9,10},{10,9},{11,... | collective-permute-start | bytes 1544 | tf_op jit(solution)/shard_map/ppermute | solution.py:294
  63.2 4.2 %collective-permute-start.3 = (bf16[768,512]{1,0:T(8,128)(2,1)S(1)}, bf16[768,512]{1,0:T(8,128)(2,1)S(1)}, u32[]{:S(2)}, u32[]{:S(2)}) collective-permute-start(bf16[768,512]{1,0:T(8,128)(2,1)S(1)} %get-tuple-element.22), channel_id=1, source_target_pairs={{0,1},{1,0},{2,3},{3,2},{4,5},{5,4},{6,7},{7,6},{8,9},{9,8},{10,11... | collective-permute-start | bytes 2359304 | tf_op jit(solution)/shard_map/ppermute | solution.py:300
  111.7 5.8 %collective-permute-start.4 = (f32[24,512]{1,0:T(8,128)S(1)}, f32[24,512]{1,0:T(8,128)S(1)}, u32[]{:S(2)}, u32[]{:S(2)}) collective-permute-start(f32[24,512]{1,0:T(8,128)S(1)} %bitcast.15), channel_id=1, source_target_pairs={{0,1},{1,0},{2,3},{3,2},{4,5},{5,4},{6,7},{7,6},{8,9},{9,8},{10,11... | collective-permute-start | bytes 147464 | tf_op jit(solution)/shard_map/ppermute | solution.py:317

commit v4 on v3

--- a/solution.py
+++ b/solution.py
@@ -293,6 +293,7 @@
     inner = lax.ppermute(inner, "seq", swap)
     outer = lax.ppermute(outer, "seq", facing)
     own = lax.all_to_all(piece, "dp", 0, 0, tiled=True).reshape(shards * block, half)
+    own, inner, outer = lax.optimization_barrier((own, inner, outer))
     other = lax.ppermute(own, "seq", swap)
 
     pooled, mine, theirs = train_step(core, inner, bases, outer, own, other, cotangent[0], kw, shards)

time: 119 us -> 109 us (0.916)
  blocking collectives: 78.5 us -> 41.9 us
  starting transfers between devices: 18.6 us -> 34.7 us
  waiting for transfers between devices: 6.72 us -> 17.5 us
    all_to_all x1 -> x0, blocking collectives: 34.6 us -> none  [local(): lax.all_to_all(piece, 'dp', 0, 0, tiled=True).reshape(shards * block, half)]
    all_to_all x0 -> x1, starting transfers between devices: none -> 14.3 us  [local(): lax.all_to_all(piece, 'dp', 0, 0, tiled=True).reshape(shards * block, half)]
    ppermute x1, waiting for transfers between devices: 3.61 us -> 9.17 us  [local(): outer = lax.ppermute(outer, 'seq', facing)]
    all_to_all x0 -> x1, waiting for transfers between devices: none -> 3.68 us  [local(): lax.all_to_all(piece, 'dp', 0, 0, tiled=True).reshape(shards * block, half)]
    ppermute x1, waiting for transfers between devices: 0.01 us -> 1.89 us  [local(): other = lax.ppermute(own, 'seq', swap)]
  transfers between devices with their start and end apart: 5 -> 6, of which waited for: 3 -> 5; matrix products, arithmetic and copies ran while one was open for 0% -> 0% of each run, Pallas kernels for 0% -> 0%
where the time goes in v4:
time: 109 us
  blocking collectives  41.9 us (38%)
  starting transfers between devices  34.7 us (32%)
  waiting for transfers between devices  17.5 us (16%)
  Pallas kernels  13.5 us (12%)
    all_to_all x1, blocking collectives, local(): parts = lax.all_to_all(summed, 'dp', 0, 0, tiled=True)  25.8 us
    all_to_all x1, blocking collectives, local(): lax.all_to_all(add_up(parts, 1.0, members // 2, BF16), 'seq', 0, 0, axis_...  16.1 us
    all_to_all x1, starting transfers between devices, local(): lax.all_to_all(piece, 'dp', 0, 0, tiled=True).reshape(shards * block, half)  14.3 us
    pallas_call x1, Pallas kernels, train_step(): pl.pallas_call(functools.partial(step_kernel, dims), out_shape=(jax.Shape...  10.6 us
    ppermute x1, waiting for transfers between devices, local(): outer = lax.ppermute(outer, 'seq', facing)  9.17 us
    ppermute x1, starting transfers between devices, local(): across = lax.ppermute(total, 'seq', swap)  5.97 us
    ppermute x1, starting transfers between devices, local(): other = lax.ppermute(own, 'seq', swap)  4.72 us
    ppermute x1, starting transfers between devices, local(): outer = lax.ppermute(outer, 'seq', facing)  4.65 us
  transfers between devices with their start and end apart: 6, of which 5 were waited for; matrix products, arithmetic and copies ran while one was open for 0% of the time, Pallas kernels for 0%

profile of v4, /device:TPU:1, one launch (start us, length us, event | category | flops | bytes accessed | tf_op | source)
XLA Modules:
  0.0 108.6 jit_solution(4917179741688480396)
XLA Ops:
  0.6 0.0 copy-start.1
  0.6 0.0 copy-start
  0.7 2.1 %pack.1 = (bf16[32,24,512]{2,1,0:T(8,128)(2,1)}, s32[1,128]{1,0:T(1,128)}, s32[1,128]{1,0:T(1,128)}) custom-call(s32[1]{0:T(128)} %bitcast.core_ref, s32[1,1536]{1,0:T(1,128)} %bases_ref.1, bf16[15,4,24]{2,1,0:T(4,128)(2,1)} %embed_hbm.1, bf16[1,24]{1,0:T(2,128)(2,1)} %bitcast.18, bf16[1,24]{1,0:T(2,128)(2,1)} %bitcast.19, bf16[24,896]{1,0:T(8,128)(2,1)} %proj_hbm.1, ...), custom_call_target="tpu_custom_call" | custom-call | tf_op jit(solution)/shard_map/pack/pallas_call | solution.py:279
  2.7 0.0 copy-start.3
  2.7 0.0 copy-start.2
  2.8 14.3 %all-to-all-start = ((bf16[32,24,512]{2,1,0:T(8,128)(2,1)}), bf16[32,24,512]{2,1,0:T(8,128)(2,1)S(1)}, u32[]{:S(2)}, u32[]{:S(2)}) async-start(bf16[32,24,512]{2,1,0:T(8,128)(2,1)} %get-tuple-element.20), calls=%async_computation | async-start | bytes 1572864 | tf_op jit(solution)/shard_map/all_to_all | solution.py:295
  17.1 2.8 %collective-permute-start = (s32[1,128]{1,0:T(1,128)S(1)}, s32[1,128]{1,0:T(1,128)S(1)}, u32[]{:S(2)}, u32[]{:S(2)}) collective-permute-start(s32[1,128]{1,0:T(1,128)S(1)} %copy-done.3), channel_id=1, source_target_pairs={{0,1},{1,0},{2,3},{3,2},{4,5},{5,4},{6,7},{7,6},{8,9},{9,8},{10,11... | collective-permute-start | bytes 1544 | tf_op jit(solution)/shard_map/ppermute | solution.py:293
  19.9 4.7 %collective-permute-start.1 = (s32[1,128]{1,0:T(1,128)S(1)}, s32[1,128]{1,0:T(1,128)S(1)}, u32[]{:S(2)}, u32[]{:S(2)}) collective-permute-start(s32[1,128]{1,0:T(1,128)S(1)} %copy-done.2), channel_id=1, source_target_pairs={{1,2},{2,1},{3,4},{4,3},{5,6},{6,5},{7,8},{8,7},{9,10},{10,9},{11,... | collective-permute-start | bytes 1544 | tf_op jit(solution)/shard_map/ppermute | solution.py:294
  24.5 0.0 collective-permute-done.inner_ref
  24.6 9.2 %collective-permute-done.1.outer_ref = s32[1,128]{1,0:T(1,128)S(1)} collective-permute-done((s32[1,128]{1,0:T(1,128)S(1)}, s32[1,128]{1,0:T(1,128)S(1)}, u32[]{:S(2)}, u32[]{:S(2)}) %collective-permute-start.1) | collective-permute-done | bytes 544 | tf_op jit(solution)/shard_map/ppermute | solution.py:294
  33.7 3.7 %all-to-all-done = bf16[32,24,512]{2,1,0:T(8,128)(2,1)S(1)} async-done(((bf16[32,24,512]{2,1,0:T(8,128)(2,1)}), bf16[32,24,512]{2,1,0:T(8,128)(2,1)S(1)}, u32[]{:S(2)}, u32[]{:S(2)}) %all-to-all-start) | async-done | bytes 786464 | tf_op jit(solution)/shard_map/all_to_all | solution.py:295
  37.4 4.7 %collective-permute-start.2 = (bf16[768,512]{1,0:T(8,128)(2,1)S(1)}, bf16[768,512]{1,0:T(8,128)(2,1)S(1)}, u32[]{:S(2)}, u32[]{:S(2)}) collective-permute-start(bf16[768,512]{1,0:T(8,128)(2,1)S(1)} %bitcast.12), channel_id=1, source_target_pairs={{0,1},{1,0},{2,3},{3,2},{4,5},{5,4},{6,7},{7,6},{8,9},{9,8},{10,11... | collective-permute-start | bytes 2359304 | tf_op jit(solution)/shard_map/ppermute | solution.py:297
  42.1 1.9 %collective-permute-done.2.other_ref = bf16[768,512]{1,0:T(8,128)(2,1)S(1)} collective-permute-done((bf16[768,512]{1,0:T(8,128)(2,1)S(1)}, bf16[768,512]{1,0:T(8,128)(2,1)S(1)}, u32[]{:S(2)}, u32[]{:S(2)}) %collective-permute-start.2) | collective-permute-done | bytes 786464 | tf_op jit(solution)/shard_map/ppermute | solution.py:297
  44.0 0.0 copy-done.1
  44.0 10.6 %train_step.1 = (bf16[768,896]{1,0:T(8,128)(2,1)}, f32[768,512]{1,0:T(8,128)S(1)}, bf16[768,512]{1,0:T(8,128)(2,1)S(1)}) custom-call(s32[1]{0:T(128)} %bitcast.core_ref, s32[1,128]{1,0:T(1,128)S(1)} %collective-permute-done.inner_ref, s32[1,1536]{1,0:T(1,128)S(1)} %copy-done.1, s32[1,128]{1,0:T(1,128)S(1)} %collective-permute-done.1.outer_ref, ...), custom_call_target="tpu_custom_call" | custom-call | tf_op jit(solution)/shard_map/train_step/pallas_call | solution.py:155
  54.6 2.3 %collective-permute-start.3 = (bf16[768,512]{1,0:T(8,128)(2,1)S(1)}, bf16[768,512]{1,0:T(8,128)(2,1)S(1)}, u32[]{:S(2)}, u32[]{:S(2)}) collective-permute-start(bf16[768,512]{1,0:T(8,128)(2,1)S(1)} %get-tuple-element.28), channel_id=1, source_target_pairs={{0,1},{1,0},{2,3},{3,2},{4,5},{5,4},{6,7},{7,6},{8,9},{9,8},{10,11... | collective-permute-start | bytes 2359304 | tf_op jit(solution)/shard_map/ppermute | solution.py:301
  56.9 1.9 %collective-permute-done.3 = bf16[768,512]{1,0:T(8,128)(2,1)S(1)} collective-permute-done((bf16[768,512]{1,0:T(8,128)(2,1)S(1)}, bf16[768,512]{1,0:T(8,128)(2,1)S(1)}, u32[]{:S(2)}, u32[]{:S(2)}) %collective-permute-start.3) | collective-permute-done | bytes 786464 | tf_op jit(solution)/shard_map/ppermute | solution.py:301
  58.8 0.3 add_convert_fusion
  59.0 25.8 %all_to_all.15.in_ref = bf16[32,24,512]{2,1,0:T(8,128)(2,1)S(1)} all-to-all(bf16[32,24,512]{2,1,0:T(8,128)(2,1)S(1)} %bitcast.17), channel_id=1, replica_groups=mesh['dp'=32,'seq'=16] {'dp'}, dimensions={0} | all-to-all | bytes 1572864 | tf_op jit(solution)/shard_map/all_to_all | solution.py:303
  84.8 0.1 add_up.2
  84.9 16.1 %all_to_all.16.in_ref = bf16[8,24,512]{2,1,0:T(8,128)(2,1)S(1)} all-to-all(bf16[8,24,512]{2,1,0:T(8,128)(2,1)S(1)} %add_up.2), channel_id=1, replica_groups={{0,2,4,6,8,10,12,14},{1,3,5,7,9,11,13,15},{16,18,20,22,24,26,28,30},{17..., dimensions={0} | all-to-all | bytes 393216 | tf_op jit(solution)/shard_map/all_to_all | solution.py:316
  101.1 6.0 %collective-permute-start.4 = (f32[24,512]{1,0:T(8,128)S(1)}, f32[24,512]{1,0:T(8,128)S(1)}, u32[]{:S(2)}, u32[]{:S(2)}) collective-permute-start(f32[24,512]{1,0:T(8,128)S(1)} %bitcast.15), channel_id=1, source_target_pairs={{0,1},{1,0},{2,3},{3,2},{4,5},{5,4},{6,7},{7,6},{8,9},{9,8},{10,11... | collective-permute-start | bytes 147464 | tf_op jit(solution)/shard_map/ppermute | solution.py:318
  107.1 0.9 collective-permute-done.4.across_ref
  107.9 0.7 unpack.1
  (4 shorter events, 0.0 us)
Async XLA Ops:
  0.6 43.4 %copy-start.1 = (s32[1,1536]{1,0:T(1,128)S(1)}, s32[1,1536]{1,0:T(1,128)}, u32[]{:S(2)}) copy-start(s32[1,1536]{1,0:T(1,128)} %bases_ref.1) | copy-start | bytes 18436
  0.6 43.4 %copy-start = (bf16[1,768,896]{2,1,0:T(8,128)(2,1)S(1)}, bf16[1,768,896]{2,1,0:T(8,128)(2,1)}, u32[]{:S(2)}) copy-start(bf16[1,768,896]{2,1,0:T(8,128)(2,1)} %param.13) | copy-start | bytes 4128772
  2.7 14.3 %copy-start.3 = (s32[1,128]{1,0:T(1,128)S(1)}, s32[1,128]{1,0:T(1,128)}, u32[]{:S(2)}) copy-start(s32[1,128]{1,0:T(1,128)} %get-tuple-element.21) | copy-start | bytes 1540
  2.7 17.1 %copy-start.2 = (s32[1,128]{1,0:T(1,128)S(1)}, s32[1,128]{1,0:T(1,128)}, u32[]{:S(2)}) copy-start(s32[1,128]{1,0:T(1,128)} %get-tuple-element.22) | copy-start | bytes 1540
  2.8 34.7 %all-to-all-start = ((bf16[32,24,512]{2,1,0:T(8,128)(2,1)}), bf16[32,24,512]{2,1,0:T(8,128)(2,1)S(1)}, u32[]{:S(2)}, u32[]{:S(2)}) async-start(bf16[32,24,512]{2,1,0:T(8,128)(2,1)} %get-tuple-element.20), calls=%async_computation | async-start | bytes 1572864 | tf_op jit(solution)/shard_map/all_to_all | solution.py:295
  17.1 7.5 %collective-permute-start = (s32[1,128]{1,0:T(1,128)S(1)}, s32[1,128]{1,0:T(1,128)S(1)}, u32[]{:S(2)}, u32[]{:S(2)}) collective-permute-start(s32[1,128]{1,0:T(1,128)S(1)} %copy-done.3), channel_id=1, source_target_pairs={{0,1},{1,0},{2,3},{3,2},{4,5},{5,4},{6,7},{7,6},{8,9},{9,8},{10,11... | collective-permute-start | bytes 1544 | tf_op jit(solution)/shard_map/ppermute | solution.py:293
  19.9 13.8 %collective-permute-start.1 = (s32[1,128]{1,0:T(1,128)S(1)}, s32[1,128]{1,0:T(1,128)S(1)}, u32[]{:S(2)}, u32[]{:S(2)}) collective-permute-start(s32[1,128]{1,0:T(1,128)S(1)} %copy-done.2), channel_id=1, source_target_pairs={{1,2},{2,1},{3,4},{4,3},{5,6},{6,5},{7,8},{8,7},{9,10},{10,9},{11,... | collective-permute-start | bytes 1544 | tf_op jit(solution)/shard_map/ppermute | solution.py:294
  37.4 6.6 %collective-permute-start.2 = (bf16[768,512]{1,0:T(8,128)(2,1)S(1)}, bf16[768,512]{1,0:T(8,128)(2,1)S(1)}, u32[]{:S(2)}, u32[]{:S(2)}) collective-permute-start(bf16[768,512]{1,0:T(8,128)(2,1)S(1)} %bitcast.12), channel_id=1, source_target_pairs={{0,1},{1,0},{2,3},{3,2},{4,5},{5,4},{6,7},{7,6},{8,9},{9,8},{10,11... | collective-permute-start | bytes 2359304 | tf_op jit(solution)/shard_map/ppermute | solution.py:297
  54.6 4.2 %collective-permute-start.3 = (bf16[768,512]{1,0:T(8,128)(2,1)S(1)}, bf16[768,512]{1,0:T(8,128)(2,1)S(1)}, u32[]{:S(2)}, u32[]{:S(2)}) collective-permute-start(bf16[768,512]{1,0:T(8,128)(2,1)S(1)} %get-tuple-element.28), channel_id=1, source_target_pairs={{0,1},{1,0},{2,3},{3,2},{4,5},{5,4},{6,7},{7,6},{8,9},{9,8},{10,11... | collective-permute-start | bytes 2359304 | tf_op jit(solution)/shard_map/ppermute | solution.py:301
  101.1 6.8 %collective-permute-start.4 = (f32[24,512]{1,0:T(8,128)S(1)}, f32[24,512]{1,0:T(8,128)S(1)}, u32[]{:S(2)}, u32[]{:S(2)}) collective-permute-start(f32[24,512]{1,0:T(8,128)S(1)} %bitcast.15), channel_id=1, source_target_pairs={{0,1},{1,0},{2,3},{3,2},{4,5},{5,4},{6,7},{7,6},{8,9},{9,8},{10,11... | collective-permute-start | bytes 147464 | tf_op jit(solution)/shard_map/ppermute | solution.py:318

commit v5 on v3

--- a/solution.py
+++ b/solution.py
@@ -24,47 +24,29 @@
     return lax.broadcasted_iota(jnp.int32, shape, dim)
 
 
-def step_kernel(dims, core_ref, inner_ref, bases_ref, outer_ref, own_ref, other_ref, cot_ref,
-                pooled_ref, mine_ref, theirs_ref,
-                w_ref, code_ref, perm_ref, feat_ref, we_ref, wide_ref, emb_ref, ga_ref, s_ref, ge_ref, gew_ref):
-    kw, shards, d0, d1, rows, tile, chunk = dims
-    half = w_ref.shape[1] // 2
-    pairs, pair_tile = rows // 2, tile // 2
-    reach = kw // 2
-    taps = kw * 4
-    core = core_ref[0]
+def by_owner(shards, d1):
     per = d1 // shards
-    block = d0 // shards
-
-    @pl.when(core == 0)
-    def _():
-        w_ref[:, :half] = own_ref[...]
-        w_ref[:, half:] = other_ref[...]
-        code_ref[:, :LANES] = outer_ref[...].astype(F32)
-        code_ref[:, LANES + rows:] = inner_ref[...].astype(F32)
-
-    @pl.when(core != 0)
-    def _():
-        w_ref[:, :half] = other_ref[...]
-        w_ref[:, half:] = own_ref[...]
-        code_ref[:, :LANES] = inner_ref[...].astype(F32)
-        code_ref[:, LANES + rows:] = outer_ref[...].astype(F32)
-
-    code_ref[:, LANES:LANES + rows] = (bases_ref[...] + 1).astype(F32)
-
-    wide = w_ref[:, d1:].astype(F32)
-    wide_ref[...] = wide
-    we_ref[...] = wide.T.astype(BF16)
-    gain = we_ref[pl.ds(64 - 8, 8), :].astype(F32)[5:6, :]
-    gain_y = gain * GELU_K
-
     column = iota((LANES, d1), 1)
     owner = (column * 2341) >> 16
     spread = (iota((LANES, d1), 0) == column - owner * per + 64).astype(F32)
-    owned = owner[:shards] == iota((shards, d1), 0)
-    pieces = wide_ref[pl.ds(0, shards, stride=block), :]
-    bias = jnp.sum(jnp.where(owned, dot(pieces.astype(BF16), spread.astype(BF16), (1, 0)), 0.0), axis=0, keepdims=True)
-
+    return owner[:shards] == iota((shards, d1), 0), spread
+
+
+def feature_kernel(kw, tile, core_ref, inner_ref, bases_ref, outer_ref, cot_ref, feat_ref, sums_ref, code_ref, perm_ref):
+    rows = bases_ref.shape[1]
+    pair_tile, reach, taps = tile // 2, kw // 2, kw * 4
+
+    @pl.when(core_ref[0] == 0)
+    def _():
+        code_ref[:, :LANES] = outer_ref[...].astype(F32)
+        code_ref[:, LANES + rows:] = inner_ref[...].astype(F32)
+
+    @pl.when(core_ref[0] != 0)
+    def _():
+        code_ref[:, :LANES] = inner_ref[...].astype(F32)
+        code_ref[:, LANES + rows:] = outer_ref[...].astype(F32)
+
+    code_ref[:, LANES:LANES + rows] = (bases_ref[...] + 1).astype(F32)
     source, place = iota((tile, tile), 0), iota((tile, tile), 1)
     perm_ref[...] = (source == jnp.where(place < pair_tile, 2 * place, 2 * (place - pair_tile) + 1)).astype(BF16)
     repeat = ((iota((LANES, 16), 0) >> 2) == iota((LANES, 16), 1)).astype(BF16)
@@ -78,6 +60,42 @@
         hot = ((spreaded == letter.astype(F32)) & (line < taps)) | (line == taps)
         ordered = dot(hot.astype(F32).astype(BF16), perm_ref[...], (1, 0))
         feat_ref[:, t * tile:(t + 1) * tile] = ordered.astype(BF16)
+
+    shards = sums_ref.shape[0]
+    owned, spread = by_owner(shards, cot_ref.shape[1])
+    sums = 4.0 * jnp.sum(cot_ref[...].astype(F32), axis=0, keepdims=True)
+    sums_ref[...] = dot(jnp.where(owned, sums, 0.0), spread, (1, 1), lax.Precision.HIGHEST)
+
+
+def step_kernel(dims, core_ref, feat_ref, sums_ref, own_ref, other_ref, cot_ref,
+                theirs_ref, s_ref, wide_ref, bias_ref,
+                w_ref, we_ref, emb_ref, ga_ref, ge_ref, gew_ref):
+    kw, shards, d0, d1, rows, tile, chunk = dims
+    half = w_ref.shape[1] // 2
+    pair_tile = tile // 2
+    taps = kw * 4
+    core = core_ref[0]
+    block = d0 // shards
+
+    @pl.when(core == 0)
+    def _():
+        w_ref[:, :half] = own_ref[...]
+        w_ref[:, half:] = other_ref[...]
+
+    @pl.when(core != 0)
+    def _():
+        w_ref[:, :half] = other_ref[...]
+        w_ref[:, half:] = own_ref[...]
+
+    wide = w_ref[:, d1:].astype(F32)
+    wide_ref[...] = wide
+    we_ref[...] = wide.T.astype(BF16)
+    gain = we_ref[pl.ds(64 - 8, 8), :].astype(F32)[5:6, :]
+    gain_y = gain * GELU_K
+
+    owned, spread = by_owner(shards, d1)
+    pieces = wide_ref[pl.ds(0, shards, stride=block), :]
+    bias_ref[...] = jnp.sum(jnp.where(owned, dot(pieces.astype(BF16), spread.astype(BF16), (1, 0)), 0.0), axis=0, keepdims=True)
 
     for t in range(rows // tile):
         at = t * tile
@@ -115,8 +133,6 @@
 
         start_total = jnp.zeros((8, d0), F32)
         gain_total = lax.fori_loop(0, pair_tile // chunk, body, start_total, unroll=True)
-        pooled_ref[half_at:half_at + pair_tile, :] = (
-            (0.25 / GELU_K) * dot(s_ref[half_at:half_at + pair_tile, :], w_ref[:, :d1], (1, 0)) + bias).astype(BF16)
         part = dot(feat_ref[:, at:at + tile], ge_ref[at:at + tile, :], (1, 0))
         is_gain = iota((LANES, d0), 0) == taps + 1
         part = jnp.where(is_gain, jnp.sum(gain_total, axis=0, keepdims=True) / gain_y, part)
@@ -126,57 +142,129 @@
             gew_ref[...] += part
 
     wide_ref[...] = gew_ref[...].T
-    sums = 4.0 * jnp.sum(cot_ref[...].astype(F32), axis=0, keepdims=True)
-    pieces = dot(jnp.where(owned, sums, 0.0), spread, (1, 1), lax.Precision.HIGHEST)
-    wide_ref[pl.ds(0, shards, stride=block), :] = wide_ref[pl.ds(0, shards, stride=block), :] + pieces
-
-    def halves(first_ref, second_ref):
-        first_ref[...] = (dot(s_ref[...], cot_ref[:, :half], (0, 0)) * (1.0 / GELU_K)).astype(first_ref.dtype)
-        second_ref[:, :d1 - half] = (dot(s_ref[...], cot_ref[:, half:], (0, 0)) * (1.0 / GELU_K)).astype(second_ref.dtype)
-        second_ref[:, d1 - half:] = wide_ref[...].astype(second_ref.dtype)
+    wide_ref[pl.ds(0, shards, stride=block), :] = wide_ref[pl.ds(0, shards, stride=block), :] + sums_ref[...]
 
     @pl.when(core == 0)
     def _():
-        halves(mine_ref, theirs_ref)
+        right_half(s_ref, cot_ref, wide_ref, theirs_ref)
 
     @pl.when(core != 0)
     def _():
-        halves(theirs_ref, mine_ref)
-
-
-def train_step(core, inner, bases, outer, own, other, cot, kw, shards):
+        left_half(s_ref, cot_ref, theirs_ref)
+
+
+def left_half(s_ref, cot_ref, out_ref):
+    half = out_ref.shape[1]
+    out_ref[...] = (dot(s_ref[...], cot_ref[:, :half], (0, 0)) * (1.0 / GELU_K)).astype(out_ref.dtype)
+
+
+def right_half(s_ref, cot_ref, wide_ref, out_ref):
+    half = out_ref.shape[1]
+    edge = cot_ref.shape[1] - half
+    out_ref[:, :edge] = (dot(s_ref[...], cot_ref[:, half:], (0, 0)) * (1.0 / GELU_K)).astype(out_ref.dtype)
+    out_ref[:, edge:] = wide_ref[...].astype(out_ref.dtype)
+
+
+def keep_kernel(core_ref, s_ref, cot_ref, wide_ref, mine_ref):
+    @pl.when(core_ref[0] == 0)
+    def _():
+        left_half(s_ref, cot_ref, mine_ref)
+
+    @pl.when(core_ref[0] != 0)
+    def _():
+        right_half(s_ref, cot_ref, wide_ref, mine_ref)
+
+
+def pool_kernel(core_ref, s_ref, own_ref, other_ref, bias_ref, pooled_ref):
+    half = own_ref.shape[1]
+    edge = pooled_ref.shape[1] - half
+
+    def project(left_ref, right_ref):
+        pooled_ref[:, :half] = ((0.25 / GELU_K) * dot(s_ref[...], left_ref[...], (1, 0)) + bias_ref[:, :half]).astype(BF16)
+        pooled_ref[:, half:] = ((0.25 / GELU_K) * dot(s_ref[...], right_ref[:, :edge], (1, 0)) + bias_ref[:, half:]).astype(BF16)
+
+    @pl.when(core_ref[0] == 0)
+    def _():
+        project(own_ref, other_ref)
+
+    @pl.when(core_ref[0] != 0)
+    def _():
+        project(other_ref, own_ref)
+
+
+VMEM = pl.BlockSpec(memory_space=pltpu.VMEM)
+SMEM = pl.BlockSpec(memory_space=pltpu.SMEM)
+TILE, CHUNK = 512, 32
+
+
+def make_features(core, inner, bases, outer, cot, kw, shards):
+    rows = bases.shape[1]
+    return pl.pallas_call(
+        functools.partial(feature_kernel, kw, TILE),
+        out_shape=(jax.ShapeDtypeStruct((LANES, rows), BF16), jax.ShapeDtypeStruct((shards, LANES), F32)),
+        in_specs=[SMEM] + [VMEM] * 4,
+        out_specs=(VMEM, VMEM),
+        scratch_shapes=[pltpu.VMEM((1, rows + 2 * LANES), F32), pltpu.VMEM((TILE, TILE), BF16)],
+        compiler_params=pltpu.CompilerParams(vmem_limit_bytes=16 << 20),
+        cost_estimate=pl.CostEstimate(flops=2 * LANES * TILE * rows, bytes_accessed=2 << 20, transcendentals=0),
+        name="features",
+    )(core, inner, bases, outer, cot)
+
+
+def backward(core, feat, sums, own, other, cot, kw, shards):
     d0, half = own.shape
     pairs, d1 = cot.shape
     rows = 2 * pairs
-    width = 2 * half
-    tile, chunk = 512, 32
-    dims = (kw, shards, d0, d1, rows, tile, chunk)
-    vmem = pl.BlockSpec(memory_space=pltpu.VMEM)
+    dims = (kw, shards, d0, d1, rows, TILE, CHUNK)
     return pl.pallas_call(
         functools.partial(step_kernel, dims),
         out_shape=(
-            jax.ShapeDtypeStruct((pairs, d1), BF16),
-            jax.ShapeDtypeStruct((d0, half), F32),
             jax.ShapeDtypeStruct((d0, half), BF16),
+            jax.ShapeDtypeStruct((pairs, d0), BF16),
+            jax.ShapeDtypeStruct((d0, LANES), F32),
+            jax.ShapeDtypeStruct((1, d1), F32),
         ),
-        in_specs=[pl.BlockSpec(memory_space=pltpu.SMEM)] + [vmem] * 6,
-        out_specs=(vmem, vmem, vmem),
+        in_specs=[SMEM] + [VMEM] * 5,
+        out_specs=(VMEM,) * 4,
         scratch_shapes=[
-            pltpu.VMEM((d0, width), BF16),
-            pltpu.VMEM((1, rows + 2 * LANES), F32),
-            pltpu.VMEM((tile, tile), BF16),
-            pltpu.VMEM((LANES, rows), BF16),
+            pltpu.VMEM((d0, 2 * half), BF16),
             pltpu.VMEM((LANES, d0), BF16),
-            pltpu.VMEM((d0, LANES), F32),
             pltpu.VMEM((rows, d0), BF16),
             pltpu.VMEM((pairs, d0), F32),
-            pltpu.VMEM((pairs, d0), BF16),
             pltpu.VMEM((rows, d0), BF16),
             pltpu.VMEM((LANES, d0), F32),
         ],
         compiler_params=pltpu.CompilerParams(vmem_limit_bytes=28 << 20),
-        name="train_step",
-    )(core, inner, bases, outer, own, other, cot)
+        cost_estimate=pl.CostEstimate(flops=6 * pairs * d0 * d1, bytes_accessed=6 << 20, transcendentals=rows * d0),
+        name="backward",
+    )(core, feat, sums, own, other, cot)
+
+
+def keep_half(core, s, cot, wide, half):
+    pairs, d0 = s.shape
+    return pl.pallas_call(
+        keep_kernel,
+        out_shape=jax.ShapeDtypeStruct((d0, half), F32),
+        in_specs=[SMEM] + [VMEM] * 3,
+        out_specs=VMEM,
+        compiler_params=pltpu.CompilerParams(vmem_limit_bytes=16 << 20),
+        cost_estimate=pl.CostEstimate(flops=2 * pairs * d0 * half, bytes_accessed=4 << 20, transcendentals=0),
+        name="keep_half",
+    )(core, s, cot, wide)
+
+
+def pool(core, s, own, other, bias):
+    pairs, d0 = s.shape
+    d1 = bias.shape[1]
+    return pl.pallas_call(
+        pool_kernel,
+        out_shape=jax.ShapeDtypeStruct((pairs, d1), BF16),
+        in_specs=[SMEM] + [VMEM] * 4,
+        out_specs=VMEM,
+        compiler_params=pltpu.CompilerParams(vmem_limit_bytes=16 << 20),
+        cost_estimate=pl.CostEstimate(flops=2 * pairs * d0 * d1, bytes_accessed=4 << 20, transcendentals=0),
+        name="pool",
+    )(core, s, own, other, bias)
 
 
 def pack_kernel(core_ref, bases_hbm, embed_hbm, embed_bias_hbm, gain_hbm, proj_hbm, proj_bias_hbm,
@@ -259,10 +347,6 @@
     gain_ref[...] = rows_ref[taps + 1:taps + 2, :block]
 
 
-VMEM = pl.BlockSpec(memory_space=pltpu.VMEM)
-SMEM = pl.BlockSpec(memory_space=pltpu.SMEM)
-
-
 def local(bases, embed_weight, embed_bias, norm_gain, proj_weight, proj_bias, cotangent):
     kw = embed_weight.shape[0]
     shards, members = lax.axis_size("dp"), lax.axis_size("seq")
@@ -293,11 +377,15 @@
     inner = lax.ppermute(inner, "seq", swap)
     outer = lax.ppermute(outer, "seq", facing)
     own = lax.all_to_all(piece, "dp", 0, 0, tiled=True).reshape(shards * block, half)
+    feat, sums = make_features(core, inner, bases, outer, cotangent[0], kw, shards)
+    own, feat, sums = lax.optimization_barrier((own, feat, sums))
     other = lax.ppermute(own, "seq", swap)
 
-    pooled, mine, theirs = train_step(core, inner, bases, outer, own, other, cotangent[0], kw, shards)
-
+    cot = cotangent[0]
+    theirs, s, wide, bias = backward(core, feat, sums, own, other, cot, kw, shards)
     came = lax.ppermute(theirs, "seq", swap)
+    mine = keep_half(core, s, cot, wide, half)
+    pooled = pool(core, s, own, other, bias)
     summed = (mine + came.astype(F32)).astype(BF16).reshape(shards, block, half)
     parts = lax.all_to_all(summed, "dp", 0, 0, tiled=True)
 

time: 119 us -> 107 us (0.90)
  blocking collectives: 78.5 us -> 41.9 us
  starting transfers between devices: 18.6 us -> 34.7 us
  waiting for transfers between devices: 6.72 us -> 14.3 us
    all_to_all x1 -> x0, blocking collectives: 34.6 us -> none  [local(): lax.all_to_all(piece, 'dp', 0, 0, tiled=True).reshape(shards * block, half)]
    all_to_all x0 -> x1, starting transfers between devices: none -> 14.3 us  [local(): lax.all_to_all(piece, 'dp', 0, 0, tiled=True).reshape(shards * block, half)]
    ppermute x1, waiting for transfers between devices: 3.61 us -> 9.17 us  [local(): outer = lax.ppermute(outer, 'seq', facing)]
    all_to_all x0 -> x1, waiting for transfers between devices: none -> 2.1 us  [local(): lax.all_to_all(piece, 'dp', 0, 0, tiled=True).reshape(shards * block, half)]
    ppermute x1, waiting for transfers between devices: 0.01 us -> 1.89 us  [local(): other = lax.ppermute(own, 'seq', swap)]
    pallas_call x1 -> x4, Pallas kernels: 10.4 us -> 11.5 us  [the longest x1 6.59 us: backward(): pl.pallas_call(functools.partial(step_kernel, dims), out_shape=(jax.Shape...]
  transfers between devices with their start and end apart: 5 -> 6, of which waited for: 3 -> 4; matrix products, arithmetic and copies ran while one was open for 0% -> 0% of each run, Pallas kernels for 0% -> 5%
where the time goes in v5:
time: 107 us; the launch traced here: 106 us
  blocking collectives  41.9 us (39%)
  starting transfers between devices  34.7 us (32%)
  Pallas kernels  14.4 us (13%)
  waiting for transfers between devices  14.3 us (13%)
    all_to_all x1, blocking collectives, local(): parts = lax.all_to_all(summed, 'dp', 0, 0, tiled=True)  25.8 us
    all_to_all x1, blocking collectives, local(): lax.all_to_all(add_up(parts, 1.0, members // 2, BF16), 'seq', 0, 0, axis_...  16.1 us
    all_to_all x1, starting transfers between devices, local(): lax.all_to_all(piece, 'dp', 0, 0, tiled=True).reshape(shards * block, half)  14.3 us
    ppermute x1, waiting for transfers between devices, local(): outer = lax.ppermute(outer, 'seq', facing)  9.17 us
    pallas_call x1, Pallas kernels, backward(): pl.pallas_call(functools.partial(step_kernel, dims), out_shape=(jax.Shape...  6.59 us
    ppermute x1, starting transfers between devices, local(): across = lax.ppermute(total, 'seq', swap)  5.96 us
    ppermute x1, starting transfers between devices, local(): other = lax.ppermute(own, 'seq', swap)  4.72 us
    ppermute x1, starting transfers between devices, local(): outer = lax.ppermute(outer, 'seq', facing)  4.65 us
  transfers between devices with their start and end apart: 6, of which 4 were waited for; matrix products, arithmetic and copies ran while one was open for 0% of the time, Pallas kernels for 5%

profile of v5, /device:TPU:1, one launch (start us, length us, event | category | flops | bytes accessed | tf_op | source)
XLA Modules:
  0.0 106.3 jit_solution(246762533849185738)
XLA Ops:
  0.7 2.1 %pack.1 = (bf16[32,24,512]{2,1,0:T(8,128)(2,1)}, s32[1,128]{1,0:T(1,128)}, s32[1,128]{1,0:T(1,128)}) custom-call(s32[1]{0:T(128)} %bitcast.core_ref, s32[1,1536]{1,0:T(1,128)} %bases_ref.1, bf16[15,4,24]{2,1,0:T(4,128)(2,1)} %embed_hbm.1, bf16[1,24]{1,0:T(2,128)(2,1)} %bitcast.22, bf16[1,24]{1,0:T(2,128)(2,1)} %bitcast.23, bf16[24,896]{1,0:T(8,128)(2,1)} %proj_hbm.1, ...), custom_call_target="tpu_custom_call" | custom-call | tf_op jit(solution)/shard_map/pack/pallas_call | solution.py:363
  2.7 0.0 copy-start.3
  2.7 0.0 copy-start.2
  2.8 14.3 %all-to-all-start = ((bf16[32,24,512]{2,1,0:T(8,128)(2,1)}), bf16[32,24,512]{2,1,0:T(8,128)(2,1)S(1)}, u32[]{:S(2)}, u32[]{:S(2)}) async-start(bf16[32,24,512]{2,1,0:T(8,128)(2,1)} %get-tuple-element.23), calls=%async_computation | async-start | bytes 1572864 | tf_op jit(solution)/shard_map/all_to_all | solution.py:379
  17.1 2.8 %collective-permute-start = (s32[1,128]{1,0:T(1,128)S(1)}, s32[1,128]{1,0:T(1,128)S(1)}, u32[]{:S(2)}, u32[]{:S(2)}) collective-permute-start(s32[1,128]{1,0:T(1,128)S(1)} %copy-done.3), channel_id=1, source_target_pairs={{0,1},{1,0},{2,3},{3,2},{4,5},{5,4},{6,7},{7,6},{8,9},{9,8},{10,11... | collective-permute-start | bytes 1544 | tf_op jit(solution)/shard_map/ppermute | solution.py:377
  19.9 4.7 %collective-permute-start.1 = (s32[1,128]{1,0:T(1,128)S(1)}, s32[1,128]{1,0:T(1,128)S(1)}, u32[]{:S(2)}, u32[]{:S(2)}) collective-permute-start(s32[1,128]{1,0:T(1,128)S(1)} %copy-done.2), channel_id=1, source_target_pairs={{1,2},{2,1},{3,4},{4,3},{5,6},{6,5},{7,8},{8,7},{9,10},{10,9},{11,... | collective-permute-start | bytes 1544 | tf_op jit(solution)/shard_map/ppermute | solution.py:378
  24.5 0.0 collective-permute-done.inner_ref
  24.6 9.2 %collective-permute-done.1.outer_ref = s32[1,128]{1,0:T(1,128)S(1)} collective-permute-done((s32[1,128]{1,0:T(1,128)S(1)}, s32[1,128]{1,0:T(1,128)S(1)}, u32[]{:S(2)}, u32[]{:S(2)}) %collective-permute-start.1) | collective-permute-done | bytes 544 | tf_op jit(solution)/shard_map/ppermute | solution.py:378
  33.7 1.6 %features.1 = (bf16[128,1536]{1,0:T(8,128)(2,1)S(1)}, f32[32,128]{1,0:T(8,128)S(1)}) custom-call(s32[1]{0:T(128)} %bitcast.core_ref, s32[1,128]{1,0:T(1,128)S(1)} %collective-permute-done.inner_ref, s32[1,1536]{1,0:T(1,128)S(1)} %copy-done.1, s32[1,128]{1,0:T(1,128)S(1)} %collective-permute-done.1.outer_ref, bf16[768,896]{1,0:T(8,128)(2,1)S(1)} %bitcast.12), custom_call_target="tpu_custom_call" | custom-call | flops 201326592 | bytes 2097152 | tf_op jit(solution)/shard_map/features/pallas_call | solution.py:202
  35.3 2.1 %all-to-all-done = bf16[32,24,512]{2,1,0:T(8,128)(2,1)S(1)} async-done(((bf16[32,24,512]{2,1,0:T(8,128)(2,1)}), bf16[32,24,512]{2,1,0:T(8,128)(2,1)S(1)}, u32[]{:S(2)}, u32[]{:S(2)}) %all-to-all-start) | async-done | bytes 786464 | tf_op jit(solution)/shard_map/all_to_all | solution.py:379
  37.4 4.7 %collective-permute-start.2 = (bf16[768,512]{1,0:T(8,128)(2,1)S(1)}, bf16[768,512]{1,0:T(8,128)(2,1)S(1)}, u32[]{:S(2)}, u32[]{:S(2)}) collective-permute-start(bf16[768,512]{1,0:T(8,128)(2,1)S(1)} %bitcast.15), channel_id=1, source_target_pairs={{0,1},{1,0},{2,3},{3,2},{4,5},{5,4},{6,7},{7,6},{8,9},{9,8},{10,11... | collective-permute-start | bytes 2359304 | tf_op jit(solution)/shard_map/ppermute | solution.py:382
  42.1 1.9 %collective-permute-done.2.other_ref = bf16[768,512]{1,0:T(8,128)(2,1)S(1)} collective-permute-done((bf16[768,512]{1,0:T(8,128)(2,1)S(1)}, bf16[768,512]{1,0:T(8,128)(2,1)S(1)}, u32[]{:S(2)}, u32[]{:S(2)}) %collective-permute-start.2) | collective-permute-done | bytes 786464 | tf_op jit(solution)/shard_map/ppermute | solution.py:382
  44.0 6.6 %backward.1 = (bf16[768,512]{1,0:T(8,128)(2,1)S(1)}, bf16[768,768]{1,0:T(8,128)(2,1)S(1)}, f32[768,128]{1,0:T(8,128)S(1)}, f32[1,896]{1,0:T(1,128)S(1)}) custom-call(s32[1]{0:T(128)} %bitcast.core_ref, bf16[128,1536]{1,0:T(8,128)(2,1)S(1)} %get-tuple-element.28.feat_ref, f32[32,128]{1,0:T(8,128)S(1)} %get-tuple-element.29.sums_ref, ...), custom_call_target="tpu_custom_call" | custom-call | flops 3170893824 | bytes 6291456 | tf_op jit(solution)/shard_map/backward/pallas_call | solution.py:219
  50.6 2.2 %collective-permute-start.3 = (bf16[768,512]{1,0:T(8,128)(2,1)S(1)}, bf16[768,512]{1,0:T(8,128)(2,1)S(1)}, u32[]{:S(2)}, u32[]{:S(2)}) collective-permute-start(bf16[768,512]{1,0:T(8,128)(2,1)S(1)} %get-tuple-element.34), channel_id=1, source_target_pairs={{0,1},{1,0},{2,3},{3,2},{4,5},{5,4},{6,7},{7,6},{8,9},{9,8},{10,11... | collective-permute-start | bytes 2359304 | tf_op jit(solution)/shard_map/ppermute | solution.py:386
  52.9 0.8 keep_half.1
  53.7 1.1 %collective-permute-done.3 = bf16[768,512]{1,0:T(8,128)(2,1)S(1)} collective-permute-done((bf16[768,512]{1,0:T(8,128)(2,1)S(1)}, bf16[768,512]{1,0:T(8,128)(2,1)S(1)}, u32[]{:S(2)}, u32[]{:S(2)}) %collective-permute-start.3) | collective-permute-done | bytes 786464 | tf_op jit(solution)/shard_map/ppermute | solution.py:386
  54.8 0.3 add_convert_fusion
  55.1 25.8 %all_to_all.15.in_ref = bf16[32,24,512]{2,1,0:T(8,128)(2,1)S(1)} all-to-all(bf16[32,24,512]{2,1,0:T(8,128)(2,1)S(1)} %bitcast.20), channel_id=1, replica_groups=mesh['dp'=32,'seq'=16] {'dp'}, dimensions={0} | all-to-all | bytes 1572864 | tf_op jit(solution)/shard_map/all_to_all | solution.py:390
  80.8 0.1 add_up.2
  81.0 16.1 %all_to_all.16.in_ref = bf16[8,24,512]{2,1,0:T(8,128)(2,1)S(1)} all-to-all(bf16[8,24,512]{2,1,0:T(8,128)(2,1)S(1)} %add_up.2), channel_id=1, replica_groups={{0,2,4,6,8,10,12,14},{1,3,5,7,9,11,13,15},{16,18,20,22,24,26,28,30},{17..., dimensions={0} | all-to-all | bytes 393216 | tf_op jit(solution)/shard_map/all_to_all | solution.py:403
  97.1 6.0 %collective-permute-start.4 = (f32[24,512]{1,0:T(8,128)S(1)}, f32[24,512]{1,0:T(8,128)S(1)}, u32[]{:S(2)}, u32[]{:S(2)}) collective-permute-start(f32[24,512]{1,0:T(8,128)S(1)} %bitcast.18), channel_id=1, source_target_pairs={{0,1},{1,0},{2,3},{3,2},{4,5},{5,4},{6,7},{7,6},{8,9},{9,8},{10,11... | collective-permute-start | bytes 147464 | tf_op jit(solution)/shard_map/ppermute | solution.py:405
  103.1 2.5 %pool.1 = bf16[768,896]{1,0:T(8,128)(2,1)} custom-call(s32[1]{0:T(128)} %bitcast.core_ref, bf16[768,768]{1,0:T(8,128)(2,1)S(1)} %get-tuple-element.31.s_ref, bf16[768,512]{1,0:T(8,128)(2,1)S(1)} %bitcast.17, bf16[768,512]{1,0:T(8,128)(2,1)S(1)} %collective-permute-done.2.other_ref, f32[1,896]{1,0:T(1,128)S(1)} %get-tuple-element.32.bias_ref), custom_call_target="tpu_custom_call" | custom-call | flops 1056964608 | bytes 4194304 | tf_op jit(solution)/shard_map/pool/pallas_call | solution.py:259
  105.6 0.0 collective-permute-done.4.across_ref
  105.6 0.7 unpack.1
  (7 shorter events, 0.0 us)
Async XLA Ops:
  0.6 33.1 %copy-start.1 = (s32[1,1536]{1,0:T(1,128)S(1)}, s32[1,1536]{1,0:T(1,128)}, u32[]{:S(2)}) copy-start(s32[1,1536]{1,0:T(1,128)} %bases_ref.1) | copy-start | bytes 18436
  0.6 33.1 %copy-start = (bf16[1,768,896]{2,1,0:T(8,128)(2,1)S(1)}, bf16[1,768,896]{2,1,0:T(8,128)(2,1)}, u32[]{:S(2)}) copy-start(bf16[1,768,896]{2,1,0:T(8,128)(2,1)} %param.13) | copy-start | bytes 4128772
  2.7 14.3 %copy-start.3 = (s32[1,128]{1,0:T(1,128)S(1)}, s32[1,128]{1,0:T(1,128)}, u32[]{:S(2)}) copy-start(s32[1,128]{1,0:T(1,128)} %get-tuple-element.24) | copy-start | bytes 1540
  2.7 17.1 %copy-start.2 = (s32[1,128]{1,0:T(1,128)S(1)}, s32[1,128]{1,0:T(1,128)}, u32[]{:S(2)}) copy-start(s32[1,128]{1,0:T(1,128)} %get-tuple-element.25) | copy-start | bytes 1540
  2.8 34.7 %all-to-all-start = ((bf16[32,24,512]{2,1,0:T(8,128)(2,1)}), bf16[32,24,512]{2,1,0:T(8,128)(2,1)S(1)}, u32[]{:S(2)}, u32[]{:S(2)}) async-start(bf16[32,24,512]{2,1,0:T(8,128)(2,1)} %get-tuple-element.23), calls=%async_computation | async-start | bytes 1572864 | tf_op jit(solution)/shard_map/all_to_all | solution.py:379
  17.1 7.5 %collective-permute-start = (s32[1,128]{1,0:T(1,128)S(1)}, s32[1,128]{1,0:T(1,128)S(1)}, u32[]{:S(2)}, u32[]{:S(2)}) collective-permute-start(s32[1,128]{1,0:T(1,128)S(1)} %copy-done.3), channel_id=1, source_target_pairs={{0,1},{1,0},{2,3},{3,2},{4,5},{5,4},{6,7},{7,6},{8,9},{9,8},{10,11... | collective-permute-start | bytes 1544 | tf_op jit(solution)/shard_map/ppermute | solution.py:377
  19.9 13.8 %collective-permute-start.1 = (s32[1,128]{1,0:T(1,128)S(1)}, s32[1,128]{1,0:T(1,128)S(1)}, u32[]{:S(2)}, u32[]{:S(2)}) collective-permute-start(s32[1,128]{1,0:T(1,128)S(1)} %copy-done.2), channel_id=1, source_target_pairs={{1,2},{2,1},{3,4},{4,3},{5,6},{6,5},{7,8},{8,7},{9,10},{10,9},{11,... | collective-permute-start | bytes 1544 | tf_op jit(solution)/shard_map/ppermute | solution.py:378
  37.4 6.6 %collective-permute-start.2 = (bf16[768,512]{1,0:T(8,128)(2,1)S(1)}, bf16[768,512]{1,0:T(8,128)(2,1)S(1)}, u32[]{:S(2)}, u32[]{:S(2)}) collective-permute-start(bf16[768,512]{1,0:T(8,128)(2,1)S(1)} %bitcast.15), channel_id=1, source_target_pairs={{0,1},{1,0},{2,3},{3,2},{4,5},{5,4},{6,7},{7,6},{8,9},{9,8},{10,11... | collective-permute-start | bytes 2359304 | tf_op jit(solution)/shard_map/ppermute | solution.py:382
  50.6 4.2 %collective-permute-start.3 = (bf16[768,512]{1,0:T(8,128)(2,1)S(1)}, bf16[768,512]{1,0:T(8,128)(2,1)S(1)}, u32[]{:S(2)}, u32[]{:S(2)}) collective-permute-start(bf16[768,512]{1,0:T(8,128)(2,1)S(1)} %get-tuple-element.34), channel_id=1, source_target_pairs={{0,1},{1,0},{2,3},{3,2},{4,5},{5,4},{6,7},{7,6},{8,9},{9,8},{10,11... | collective-permute-start | bytes 2359304 | tf_op jit(solution)/shard_map/ppermute | solution.py:386
  97.1 8.5 %collective-permute-start.4 = (f32[24,512]{1,0:T(8,128)S(1)}, f32[24,512]{1,0:T(8,128)S(1)}, u32[]{:S(2)}, u32[]{:S(2)}) collective-permute-start(f32[24,512]{1,0:T(8,128)S(1)} %bitcast.18), channel_id=1, source_target_pairs={{0,1},{1,0},{2,3},{3,2},{4,5},{5,4},{6,7},{7,6},{8,9},{9,8},{10,11... | collective-permute-start | bytes 147464 | tf_op jit(solution)/shard_map/ppermute | solution.py:405

commit v6 on v5

--- a/solution.py
+++ b/solution.py
@@ -388,6 +388,7 @@
     pooled = pool(core, s, own, other, bias)
     summed = (mine + came.astype(F32)).astype(BF16).reshape(shards, block, half)
     parts = lax.all_to_all(summed, "dp", 0, 0, tiled=True)
+    parts, pooled = lax.optimization_barrier((parts, pooled))
 
     def add_up(parts, scale, copies, kind):
         return pl.pallas_call(

time: 107 us -> 108 us (level)
  blocking collectives: 41.9 us -> 16.5 us
  waiting for transfers between devices: 14.3 us -> 32.2 us
  starting transfers between devices: 34.7 us -> 39.5 us
  local copies, waits for them, and re-layouts: 0.02 us -> 2.92 us
    all_to_all x1 -> x0, blocking collectives: 25.8 us -> none  [local(): parts = lax.all_to_all(summed, 'dp', 0, 0, tiled=True)]
    all_to_all x0 -> x1, waiting for transfers between devices: none -> 17.9 us  [local(): parts = lax.all_to_all(summed, 'dp', 0, 0, tiled=True)]
    all_to_all x0 -> x1, starting transfers between devices: none -> 5.9 us  [local(): parts = lax.all_to_all(summed, 'dp', 0, 0, tiled=True)]
    unnamed x8 -> x16, local copies, waits for them, and re-layouts: 0.02 us -> 2.92 us
  transfers between devices with their start and end apart: 6 -> 7, of which waited for: 4 -> 6; matrix products, arithmetic and copies ran while one was open for 0% -> 0% of each run, Pallas kernels for 5% -> 5%
where the time goes in v6:
time: 108 us
  starting transfers between devices  39.5 us (37%)
  waiting for transfers between devices  32.2 us (30%)
  blocking collectives  16.5 us (15%)
  Pallas kernels  14.4 us (13%)
  local copies, waits for them, and re-layouts  2.92 us (3%)
  other arithmetic  1.15 us (1%)
    all_to_all x1, waiting for transfers between devices, local(): parts = lax.all_to_all(summed, 'dp', 0, 0, tiled=True)  17.9 us
    all_to_all x1, blocking collectives, local(): lax.all_to_all(add_up(parts, 1.0, members // 2, BF16), 'seq', 0, 0, axis_...  16.5 us
    all_to_all x1, starting transfers between devices, local(): lax.all_to_all(piece, 'dp', 0, 0, tiled=True).reshape(shards * block, half)  14.3 us
    ppermute x1, waiting for transfers between devices, local(): outer = lax.ppermute(outer, 'seq', facing)  9.17 us
    pallas_call x1, Pallas kernels, backward(): pl.pallas_call(functools.partial(step_kernel, dims), out_shape=(jax.Shape...  6.6 us
    all_to_all x1, starting transfers between devices, local(): parts = lax.all_to_all(summed, 'dp', 0, 0, tiled=True)  5.9 us
    ppermute x1, starting transfers between devices, local(): across = lax.ppermute(total, 'seq', swap)  4.9 us
    ppermute x1, starting transfers between devices, local(): other = lax.ppermute(own, 'seq', swap)  4.72 us
  transfers between devices with their start and end apart: 7, of which 6 were waited for; matrix products, arithmetic and copies ran while one was open for 0% of the time, Pallas kernels for 5%

profile of v6, /device:TPU:1, one launch (start us, length us, event | category | flops | bytes accessed | tf_op | source)
XLA Modules:
  0.0 107.5 jit_solution(14041144746611402052)
XLA Ops:
  0.7 2.1 %pack.1 = (bf16[32,24,512]{2,1,0:T(8,128)(2,1)}, s32[1,128]{1,0:T(1,128)}, s32[1,128]{1,0:T(1,128)}) custom-call(s32[1]{0:T(128)} %bitcast.core_ref, s32[1,1536]{1,0:T(1,128)} %bases_ref.1, bf16[15,4,24]{2,1,0:T(4,128)(2,1)} %embed_hbm.1, bf16[1,24]{1,0:T(2,128)(2,1)} %bitcast.22, bf16[1,24]{1,0:T(2,128)(2,1)} %bitcast.23, bf16[24,896]{1,0:T(8,128)(2,1)} %proj_hbm.1, ...), custom_call_target="tpu_custom_call" | custom-call | tf_op jit(solution)/shard_map/pack/pallas_call | solution.py:363
  2.8 14.3 %all-to-all-start = ((bf16[32,24,512]{2,1,0:T(8,128)(2,1)}), bf16[32,24,512]{2,1,0:T(8,128)(2,1)S(1)}, u32[]{:S(2)}, u32[]{:S(2)}) async-start(bf16[32,24,512]{2,1,0:T(8,128)(2,1)} %get-tuple-element.25), calls=%async_computation | async-start | bytes 1572864 | tf_op jit(solution)/shard_map/all_to_all | solution.py:379
  17.1 2.8 %collective-permute-start = (s32[1,128]{1,0:T(1,128)S(1)}, s32[1,128]{1,0:T(1,128)S(1)}, u32[]{:S(2)}, u32[]{:S(2)}) collective-permute-start(s32[1,128]{1,0:T(1,128)S(1)} %copy-done.7), channel_id=1, source_target_pairs={{0,1},{1,0},{2,3},{3,2},{4,5},{5,4},{6,7},{7,6},{8,9},{9,8},{10,11... | collective-permute-start | bytes 1544 | tf_op jit(solution)/shard_map/ppermute | solution.py:377
  19.9 4.7 %collective-permute-start.1 = (s32[1,128]{1,0:T(1,128)S(1)}, s32[1,128]{1,0:T(1,128)S(1)}, u32[]{:S(2)}, u32[]{:S(2)}) collective-permute-start(s32[1,128]{1,0:T(1,128)S(1)} %copy-done.6), channel_id=1, source_target_pairs={{1,2},{2,1},{3,4},{4,3},{5,6},{6,5},{7,8},{8,7},{9,10},{10,9},{11,... | collective-permute-start | bytes 1544 | tf_op jit(solution)/shard_map/ppermute | solution.py:378
  24.6 9.2 %collective-permute-done.1.outer_ref = s32[1,128]{1,0:T(1,128)S(1)} collective-permute-done((s32[1,128]{1,0:T(1,128)S(1)}, s32[1,128]{1,0:T(1,128)S(1)}, u32[]{:S(2)}, u32[]{:S(2)}) %collective-permute-start.1) | collective-permute-done | bytes 544 | tf_op jit(solution)/shard_map/ppermute | solution.py:378
  33.7 1.6 %features.1 = (bf16[128,1536]{1,0:T(8,128)(2,1)S(1)}, f32[32,128]{1,0:T(8,128)S(1)}) custom-call(s32[1]{0:T(128)} %bitcast.core_ref, s32[1,128]{1,0:T(1,128)S(1)} %collective-permute-done.inner_ref, s32[1,1536]{1,0:T(1,128)S(1)} %copy-done.3, s32[1,128]{1,0:T(1,128)S(1)} %collective-permute-done.1.outer_ref, bf16[768,896]{1,0:T(8,128)(2,1)S(1)} %bitcast.12), custom_call_target="tpu_custom_call" | custom-call | flops 201326592 | bytes 2097152 | tf_op jit(solution)/shard_map/features/pallas_call | solution.py:202
  35.3 0.8 copy-done.4
  36.1 1.3 %all-to-all-done = bf16[32,24,512]{2,1,0:T(8,128)(2,1)S(1)} async-done(((bf16[32,24,512]{2,1,0:T(8,128)(2,1)}), bf16[32,24,512]{2,1,0:T(8,128)(2,1)S(1)}, u32[]{:S(2)}, u32[]{:S(2)}) %all-to-all-start) | async-done | bytes 786464 | tf_op jit(solution)/shard_map/all_to_all | solution.py:379
  37.4 4.7 %collective-permute-start.2 = (bf16[768,512]{1,0:T(8,128)(2,1)S(1)}, bf16[768,512]{1,0:T(8,128)(2,1)S(1)}, u32[]{:S(2)}, u32[]{:S(2)}) collective-permute-start(bf16[768,512]{1,0:T(8,128)(2,1)S(1)} %bitcast.15), channel_id=1, source_target_pairs={{0,1},{1,0},{2,3},{3,2},{4,5},{5,4},{6,7},{7,6},{8,9},{9,8},{10,11... | collective-permute-start | bytes 2359304 | tf_op jit(solution)/shard_map/ppermute | solution.py:382
  42.1 1.9 %collective-permute-done.2.other_ref = bf16[768,512]{1,0:T(8,128)(2,1)S(1)} collective-permute-done((bf16[768,512]{1,0:T(8,128)(2,1)S(1)}, bf16[768,512]{1,0:T(8,128)(2,1)S(1)}, u32[]{:S(2)}, u32[]{:S(2)}) %collective-permute-start.2) | collective-permute-done | bytes 786464 | tf_op jit(solution)/shard_map/ppermute | solution.py:382
  44.0 1.0 copy-done.5
  45.0 6.6 %backward.1 = (bf16[768,512]{1,0:T(8,128)(2,1)S(1)}, bf16[768,768]{1,0:T(8,128)(2,1)S(1)}, f32[768,128]{1,0:T(8,128)S(1)}, f32[1,896]{1,0:T(1,128)S(1)}) custom-call(s32[1]{0:T(128)} %bitcast.core_ref, bf16[128,1536]{1,0:T(8,128)(2,1)S(1)} %copy-done.5, f32[32,128]{1,0:T(8,128)S(1)} %get-tuple-element.31.sums_ref, bf16[768,512]{1,0:T(8,128)(2,1)S(1)} %bitcast.16, ...), custom_call_target="tpu_custom_call" | custom-call | flops 3170893824 | bytes 6291456 | tf_op jit(solution)/shard_map/backward/pallas_call | solution.py:219
  51.6 2.2 %collective-permute-start.3 = (bf16[768,512]{1,0:T(8,128)(2,1)S(1)}, bf16[768,512]{1,0:T(8,128)(2,1)S(1)}, u32[]{:S(2)}, u32[]{:S(2)}) collective-permute-start(bf16[768,512]{1,0:T(8,128)(2,1)S(1)} %get-tuple-element.35), channel_id=1, source_target_pairs={{0,1},{1,0},{2,3},{3,2},{4,5},{5,4},{6,7},{7,6},{8,9},{9,8},{10,11... | collective-permute-start | bytes 2359304 | tf_op jit(solution)/shard_map/ppermute | solution.py:386
  53.9 0.8 keep_half.1
  54.7 1.1 %collective-permute-done.3 = bf16[768,512]{1,0:T(8,128)(2,1)S(1)} collective-permute-done((bf16[768,512]{1,0:T(8,128)(2,1)S(1)}, bf16[768,512]{1,0:T(8,128)(2,1)S(1)}, u32[]{:S(2)}, u32[]{:S(2)}) %collective-permute-start.3) | collective-permute-done | bytes 786464 | tf_op jit(solution)/shard_map/ppermute | solution.py:386
  55.8 1.2 %add_convert_fusion = bf16[768,512]{1,0:T(8,128)(2,1)} fusion(f32[768,512]{1,0:T(8,128)S(1)} %keep_half.1, bf16[768,512]{1,0:T(8,128)(2,1)S(1)} %collective-permute-done.3), kind=kLoop, calls=%fused_computation | loop fusion | flops 1179648 | bytes 3145728 | tf_op jit(solution)/shard_map/convert_element_type | solution.py:389
  57.0 5.9 %all-to-all-start.1 = ((bf16[32,24,512]{2,1,0:T(8,128)(2,1)}), bf16[32,24,512]{2,1,0:T(8,128)(2,1)S(1)}, u32[]{:S(2)}, u32[]{:S(2)}) async-start(bf16[32,24,512]{2,1,0:T(8,128)(2,1)} %bitcast.20), calls=%async_computation.1 | async-start | bytes 1572864 | tf_op jit(solution)/shard_map/all_to_all | solution.py:390
  62.9 1.1 %copy-done.2 = bf16[768,512]{1,0:T(8,128)(2,1)S(1)} copy-done((bf16[768,512]{1,0:T(8,128)(2,1)S(1)}, bf16[768,512]{1,0:T(8,128)(2,1)}, u32[]{:S(2)}) %copy-start.2) | copy-done | bytes 786456
  64.0 2.5 %pool.1 = bf16[768,896]{1,0:T(8,128)(2,1)} custom-call(s32[1]{0:T(128)} %bitcast.core_ref, bf16[768,768]{1,0:T(8,128)(2,1)S(1)} %get-tuple-element.33.s_ref, bf16[768,512]{1,0:T(8,128)(2,1)S(1)} %bitcast.17, bf16[768,512]{1,0:T(8,128)(2,1)S(1)} %copy-done.2, f32[1,896]{1,0:T(1,128)S(1)} %get-tuple-element.36.bias_ref), custom_call_target="tpu_custom_call" | custom-call | flops 1056964608 | bytes 4194304 | tf_op jit(solution)/shard_map/pool/pallas_call | solution.py:259
  66.5 17.9 %all-to-all-done.1.in_ref = bf16[32,24,512]{2,1,0:T(8,128)(2,1)S(1)} async-done(((bf16[32,24,512]{2,1,0:T(8,128)(2,1)}), bf16[32,24,512]{2,1,0:T(8,128)(2,1)S(1)}, u32[]{:S(2)}, u32[]{:S(2)}) %all-to-all-start.1) | async-done | bytes 786464 | tf_op jit(solution)/shard_map/all_to_all | solution.py:390
  84.5 16.5 %all_to_all.15.in_ref = bf16[8,24,512]{2,1,0:T(8,128)(2,1)S(1)} all-to-all(bf16[8,24,512]{2,1,0:T(8,128)(2,1)S(1)} %add_up.2), channel_id=1, replica_groups={{0,2,4,6,8,10,12,14},{1,3,5,7,9,11,13,15},{16,18,20,22,24,26,28,30},{17..., dimensions={0} | all-to-all | bytes 393216 | tf_op jit(solution)/shard_map/all_to_all | solution.py:404
  101.0 4.9 %collective-permute-start.4 = (f32[24,512]{1,0:T(8,128)S(1)}, f32[24,512]{1,0:T(8,128)S(1)}, u32[]{:S(2)}, u32[]{:S(2)}) collective-permute-start(f32[24,512]{1,0:T(8,128)S(1)} %bitcast.18), channel_id=1, source_target_pairs={{0,1},{1,0},{2,3},{3,2},{4,5},{5,4},{6,7},{7,6},{8,9},{9,8},{10,11... | collective-permute-start | bytes 147464 | tf_op jit(solution)/shard_map/ppermute | solution.py:406
  105.9 0.9 collective-permute-done.4.across_ref
  106.8 0.7 unpack.1
  (16 shorter events, 0.2 us)
Async XLA Ops:
  0.6 33.1 %copy-start.3 = (s32[1,1536]{1,0:T(1,128)S(1)}, s32[1,1536]{1,0:T(1,128)}, u32[]{:S(2)}) copy-start(s32[1,1536]{1,0:T(1,128)} %bases_ref.1) | copy-start | bytes 18436
  0.6 33.1 %copy-start = (bf16[1,768,896]{2,1,0:T(8,128)(2,1)S(1)}, bf16[1,768,896]{2,1,0:T(8,128)(2,1)}, u32[]{:S(2)}) copy-start(bf16[1,768,896]{2,1,0:T(8,128)(2,1)} %param.13) | copy-start | bytes 4128772
  2.7 14.3 %copy-start.7 = (s32[1,128]{1,0:T(1,128)S(1)}, s32[1,128]{1,0:T(1,128)}, u32[]{:S(2)}) copy-start(s32[1,128]{1,0:T(1,128)} %get-tuple-element.26) | copy-start | bytes 1540
  2.7 17.1 %copy-start.6 = (s32[1,128]{1,0:T(1,128)S(1)}, s32[1,128]{1,0:T(1,128)}, u32[]{:S(2)}) copy-start(s32[1,128]{1,0:T(1,128)} %get-tuple-element.27) | copy-start | bytes 1540
  2.8 34.7 %all-to-all-start = ((bf16[32,24,512]{2,1,0:T(8,128)(2,1)}), bf16[32,24,512]{2,1,0:T(8,128)(2,1)S(1)}, u32[]{:S(2)}, u32[]{:S(2)}) async-start(bf16[32,24,512]{2,1,0:T(8,128)(2,1)} %get-tuple-element.25), calls=%async_computation | async-start | bytes 1572864 | tf_op jit(solution)/shard_map/all_to_all | solution.py:379
  17.1 7.5 %collective-permute-start = (s32[1,128]{1,0:T(1,128)S(1)}, s32[1,128]{1,0:T(1,128)S(1)}, u32[]{:S(2)}, u32[]{:S(2)}) collective-permute-start(s32[1,128]{1,0:T(1,128)S(1)} %copy-done.7), channel_id=1, source_target_pairs={{0,1},{1,0},{2,3},{3,2},{4,5},{5,4},{6,7},{7,6},{8,9},{9,8},{10,11... | collective-permute-start | bytes 1544 | tf_op jit(solution)/shard_map/ppermute | solution.py:377
  19.9 13.8 %collective-permute-start.1 = (s32[1,128]{1,0:T(1,128)S(1)}, s32[1,128]{1,0:T(1,128)S(1)}, u32[]{:S(2)}, u32[]{:S(2)}) collective-permute-start(s32[1,128]{1,0:T(1,128)S(1)} %copy-done.6), channel_id=1, source_target_pairs={{1,2},{2,1},{3,4},{4,3},{5,6},{6,5},{7,8},{8,7},{9,10},{10,9},{11,... | collective-permute-start | bytes 1544 | tf_op jit(solution)/shard_map/ppermute | solution.py:378
  35.3 0.8 copy-start.4
  37.4 6.6 %collective-permute-start.2 = (bf16[768,512]{1,0:T(8,128)(2,1)S(1)}, bf16[768,512]{1,0:T(8,128)(2,1)S(1)}, u32[]{:S(2)}, u32[]{:S(2)}) collective-permute-start(bf16[768,512]{1,0:T(8,128)(2,1)S(1)} %bitcast.15), channel_id=1, source_target_pairs={{0,1},{1,0},{2,3},{3,2},{4,5},{5,4},{6,7},{7,6},{8,9},{9,8},{10,11... | collective-permute-start | bytes 2359304 | tf_op jit(solution)/shard_map/ppermute | solution.py:382
  44.0 1.0 copy-start.5
  45.0 6.6 %copy-start.1 = (bf16[768,512]{1,0:T(8,128)(2,1)}, bf16[768,512]{1,0:T(8,128)(2,1)S(1)}, u32[]{:S(2)}) copy-start(bf16[768,512]{1,0:T(8,128)(2,1)S(1)} %collective-permute-done.2.other_ref) | copy-start | bytes 2359300
  51.6 4.2 %collective-permute-start.3 = (bf16[768,512]{1,0:T(8,128)(2,1)S(1)}, bf16[768,512]{1,0:T(8,128)(2,1)S(1)}, u32[]{:S(2)}, u32[]{:S(2)}) collective-permute-start(bf16[768,512]{1,0:T(8,128)(2,1)S(1)} %get-tuple-element.35), channel_id=1, source_target_pairs={{0,1},{1,0},{2,3},{3,2},{4,5},{5,4},{6,7},{7,6},{8,9},{9,8},{10,11... | collective-permute-start | bytes 2359304 | tf_op jit(solution)/shard_map/ppermute | solution.py:386
  57.0 27.4 %all-to-all-start.1 = ((bf16[32,24,512]{2,1,0:T(8,128)(2,1)}), bf16[32,24,512]{2,1,0:T(8,128)(2,1)S(1)}, u32[]{:S(2)}, u32[]{:S(2)}) async-start(bf16[32,24,512]{2,1,0:T(8,128)(2,1)} %bitcast.20), calls=%async_computation.1 | async-start | bytes 1572864 | tf_op jit(solution)/shard_map/all_to_all | solution.py:390
  62.9 1.1 %copy-start.2 = (bf16[768,512]{1,0:T(8,128)(2,1)S(1)}, bf16[768,512]{1,0:T(8,128)(2,1)}, u32[]{:S(2)}) copy-start(bf16[768,512]{1,0:T(8,128)(2,1)} %copy-done.1) | copy-start | bytes 2359300
  101.0 5.8 %collective-permute-start.4 = (f32[24,512]{1,0:T(8,128)S(1)}, f32[24,512]{1,0:T(8,128)S(1)}, u32[]{:S(2)}, u32[]{:S(2)}) collective-permute-start(f32[24,512]{1,0:T(8,128)S(1)} %bitcast.18), channel_id=1, source_target_pairs={{0,1},{1,0},{2,3},{3,2},{4,5},{5,4},{6,7},{7,6},{8,9},{9,8},{10,11... | collective-permute-start | bytes 147464 | tf_op jit(solution)/shard_map/ppermute | solution.py:406

commit v7 on v5

--- a/solution.py
+++ b/solution.py
@@ -68,8 +68,8 @@
 
 
 def step_kernel(dims, core_ref, feat_ref, sums_ref, own_ref, other_ref, cot_ref,
-                theirs_ref, s_ref, wide_ref, bias_ref,
-                w_ref, we_ref, emb_ref, ga_ref, ge_ref, gew_ref):
+                theirs_ref, s_ref, wide_ref, bias_ref, w_ref,
+                we_ref, emb_ref, ga_ref, ge_ref, gew_ref):
     kw, shards, d0, d1, rows, tile, chunk = dims
     half = w_ref.shape[1] // 2
     pair_tile = tile // 2
@@ -175,26 +175,20 @@
         right_half(s_ref, cot_ref, wide_ref, mine_ref)
 
 
-def pool_kernel(core_ref, s_ref, own_ref, other_ref, bias_ref, pooled_ref):
-    half = own_ref.shape[1]
-    edge = pooled_ref.shape[1] - half
-
-    def project(left_ref, right_ref):
-        pooled_ref[:, :half] = ((0.25 / GELU_K) * dot(s_ref[...], left_ref[...], (1, 0)) + bias_ref[:, :half]).astype(BF16)
-        pooled_ref[:, half:] = ((0.25 / GELU_K) * dot(s_ref[...], right_ref[:, :edge], (1, 0)) + bias_ref[:, half:]).astype(BF16)
-
-    @pl.when(core_ref[0] == 0)
-    def _():
-        project(own_ref, other_ref)
-
-    @pl.when(core_ref[0] != 0)
-    def _():
-        project(other_ref, own_ref)
+def pool_kernel(s_ref, w_ref, bias_ref, pooled_hbm, stage_ref, sems):
+    parts, step, d1 = stage_ref.shape
+    copies = [pltpu.make_async_copy(stage_ref.at[n], pooled_hbm.at[pl.ds(n * step, step), :], sems.at[n]) for n in range(parts)]
+    for n in range(parts):
+        mixed = dot(s_ref[n * step:(n + 1) * step, :], w_ref[:, :d1], (1, 0))
+        stage_ref[n] = ((0.25 / GELU_K) * mixed + bias_ref[...]).astype(BF16)
+        copies[n].start()
+    for copy in copies:
+        copy.wait()
 
 
 VMEM = pl.BlockSpec(memory_space=pltpu.VMEM)
 SMEM = pl.BlockSpec(memory_space=pltpu.SMEM)
-TILE, CHUNK = 512, 32
+TILE, CHUNK = 1536, 32
 
 
 def make_features(core, inner, bases, outer, cot, kw, shards):
@@ -223,11 +217,11 @@
             jax.ShapeDtypeStruct((pairs, d0), BF16),
             jax.ShapeDtypeStruct((d0, LANES), F32),
             jax.ShapeDtypeStruct((1, d1), F32),
+            jax.ShapeDtypeStruct((d0, 2 * half), BF16),
         ),
         in_specs=[SMEM] + [VMEM] * 5,
-        out_specs=(VMEM,) * 4,
+        out_specs=(VMEM,) * 5,
         scratch_shapes=[
-            pltpu.VMEM((d0, 2 * half), BF16),
             pltpu.VMEM((LANES, d0), BF16),
             pltpu.VMEM((rows, d0), BF16),
             pltpu.VMEM((pairs, d0), F32),
@@ -253,25 +247,28 @@
     )(core, s, cot, wide)
 
 
-def pool(core, s, own, other, bias):
+def pool(s, w, bias):
     pairs, d0 = s.shape
     d1 = bias.shape[1]
+    hbm = pl.BlockSpec(memory_space=pltpu.HBM)
+    parts = 3
     return pl.pallas_call(
         pool_kernel,
         out_shape=jax.ShapeDtypeStruct((pairs, d1), BF16),
-        in_specs=[SMEM] + [VMEM] * 4,
-        out_specs=VMEM,
+        in_specs=[VMEM] * 3,
+        out_specs=hbm,
+        scratch_shapes=[pltpu.VMEM((parts, pairs // parts, d1), BF16), pltpu.SemaphoreType.DMA((parts,))],
         compiler_params=pltpu.CompilerParams(vmem_limit_bytes=16 << 20),
         cost_estimate=pl.CostEstimate(flops=2 * pairs * d0 * d1, bytes_accessed=4 << 20, transcendentals=0),
         name="pool",
-    )(core, s, own, other, bias)
+    )(s, w, bias)
 
 
 def pack_kernel(core_ref, bases_hbm, embed_hbm, embed_bias_hbm, gain_hbm, proj_hbm, proj_bias_hbm,
-                out_ref, inner_ref, outer_ref,
-                bases_ref, embed_ref, embed_bias_ref, gain_ref, proj_ref, proj_bias_ref, rows_ref, block_ref, sems):
+                out_hbm, inner_ref, outer_ref,
+                bases_ref, embed_ref, embed_bias_ref, gain_ref, proj_ref, proj_bias_ref, rows_ref, stage_ref, sems, sent):
     kw, block, d1 = embed_ref.shape[0], proj_ref.shape[0], proj_ref.shape[1]
-    copies, _, half = out_ref.shape
+    copies, _, half = out_hbm.shape
     taps, per = kw * 4, proj_bias_ref.shape[1]
     fetched = [
         pltpu.make_async_copy(source, target, sems.at[n])
@@ -284,29 +281,33 @@
     rows_ref[...] = jnp.zeros_like(rows_ref)
     for copy in fetched:
         copy.wait()
+    even = core_ref[0] == 0
+    edge = d1 - half
+
+    @pl.when(even)
+    def _():
+        stage_ref[...] = proj_ref[:, :half]
+
+    @pl.when(jnp.logical_not(even))
+    def _():
+        for k in range(kw):
+            rows_ref[4 * k:4 * k + 4, :block] = embed_ref[k].astype(F32)
+        rows_ref[taps:taps + 1, :block] = embed_bias_ref[...].astype(F32)
+        rows_ref[taps + 1:taps + 2, :block] = gain_ref[...].astype(F32)
+        rows_ref[...] = rows_ref[...].T
+        rows_ref[:1, 64:64 + per] = proj_bias_ref[...].astype(F32)
+        stage_ref[:, :edge] = proj_ref[:, half:]
+        stage_ref[:, edge:] = rows_ref[:block, :].astype(BF16)
+
+    sends = [pltpu.make_async_copy(stage_ref, out_hbm.at[i], sent.at[i]) for i in range(copies)]
+    for send in sends:
+        send.start()
     first = bases_ref[:, :LANES] + 1
     last = bases_ref[:, bases_ref.shape[1] - LANES:] + 1
-    even = core_ref[0] == 0
     inner_ref[...] = jnp.where(even, last, first)
     outer_ref[...] = jnp.where(even, first, last)
-    for k in range(kw):
-        rows_ref[4 * k:4 * k + 4, :block] = embed_ref[k].astype(F32)
-    rows_ref[taps:taps + 1, :block] = embed_bias_ref[...].astype(F32)
-    rows_ref[taps + 1:taps + 2, :block] = gain_ref[...].astype(F32)
-    block_ref[...] = rows_ref[...].T[:block]
-    block_ref[:1, 64:64 + per] = proj_bias_ref[...].astype(F32)
-    edge = d1 - half
-
-    @pl.when(even)
-    def _():
-        for i in range(copies):
-            out_ref[i] = proj_ref[:, :half]
-
-    @pl.when(jnp.logical_not(even))
-    def _():
-        for i in range(copies):
-            out_ref[i, :, :edge] = proj_ref[:, half:]
-            out_ref[i, :, edge:] = block_ref[...].astype(BF16)
+    for send in sends:
+        send.wait()
 
 
 def sum_kernel(scale, in_ref, out_ref):
@@ -368,9 +369,10 @@
             jax.ShapeDtypeStruct((1, LANES), jnp.int32),
         ),
         in_specs=[SMEM] + [hbm] * 6,
-        out_specs=(VMEM,) * 3,
+        out_specs=(hbm, VMEM, VMEM),
         scratch_shapes=[pltpu.VMEM(x.shape, x.dtype) for x in gathered] + [
-            pltpu.VMEM((LANES, LANES), F32), pltpu.VMEM((block, LANES), F32), pltpu.SemaphoreType.DMA((6,))],
+            pltpu.VMEM((LANES, LANES), F32), pltpu.VMEM((block, half), BF16),
+            pltpu.SemaphoreType.DMA((6,)), pltpu.SemaphoreType.DMA((shards,))],
         compiler_params=pltpu.CompilerParams(vmem_limit_bytes=60 << 20),
         name="pack",
     )(core, *gathered)
@@ -382,10 +384,10 @@
     other = lax.ppermute(own, "seq", swap)
 
     cot = cotangent[0]
-    theirs, s, wide, bias = backward(core, feat, sums, own, other, cot, kw, shards)
+    theirs, s, wide, bias, w = backward(core, feat, sums, own, other, cot, kw, shards)
     came = lax.ppermute(theirs, "seq", swap)
     mine = keep_half(core, s, cot, wide, half)
-    pooled = pool(core, s, own, other, bias)
+    pooled = pool(s, w, bias)
     summed = (mine + came.astype(F32)).astype(BF16).reshape(shards, block, half)
     parts = lax.all_to_all(summed, "dp", 0, 0, tiled=True)
 

time: 107 us -> 107 us (level)
  blocking collectives: 41.9 us -> 43.3 us
  starting transfers between devices: 34.7 us -> 33.5 us
    all_to_all x1, blocking collectives: 16.1 us -> 17.4 us  [local(): lax.all_to_all(add_up(parts, 1.0, members // 2, BF16), 'seq', 0, 0, axis_...]
where the time goes in v7:
time: 107 us
  blocking collectives  43.3 us (40%)
  starting transfers between devices  33.5 us (31%)
  Pallas kernels  14.8 us (14%)
  waiting for transfers between devices  14 us (13%)
    all_to_all x1, blocking collectives, local(): parts = lax.all_to_all(summed, 'dp', 0, 0, tiled=True)  25.9 us
    all_to_all x1, blocking collectives, local(): lax.all_to_all(add_up(parts, 1.0, members // 2, BF16), 'seq', 0, 0, axis_...  17.4 us
    all_to_all x1, starting transfers between devices, local(): lax.all_to_all(piece, 'dp', 0, 0, tiled=True).reshape(shards * block, half)  14.3 us
    ppermute x1, waiting for transfers between devices, local(): outer = lax.ppermute(outer, 'seq', facing)  9.16 us
    pallas_call x1, Pallas kernels, backward(): pl.pallas_call(functools.partial(step_kernel, dims), out_shape=(jax.Shape...  6.21 us
    ppermute x1, starting transfers between devices, local(): across = lax.ppermute(total, 'seq', swap)  4.94 us
    ppermute x1, starting transfers between devices, local(): outer = lax.ppermute(outer, 'seq', facing)  4.65 us
    ppermute x1, starting transfers between devices, local(): other = lax.ppermute(own, 'seq', swap)  4.62 us
  transfers between devices with their start and end apart: 6, of which 4 were waited for; matrix products, arithmetic and copies ran while one was open for 0% of the time, Pallas kernels for 5%

profile of v7, /device:TPU:1, one launch (start us, length us, event | category | flops | bytes accessed | tf_op | source)
XLA Modules:
  0.0 106.7 jit_solution(2015705820923859240)
XLA Ops:
  0.7 2.8 %pack.1 = (bf16[32,24,512]{2,1,0:T(8,128)(2,1)}, s32[1,128]{1,0:T(1,128)}, s32[1,128]{1,0:T(1,128)}) custom-call(s32[1]{0:T(128)} %bitcast.core_ref, s32[1,1536]{1,0:T(1,128)} %bases_ref.1, bf16[15,4,24]{2,1,0:T(4,128)(2,1)} %embed_hbm.1, bf16[1,24]{1,0:T(2,128)(2,1)} %bitcast.21, bf16[1,24]{1,0:T(2,128)(2,1)} %bitcast.22, bf16[24,896]{1,0:T(8,128)(2,1)} %proj_hbm.1, ...), custom_call_target="tpu_custom_call" | custom-call | tf_op jit(solution)/shard_map/pack/pallas_call | solution.py:364
  3.4 0.0 copy-start.3
  3.5 0.0 copy-start.2
  3.5 14.3 %all-to-all-start = ((bf16[32,24,512]{2,1,0:T(8,128)(2,1)}), bf16[32,24,512]{2,1,0:T(8,128)(2,1)S(1)}, u32[]{:S(2)}, u32[]{:S(2)}) async-start(bf16[32,24,512]{2,1,0:T(8,128)(2,1)} %get-tuple-element.24), calls=%async_computation | async-start | bytes 1572864 | tf_op jit(solution)/shard_map/all_to_all | solution.py:381
  17.8 2.7 %collective-permute-start = (s32[1,128]{1,0:T(1,128)S(1)}, s32[1,128]{1,0:T(1,128)S(1)}, u32[]{:S(2)}, u32[]{:S(2)}) collective-permute-start(s32[1,128]{1,0:T(1,128)S(1)} %copy-done.3), channel_id=1, source_target_pairs={{0,1},{1,0},{2,3},{3,2},{4,5},{5,4},{6,7},{7,6},{8,9},{9,8},{10,11... | collective-permute-start | bytes 1544 | tf_op jit(solution)/shard_map/ppermute | solution.py:379
  20.6 4.7 %collective-permute-start.1 = (s32[1,128]{1,0:T(1,128)S(1)}, s32[1,128]{1,0:T(1,128)S(1)}, u32[]{:S(2)}, u32[]{:S(2)}) collective-permute-start(s32[1,128]{1,0:T(1,128)S(1)} %copy-done.2), channel_id=1, source_target_pairs={{1,2},{2,1},{3,4},{4,3},{5,6},{6,5},{7,8},{8,7},{9,10},{10,9},{11,... | collective-permute-start | bytes 1544 | tf_op jit(solution)/shard_map/ppermute | solution.py:380
  25.2 0.0 collective-permute-done.inner_ref
  25.2 9.2 %collective-permute-done.1.outer_ref = s32[1,128]{1,0:T(1,128)S(1)} collective-permute-done((s32[1,128]{1,0:T(1,128)S(1)}, s32[1,128]{1,0:T(1,128)S(1)}, u32[]{:S(2)}, u32[]{:S(2)}) %collective-permute-start.1) | collective-permute-done | bytes 544 | tf_op jit(solution)/shard_map/ppermute | solution.py:380
  34.4 1.9 %features.1 = (bf16[128,1536]{1,0:T(8,128)(2,1)S(1)}, f32[32,128]{1,0:T(8,128)S(1)}) custom-call(s32[1]{0:T(128)} %bitcast.core_ref, s32[1,128]{1,0:T(1,128)S(1)} %collective-permute-done.inner_ref, s32[1,1536]{1,0:T(1,128)S(1)} %copy-done.1, s32[1,128]{1,0:T(1,128)S(1)} %collective-permute-done.1.outer_ref, bf16[768,896]{1,0:T(8,128)(2,1)S(1)} %bitcast.12), custom_call_target="tpu_custom_call" | custom-call | flops 603979776 | bytes 2097152 | tf_op jit(solution)/shard_map/features/pallas_call | solution.py:196
  36.3 1.9 %all-to-all-done = bf16[32,24,512]{2,1,0:T(8,128)(2,1)S(1)} async-done(((bf16[32,24,512]{2,1,0:T(8,128)(2,1)}), bf16[32,24,512]{2,1,0:T(8,128)(2,1)S(1)}, u32[]{:S(2)}, u32[]{:S(2)}) %all-to-all-start) | async-done | bytes 786464 | tf_op jit(solution)/shard_map/all_to_all | solution.py:381
  38.2 4.6 %collective-permute-start.2 = (bf16[768,512]{1,0:T(8,128)(2,1)S(1)}, bf16[768,512]{1,0:T(8,128)(2,1)S(1)}, u32[]{:S(2)}, u32[]{:S(2)}) collective-permute-start(bf16[768,512]{1,0:T(8,128)(2,1)S(1)} %bitcast.15), channel_id=1, source_target_pairs={{0,1},{1,0},{2,3},{3,2},{4,5},{5,4},{6,7},{7,6},{8,9},{9,8},{10,11... | collective-permute-start | bytes 2359304 | tf_op jit(solution)/shard_map/ppermute | solution.py:384
  42.8 1.9 %collective-permute-done.2.other_ref = bf16[768,512]{1,0:T(8,128)(2,1)S(1)} collective-permute-done((bf16[768,512]{1,0:T(8,128)(2,1)S(1)}, bf16[768,512]{1,0:T(8,128)(2,1)S(1)}, u32[]{:S(2)}, u32[]{:S(2)}) %collective-permute-start.2) | collective-permute-done | bytes 786464 | tf_op jit(solution)/shard_map/ppermute | solution.py:384
  44.7 6.2 %backward.1 = (bf16[768,512]{1,0:T(8,128)(2,1)S(1)}, bf16[768,768]{1,0:T(8,128)(2,1)S(1)}, f32[768,128]{1,0:T(8,128)S(1)}, f32[1,896]{1,0:T(1,128)S(1)}, bf16[768,1024]{1,0:T(8,128)(2,1)S(1)}) custom-call(s32[1]{0:T(128)} %bitcast.core_ref, bf16[128,1536]{1,0:T(8,128)(2,1)S(1)} %get-tuple-element.29.feat_ref, f32[32,128]{1,0:T(8,128)S(1)} %get-tuple-element.30.sums_ref, ...), custom_call_target="tpu_custom_call" | custom-call | flops 3170893824 | bytes 6291456 | tf_op jit(solution)/shard_map/backward/pallas_call | solution.py:213
  50.9 2.2 %collective-permute-start.3 = (bf16[768,512]{1,0:T(8,128)(2,1)S(1)}, bf16[768,512]{1,0:T(8,128)(2,1)S(1)}, u32[]{:S(2)}, u32[]{:S(2)}) collective-permute-start(bf16[768,512]{1,0:T(8,128)(2,1)S(1)} %get-tuple-element.36), channel_id=1, source_target_pairs={{0,1},{1,0},{2,3},{3,2},{4,5},{5,4},{6,7},{7,6},{8,9},{9,8},{10,11... | collective-permute-start | bytes 2359304 | tf_op jit(solution)/shard_map/ppermute | solution.py:388
  53.1 0.8 keep_half.1
  54.0 1.1 %collective-permute-done.3 = bf16[768,512]{1,0:T(8,128)(2,1)S(1)} collective-permute-done((bf16[768,512]{1,0:T(8,128)(2,1)S(1)}, bf16[768,512]{1,0:T(8,128)(2,1)S(1)}, u32[]{:S(2)}, u32[]{:S(2)}) %collective-permute-start.3) | collective-permute-done | bytes 786464 | tf_op jit(solution)/shard_map/ppermute | solution.py:388
  55.1 0.3 add_convert_fusion
  55.4 25.9 %all_to_all.15.in_ref = bf16[32,24,512]{2,1,0:T(8,128)(2,1)S(1)} all-to-all(bf16[32,24,512]{2,1,0:T(8,128)(2,1)S(1)} %bitcast.19), channel_id=1, replica_groups=mesh['dp'=32,'seq'=16] {'dp'}, dimensions={0} | all-to-all | bytes 1572864 | tf_op jit(solution)/shard_map/all_to_all | solution.py:392
  81.2 0.1 add_up.2
  81.3 17.4 %all_to_all.16.in_ref = bf16[8,24,512]{2,1,0:T(8,128)(2,1)S(1)} all-to-all(bf16[8,24,512]{2,1,0:T(8,128)(2,1)S(1)} %add_up.2), channel_id=1, replica_groups={{0,2,4,6,8,10,12,14},{1,3,5,7,9,11,13,15},{16,18,20,22,24,26,28,30},{17..., dimensions={0} | all-to-all | bytes 393216 | tf_op jit(solution)/shard_map/all_to_all | solution.py:405
  98.8 4.9 %collective-permute-start.4 = (f32[24,512]{1,0:T(8,128)S(1)}, f32[24,512]{1,0:T(8,128)S(1)}, u32[]{:S(2)}, u32[]{:S(2)}) collective-permute-start(f32[24,512]{1,0:T(8,128)S(1)} %bitcast.17), channel_id=1, source_target_pairs={{0,1},{1,0},{2,3},{3,2},{4,5},{5,4},{6,7},{7,6},{8,9},{9,8},{10,11... | collective-permute-start | bytes 147464 | tf_op jit(solution)/shard_map/ppermute | solution.py:407
  103.7 2.2 %pool.1 = bf16[768,896]{1,0:T(8,128)(2,1)} custom-call(bf16[768,768]{1,0:T(8,128)(2,1)S(1)} %get-tuple-element.32.s_ref, bf16[768,1024]{1,0:T(8,128)(2,1)S(1)} %get-tuple-element.33.w_ref, f32[1,896]{1,0:T(1,128)S(1)} %get-tuple-element.34.bias_ref), custom_call_target="tpu_custom_call" | custom-call | flops 1056964608 | bytes 4194304 | tf_op jit(solution)/shard_map/pool/pallas_call | solution.py:255
  106.0 0.0 collective-permute-done.4.across_ref
  106.0 0.8 unpack.1
  (7 shorter events, 0.0 us)
Async XLA Ops:
  0.6 33.8 %copy-start.1 = (s32[1,1536]{1,0:T(1,128)S(1)}, s32[1,1536]{1,0:T(1,128)}, u32[]{:S(2)}) copy-start(s32[1,1536]{1,0:T(1,128)} %bases_ref.1) | copy-start | bytes 18436
  0.6 33.8 %copy-start = (bf16[1,768,896]{2,1,0:T(8,128)(2,1)S(1)}, bf16[1,768,896]{2,1,0:T(8,128)(2,1)}, u32[]{:S(2)}) copy-start(bf16[1,768,896]{2,1,0:T(8,128)(2,1)} %param.13) | copy-start | bytes 4128772
  3.4 14.3 %copy-start.3 = (s32[1,128]{1,0:T(1,128)S(1)}, s32[1,128]{1,0:T(1,128)}, u32[]{:S(2)}) copy-start(s32[1,128]{1,0:T(1,128)} %get-tuple-element.25) | copy-start | bytes 1540
  3.5 17.1 %copy-start.2 = (s32[1,128]{1,0:T(1,128)S(1)}, s32[1,128]{1,0:T(1,128)}, u32[]{:S(2)}) copy-start(s32[1,128]{1,0:T(1,128)} %get-tuple-element.26) | copy-start | bytes 1540
  3.5 34.7 %all-to-all-start = ((bf16[32,24,512]{2,1,0:T(8,128)(2,1)}), bf16[32,24,512]{2,1,0:T(8,128)(2,1)S(1)}, u32[]{:S(2)}, u32[]{:S(2)}) async-start(bf16[32,24,512]{2,1,0:T(8,128)(2,1)} %get-tuple-element.24), calls=%async_computation | async-start | bytes 1572864 | tf_op jit(solution)/shard_map/all_to_all | solution.py:381
  17.8 7.4 %collective-permute-start = (s32[1,128]{1,0:T(1,128)S(1)}, s32[1,128]{1,0:T(1,128)S(1)}, u32[]{:S(2)}, u32[]{:S(2)}) collective-permute-start(s32[1,128]{1,0:T(1,128)S(1)} %copy-done.3), channel_id=1, source_target_pairs={{0,1},{1,0},{2,3},{3,2},{4,5},{5,4},{6,7},{7,6},{8,9},{9,8},{10,11... | collective-permute-start | bytes 1544 | tf_op jit(solution)/shard_map/ppermute | solution.py:379
  20.6 13.8 %collective-permute-start.1 = (s32[1,128]{1,0:T(1,128)S(1)}, s32[1,128]{1,0:T(1,128)S(1)}, u32[]{:S(2)}, u32[]{:S(2)}) collective-permute-start(s32[1,128]{1,0:T(1,128)S(1)} %copy-done.2), channel_id=1, source_target_pairs={{1,2},{2,1},{3,4},{4,3},{5,6},{6,5},{7,8},{8,7},{9,10},{10,9},{11,... | collective-permute-start | bytes 1544 | tf_op jit(solution)/shard_map/ppermute | solution.py:380
  38.2 6.5 %collective-permute-start.2 = (bf16[768,512]{1,0:T(8,128)(2,1)S(1)}, bf16[768,512]{1,0:T(8,128)(2,1)S(1)}, u32[]{:S(2)}, u32[]{:S(2)}) collective-permute-start(bf16[768,512]{1,0:T(8,128)(2,1)S(1)} %bitcast.15), channel_id=1, source_target_pairs={{0,1},{1,0},{2,3},{3,2},{4,5},{5,4},{6,7},{7,6},{8,9},{9,8},{10,11... | collective-permute-start | bytes 2359304 | tf_op jit(solution)/shard_map/ppermute | solution.py:384
  50.9 4.2 %collective-permute-start.3 = (bf16[768,512]{1,0:T(8,128)(2,1)S(1)}, bf16[768,512]{1,0:T(8,128)(2,1)S(1)}, u32[]{:S(2)}, u32[]{:S(2)}) collective-permute-start(bf16[768,512]{1,0:T(8,128)(2,1)S(1)} %get-tuple-element.36), channel_id=1, source_target_pairs={{0,1},{1,0},{2,3},{3,2},{4,5},{5,4},{6,7},{7,6},{8,9},{9,8},{10,11... | collective-permute-start | bytes 2359304 | tf_op jit(solution)/shard_map/ppermute | solution.py:388
  98.8 7.2 %collective-permute-start.4 = (f32[24,512]{1,0:T(8,128)S(1)}, f32[24,512]{1,0:T(8,128)S(1)}, u32[]{:S(2)}, u32[]{:S(2)}) collective-permute-start(f32[24,512]{1,0:T(8,128)S(1)} %bitcast.17), channel_id=1, source_target_pairs={{0,1},{1,0},{2,3},{3,2},{4,5},{5,4},{6,7},{7,6},{8,9},{9,8},{10,11... | collective-permute-start | bytes 147464 | tf_op jit(solution)/shard_map/ppermute | solution.py:407

commit v8 on v7

--- a/solution.py
+++ b/solution.py
@@ -265,10 +265,10 @@
 
 
 def pack_kernel(core_ref, bases_hbm, embed_hbm, embed_bias_hbm, gain_hbm, proj_hbm, proj_bias_hbm,
-                out_hbm, inner_ref, outer_ref,
-                bases_ref, embed_ref, embed_bias_ref, gain_ref, proj_ref, proj_bias_ref, rows_ref, stage_ref, sems, sent):
+                out_ref, inner_ref, outer_ref,
+                bases_ref, embed_ref, embed_bias_ref, gain_ref, proj_ref, proj_bias_ref, rows_ref, block_ref, sems):
     kw, block, d1 = embed_ref.shape[0], proj_ref.shape[0], proj_ref.shape[1]
-    copies, _, half = out_hbm.shape
+    copies, _, half = out_ref.shape
     taps, per = kw * 4, proj_bias_ref.shape[1]
     fetched = [
         pltpu.make_async_copy(source, target, sems.at[n])
@@ -281,33 +281,29 @@
     rows_ref[...] = jnp.zeros_like(rows_ref)
     for copy in fetched:
         copy.wait()
-    even = core_ref[0] == 0
-    edge = d1 - half
-
-    @pl.when(even)
-    def _():
-        stage_ref[...] = proj_ref[:, :half]
-
-    @pl.when(jnp.logical_not(even))
-    def _():
-        for k in range(kw):
-            rows_ref[4 * k:4 * k + 4, :block] = embed_ref[k].astype(F32)
-        rows_ref[taps:taps + 1, :block] = embed_bias_ref[...].astype(F32)
-        rows_ref[taps + 1:taps + 2, :block] = gain_ref[...].astype(F32)
-        rows_ref[...] = rows_ref[...].T
-        rows_ref[:1, 64:64 + per] = proj_bias_ref[...].astype(F32)
-        stage_ref[:, :edge] = proj_ref[:, half:]
-        stage_ref[:, edge:] = rows_ref[:block, :].astype(BF16)
-
-    sends = [pltpu.make_async_copy(stage_ref, out_hbm.at[i], sent.at[i]) for i in range(copies)]
-    for send in sends:
-        send.start()
     first = bases_ref[:, :LANES] + 1
     last = bases_ref[:, bases_ref.shape[1] - LANES:] + 1
+    even = core_ref[0] == 0
     inner_ref[...] = jnp.where(even, last, first)
     outer_ref[...] = jnp.where(even, first, last)
-    for send in sends:
-        send.wait()
+    for k in range(kw):
+        rows_ref[4 * k:4 * k + 4, :block] = embed_ref[k].astype(F32)
+    rows_ref[taps:taps + 1, :block] = embed_bias_ref[...].astype(F32)
+    rows_ref[taps + 1:taps + 2, :block] = gain_ref[...].astype(F32)
+    block_ref[...] = rows_ref[...].T[:block]
+    block_ref[:1, 64:64 + per] = proj_bias_ref[...].astype(F32)
+    edge = d1 - half
+
+    @pl.when(even)
+    def _():
+        for i in range(copies):
+            out_ref[i] = proj_ref[:, :half]
+
+    @pl.when(jnp.logical_not(even))
+    def _():
+        for i in range(copies):
+            out_ref[i, :, :edge] = proj_ref[:, half:]
+            out_ref[i, :, edge:] = block_ref[...].astype(BF16)
 
 
 def sum_kernel(scale, in_ref, out_ref):
@@ -369,10 +365,9 @@
             jax.ShapeDtypeStruct((1, LANES), jnp.int32),
         ),
         in_specs=[SMEM] + [hbm] * 6,
-        out_specs=(hbm, VMEM, VMEM),
+        out_specs=(VMEM,) * 3,
         scratch_shapes=[pltpu.VMEM(x.shape, x.dtype) for x in gathered] + [
-            pltpu.VMEM((LANES, LANES), F32), pltpu.VMEM((block, half), BF16),
-            pltpu.SemaphoreType.DMA((6,)), pltpu.SemaphoreType.DMA((shards,))],
+            pltpu.VMEM((LANES, LANES), F32), pltpu.VMEM((block, LANES), F32), pltpu.SemaphoreType.DMA((6,))],
         compiler_params=pltpu.CompilerParams(vmem_limit_bytes=60 << 20),
         name="pack",
     )(core, *gathered)

time: 107 us -> 107 us (level)
  no operation moved by 1% of the time
where the time goes in v8:
time: 107 us; the launch traced here: 106 us
  blocking collectives  43.2 us (40%)
  starting transfers between devices  33.6 us (31%)
  Pallas kernels  14.1 us (13%)
  waiting for transfers between devices  14 us (13%)
    all_to_all x1, blocking collectives, local(): parts = lax.all_to_all(summed, 'dp', 0, 0, tiled=True)  25.8 us
    all_to_all x1, blocking collectives, local(): lax.all_to_all(add_up(parts, 1.0, members // 2, BF16), 'seq', 0, 0, axis_...  17.4 us
    all_to_all x1, starting transfers between devices, local(): lax.all_to_all(piece, 'dp', 0, 0, tiled=True).reshape(shards * block, half)  14.3 us
    ppermute x1, waiting for transfers between devices, local(): outer = lax.ppermute(outer, 'seq', facing)  9.17 us
    pallas_call x1, Pallas kernels, backward(): pl.pallas_call(functools.partial(step_kernel, dims), out_shape=(jax.Shape...  6.21 us
    ppermute x1, starting transfers between devices, local(): across = lax.ppermute(total, 'seq', swap)  4.94 us
    ppermute x1, starting transfers between devices, local(): other = lax.ppermute(own, 'seq', swap)  4.72 us
    ppermute x1, starting transfers between devices, local(): outer = lax.ppermute(outer, 'seq', facing)  4.65 us
  transfers between devices with their start and end apart: 6, of which 4 were waited for; matrix products, arithmetic and copies ran while one was open for 0% of the time, Pallas kernels for 5%

profile of v8, /device:TPU:1, one launch (start us, length us, event | category | flops | bytes accessed | tf_op | source)
XLA Modules:
  0.0 106.0 jit_solution(9332478260306852043)
XLA Ops:
  0.7 2.1 %pack.1 = (bf16[32,24,512]{2,1,0:T(8,128)(2,1)}, s32[1,128]{1,0:T(1,128)}, s32[1,128]{1,0:T(1,128)}) custom-call(s32[1]{0:T(128)} %bitcast.core_ref, s32[1,1536]{1,0:T(1,128)} %bases_ref.1, bf16[15,4,24]{2,1,0:T(4,128)(2,1)} %embed_hbm.1, bf16[1,24]{1,0:T(2,128)(2,1)} %bitcast.21, bf16[1,24]{1,0:T(2,128)(2,1)} %bitcast.22, bf16[24,896]{1,0:T(8,128)(2,1)} %proj_hbm.1, ...), custom_call_target="tpu_custom_call" | custom-call | tf_op jit(solution)/shard_map/pack/pallas_call | solution.py:360
  2.7 0.0 copy-start.3
  2.7 0.0 copy-start.2
  2.8 14.3 %all-to-all-start = ((bf16[32,24,512]{2,1,0:T(8,128)(2,1)}), bf16[32,24,512]{2,1,0:T(8,128)(2,1)S(1)}, u32[]{:S(2)}, u32[]{:S(2)}) async-start(bf16[32,24,512]{2,1,0:T(8,128)(2,1)} %get-tuple-element.24), calls=%async_computation | async-start | bytes 1572864 | tf_op jit(solution)/shard_map/all_to_all | solution.py:376
  17.1 2.8 %collective-permute-start = (s32[1,128]{1,0:T(1,128)S(1)}, s32[1,128]{1,0:T(1,128)S(1)}, u32[]{:S(2)}, u32[]{:S(2)}) collective-permute-start(s32[1,128]{1,0:T(1,128)S(1)} %copy-done.3), channel_id=1, source_target_pairs={{0,1},{1,0},{2,3},{3,2},{4,5},{5,4},{6,7},{7,6},{8,9},{9,8},{10,11... | collective-permute-start | bytes 1544 | tf_op jit(solution)/shard_map/ppermute | solution.py:374
  19.9 4.7 %collective-permute-start.1 = (s32[1,128]{1,0:T(1,128)S(1)}, s32[1,128]{1,0:T(1,128)S(1)}, u32[]{:S(2)}, u32[]{:S(2)}) collective-permute-start(s32[1,128]{1,0:T(1,128)S(1)} %copy-done.2), channel_id=1, source_target_pairs={{1,2},{2,1},{3,4},{4,3},{5,6},{6,5},{7,8},{8,7},{9,10},{10,9},{11,... | collective-permute-start | bytes 1544 | tf_op jit(solution)/shard_map/ppermute | solution.py:375
  24.5 0.0 collective-permute-done.inner_ref
  24.6 9.2 %collective-permute-done.1.outer_ref = s32[1,128]{1,0:T(1,128)S(1)} collective-permute-done((s32[1,128]{1,0:T(1,128)S(1)}, s32[1,128]{1,0:T(1,128)S(1)}, u32[]{:S(2)}, u32[]{:S(2)}) %collective-permute-start.1) | collective-permute-done | bytes 544 | tf_op jit(solution)/shard_map/ppermute | solution.py:375
  33.7 1.9 %features.1 = (bf16[128,1536]{1,0:T(8,128)(2,1)S(1)}, f32[32,128]{1,0:T(8,128)S(1)}) custom-call(s32[1]{0:T(128)} %bitcast.core_ref, s32[1,128]{1,0:T(1,128)S(1)} %collective-permute-done.inner_ref, s32[1,1536]{1,0:T(1,128)S(1)} %copy-done.1, s32[1,128]{1,0:T(1,128)S(1)} %collective-permute-done.1.outer_ref, bf16[768,896]{1,0:T(8,128)(2,1)S(1)} %bitcast.12), custom_call_target="tpu_custom_call" | custom-call | flops 603979776 | bytes 2097152 | tf_op jit(solution)/shard_map/features/pallas_call | solution.py:196
  35.6 1.8 %all-to-all-done = bf16[32,24,512]{2,1,0:T(8,128)(2,1)S(1)} async-done(((bf16[32,24,512]{2,1,0:T(8,128)(2,1)}), bf16[32,24,512]{2,1,0:T(8,128)(2,1)S(1)}, u32[]{:S(2)}, u32[]{:S(2)}) %all-to-all-start) | async-done | bytes 786464 | tf_op jit(solution)/shard_map/all_to_all | solution.py:376
  37.4 4.7 %collective-permute-start.2 = (bf16[768,512]{1,0:T(8,128)(2,1)S(1)}, bf16[768,512]{1,0:T(8,128)(2,1)S(1)}, u32[]{:S(2)}, u32[]{:S(2)}) collective-permute-start(bf16[768,512]{1,0:T(8,128)(2,1)S(1)} %bitcast.15), channel_id=1, source_target_pairs={{0,1},{1,0},{2,3},{3,2},{4,5},{5,4},{6,7},{7,6},{8,9},{9,8},{10,11... | collective-permute-start | bytes 2359304 | tf_op jit(solution)/shard_map/ppermute | solution.py:379
  42.1 1.9 %collective-permute-done.2.other_ref = bf16[768,512]{1,0:T(8,128)(2,1)S(1)} collective-permute-done((bf16[768,512]{1,0:T(8,128)(2,1)S(1)}, bf16[768,512]{1,0:T(8,128)(2,1)S(1)}, u32[]{:S(2)}, u32[]{:S(2)}) %collective-permute-start.2) | collective-permute-done | bytes 786464 | tf_op jit(solution)/shard_map/ppermute | solution.py:379
  44.0 6.2 %backward.1 = (bf16[768,512]{1,0:T(8,128)(2,1)S(1)}, bf16[768,768]{1,0:T(8,128)(2,1)S(1)}, f32[768,128]{1,0:T(8,128)S(1)}, f32[1,896]{1,0:T(1,128)S(1)}, bf16[768,1024]{1,0:T(8,128)(2,1)S(1)}) custom-call(s32[1]{0:T(128)} %bitcast.core_ref, bf16[128,1536]{1,0:T(8,128)(2,1)S(1)} %get-tuple-element.29.feat_ref, f32[32,128]{1,0:T(8,128)S(1)} %get-tuple-element.30.sums_ref, ...), custom_call_target="tpu_custom_call" | custom-call | flops 3170893824 | bytes 6291456 | tf_op jit(solution)/shard_map/backward/pallas_call | solution.py:213
  50.2 2.2 %collective-permute-start.3 = (bf16[768,512]{1,0:T(8,128)(2,1)S(1)}, bf16[768,512]{1,0:T(8,128)(2,1)S(1)}, u32[]{:S(2)}, u32[]{:S(2)}) collective-permute-start(bf16[768,512]{1,0:T(8,128)(2,1)S(1)} %get-tuple-element.36), channel_id=1, source_target_pairs={{0,1},{1,0},{2,3},{3,2},{4,5},{5,4},{6,7},{7,6},{8,9},{9,8},{10,11... | collective-permute-start | bytes 2359304 | tf_op jit(solution)/shard_map/ppermute | solution.py:383
  52.5 0.8 keep_half.1
  53.3 1.1 %collective-permute-done.3 = bf16[768,512]{1,0:T(8,128)(2,1)S(1)} collective-permute-done((bf16[768,512]{1,0:T(8,128)(2,1)S(1)}, bf16[768,512]{1,0:T(8,128)(2,1)S(1)}, u32[]{:S(2)}, u32[]{:S(2)}) %collective-permute-start.3) | collective-permute-done | bytes 786464 | tf_op jit(solution)/shard_map/ppermute | solution.py:383
  54.4 0.3 add_convert_fusion
  54.7 25.8 %all_to_all.15.in_ref = bf16[32,24,512]{2,1,0:T(8,128)(2,1)S(1)} all-to-all(bf16[32,24,512]{2,1,0:T(8,128)(2,1)S(1)} %bitcast.19), channel_id=1, replica_groups=mesh['dp'=32,'seq'=16] {'dp'}, dimensions={0} | all-to-all | bytes 1572864 | tf_op jit(solution)/shard_map/all_to_all | solution.py:387
  80.5 0.1 add_up.2
  80.6 17.4 %all_to_all.16.in_ref = bf16[8,24,512]{2,1,0:T(8,128)(2,1)S(1)} all-to-all(bf16[8,24,512]{2,1,0:T(8,128)(2,1)S(1)} %add_up.2), channel_id=1, replica_groups={{0,2,4,6,8,10,12,14},{1,3,5,7,9,11,13,15},{16,18,20,22,24,26,28,30},{17..., dimensions={0} | all-to-all | bytes 393216 | tf_op jit(solution)/shard_map/all_to_all | solution.py:400
  98.1 4.9 %collective-permute-start.4 = (f32[24,512]{1,0:T(8,128)S(1)}, f32[24,512]{1,0:T(8,128)S(1)}, u32[]{:S(2)}, u32[]{:S(2)}) collective-permute-start(f32[24,512]{1,0:T(8,128)S(1)} %bitcast.17), channel_id=1, source_target_pairs={{0,1},{1,0},{2,3},{3,2},{4,5},{5,4},{6,7},{7,6},{8,9},{9,8},{10,11... | collective-permute-start | bytes 147464 | tf_op jit(solution)/shard_map/ppermute | solution.py:402
  103.0 2.2 %pool.1 = bf16[768,896]{1,0:T(8,128)(2,1)} custom-call(bf16[768,768]{1,0:T(8,128)(2,1)S(1)} %get-tuple-element.32.s_ref, bf16[768,1024]{1,0:T(8,128)(2,1)S(1)} %get-tuple-element.33.w_ref, f32[1,896]{1,0:T(1,128)S(1)} %get-tuple-element.34.bias_ref), custom_call_target="tpu_custom_call" | custom-call | flops 1056964608 | bytes 4194304 | tf_op jit(solution)/shard_map/pool/pallas_call | solution.py:255
  105.2 0.0 collective-permute-done.4.across_ref
  105.2 0.8 unpack.1
  (7 shorter events, 0.0 us)
Async XLA Ops:
  0.6 33.1 %copy-start.1 = (s32[1,1536]{1,0:T(1,128)S(1)}, s32[1,1536]{1,0:T(1,128)}, u32[]{:S(2)}) copy-start(s32[1,1536]{1,0:T(1,128)} %bases_ref.1) | copy-start | bytes 18436
  0.6 33.1 %copy-start = (bf16[1,768,896]{2,1,0:T(8,128)(2,1)S(1)}, bf16[1,768,896]{2,1,0:T(8,128)(2,1)}, u32[]{:S(2)}) copy-start(bf16[1,768,896]{2,1,0:T(8,128)(2,1)} %param.13) | copy-start | bytes 4128772
  2.7 14.3 %copy-start.3 = (s32[1,128]{1,0:T(1,128)S(1)}, s32[1,128]{1,0:T(1,128)}, u32[]{:S(2)}) copy-start(s32[1,128]{1,0:T(1,128)} %get-tuple-element.25) | copy-start | bytes 1540
  2.7 17.1 %copy-start.2 = (s32[1,128]{1,0:T(1,128)S(1)}, s32[1,128]{1,0:T(1,128)}, u32[]{:S(2)}) copy-start(s32[1,128]{1,0:T(1,128)} %get-tuple-element.26) | copy-start | bytes 1540
  2.8 34.7 %all-to-all-start = ((bf16[32,24,512]{2,1,0:T(8,128)(2,1)}), bf16[32,24,512]{2,1,0:T(8,128)(2,1)S(1)}, u32[]{:S(2)}, u32[]{:S(2)}) async-start(bf16[32,24,512]{2,1,0:T(8,128)(2,1)} %get-tuple-element.24), calls=%async_computation | async-start | bytes 1572864 | tf_op jit(solution)/shard_map/all_to_all | solution.py:376
  17.1 7.5 %collective-permute-start = (s32[1,128]{1,0:T(1,128)S(1)}, s32[1,128]{1,0:T(1,128)S(1)}, u32[]{:S(2)}, u32[]{:S(2)}) collective-permute-start(s32[1,128]{1,0:T(1,128)S(1)} %copy-done.3), channel_id=1, source_target_pairs={{0,1},{1,0},{2,3},{3,2},{4,5},{5,4},{6,7},{7,6},{8,9},{9,8},{10,11... | collective-permute-start | bytes 1544 | tf_op jit(solution)/shard_map/ppermute | solution.py:374
  19.9 13.8 %collective-permute-start.1 = (s32[1,128]{1,0:T(1,128)S(1)}, s32[1,128]{1,0:T(1,128)S(1)}, u32[]{:S(2)}, u32[]{:S(2)}) collective-permute-start(s32[1,128]{1,0:T(1,128)S(1)} %copy-done.2), channel_id=1, source_target_pairs={{1,2},{2,1},{3,4},{4,3},{5,6},{6,5},{7,8},{8,7},{9,10},{10,9},{11,... | collective-permute-start | bytes 1544 | tf_op jit(solution)/shard_map/ppermute | solution.py:375
  37.4 6.6 %collective-permute-start.2 = (bf16[768,512]{1,0:T(8,128)(2,1)S(1)}, bf16[768,512]{1,0:T(8,128)(2,1)S(1)}, u32[]{:S(2)}, u32[]{:S(2)}) collective-permute-start(bf16[768,512]{1,0:T(8,128)(2,1)S(1)} %bitcast.15), channel_id=1, source_target_pairs={{0,1},{1,0},{2,3},{3,2},{4,5},{5,4},{6,7},{7,6},{8,9},{9,8},{10,11... | collective-permute-start | bytes 2359304 | tf_op jit(solution)/shard_map/ppermute | solution.py:379
  50.2 4.2 %collective-permute-start.3 = (bf16[768,512]{1,0:T(8,128)(2,1)S(1)}, bf16[768,512]{1,0:T(8,128)(2,1)S(1)}, u32[]{:S(2)}, u32[]{:S(2)}) collective-permute-start(bf16[768,512]{1,0:T(8,128)(2,1)S(1)} %get-tuple-element.36), channel_id=1, source_target_pairs={{0,1},{1,0},{2,3},{3,2},{4,5},{5,4},{6,7},{7,6},{8,9},{9,8},{10,11... | collective-permute-start | bytes 2359304 | tf_op jit(solution)/shard_map/ppermute | solution.py:383
  98.1 7.2 %collective-permute-start.4 = (f32[24,512]{1,0:T(8,128)S(1)}, f32[24,512]{1,0:T(8,128)S(1)}, u32[]{:S(2)}, u32[]{:S(2)}) collective-permute-start(f32[24,512]{1,0:T(8,128)S(1)} %bitcast.17), channel_id=1, source_target_pairs={{0,1},{1,0},{2,3},{3,2},{4,5},{5,4},{6,7},{7,6},{8,9},{9,8},{10,11... | collective-permute-start | bytes 147464 | tf_op jit(solution)/shard_map/ppermute | solution.py:402

commit v9 on v8

--- a/solution.py
+++ b/solution.py
@@ -317,24 +317,14 @@
         out_ref[i] = total
 
 
-def unpack_kernel(core_ref, total_ref, across_ref, embed_ref, embed_bias_ref, gain_ref, proj_ref, proj_bias_ref, rows_ref):
+def unpack_kernel(scale, parts_ref, embed_ref, embed_bias_ref, gain_ref, proj_ref, proj_bias_ref, rows_ref):
     kw, block, d1 = embed_ref.shape[0], proj_ref.shape[0], proj_ref.shape[1]
-    half = total_ref.shape[1]
+    half = parts_ref.shape[2]
     taps, per, edge = kw * 4, proj_bias_ref.shape[1], d1 - half
-
-    def place(left_ref, right_ref):
-        proj_ref[:, :half] = left_ref[...]
-        proj_ref[:, half:] = right_ref[:, :edge]
-        rows_ref[:block, :] = right_ref[:, edge:]
-
-    @pl.when(core_ref[0] == 0)
-    def _():
-        place(total_ref, across_ref)
-
-    @pl.when(core_ref[0] != 0)
-    def _():
-        place(across_ref, total_ref)
-
+    right = (parts_ref[1] + parts_ref[3]) * scale
+    proj_ref[:, :half] = (parts_ref[0] + parts_ref[2]) * scale
+    proj_ref[:, half:] = right[:, :edge]
+    rows_ref[:block, :] = right[:, edge:]
     proj_bias_ref[...] = rows_ref[:1, 64:64 + per]
     rows_ref[block:, :] = jnp.zeros((LANES - block, LANES), F32)
     rows_ref[...] = rows_ref[...].T
@@ -396,12 +386,13 @@
             name="add_up",
         )(parts)
 
-    groups = [[i for i in range(members) if i % 2 == c] for c in range(2)]
-    spread = lax.all_to_all(add_up(parts, 1.0, members // 2, BF16), "seq", 0, 0, axis_index_groups=groups, tiled=True)
-    total = add_up(spread, 0.125 / (cotangent.shape[1] * members * shards), 1, F32)[0]
-    across = lax.ppermute(total, "seq", swap)
+    along_x = [list(range(i, members, 4)) for i in range(4)]
+    within = [list(range(i, i + 4)) for i in range(0, members, 4)]
+    spread = lax.all_to_all(add_up(parts, 1.0, members // 4, BF16), "seq", 0, 0, axis_index_groups=along_x, tiled=True)
+    spread = lax.all_to_all(add_up(spread, 1.0, 4, F32), "seq", 0, 0, axis_index_groups=within, tiled=True)
+    scale = 0.125 / (cotangent.shape[1] * members * shards)
     grad_embed, grad_embed_bias, grad_gain, grad_proj, grad_proj_bias = pl.pallas_call(
-        unpack_kernel,
+        functools.partial(unpack_kernel, scale),
         out_shape=(
             jax.ShapeDtypeStruct(embed_weight.shape, F32),
             jax.ShapeDtypeStruct((1, block), F32),
@@ -409,12 +400,12 @@
             jax.ShapeDtypeStruct((block, d1), F32),
             jax.ShapeDtypeStruct((1, per), F32),
         ),
-        in_specs=[SMEM, VMEM, VMEM],
+        in_specs=[VMEM],
         out_specs=(VMEM,) * 5,
         scratch_shapes=[pltpu.VMEM((LANES, LANES), F32)],
         compiler_params=pltpu.CompilerParams(vmem_limit_bytes=4 << 20),
         name="unpack",
-    )(core, total, across)
+    )(spread)
     return (pooled[None], grad_embed, grad_embed_bias[0], grad_gain[0], grad_proj, grad_proj_bias[0])
 
 

time: 107 us -> 113 us (1.056)
  blocking collectives: 43.2 us -> 36.5 us
  waiting for transfers between devices: 14 us -> 18.7 us
  local copies, waits for them, and re-layouts: 0.02 us -> 4.45 us
  starting transfers between devices: 33.6 us -> 36.4 us
    all_to_all x1, blocking collectives: 17.4 us -> 8.47 us  [local(): lax.all_to_all(add_up(parts, 1.0, members // 4, BF16), 'seq', 0, 0, axis_...]
    all_to_all x0 -> x1, starting transfers between devices: none -> 7.74 us  [local(): lax.all_to_all(add_up(spread, 1.0, 4, F32), 'seq', 0, 0, axis_index_group...]
    all_to_all x0 -> x1, waiting for transfers between devices: none -> 6.17 us  [local(): lax.all_to_all(add_up(spread, 1.0, 4, F32), 'seq', 0, 0, axis_index_group...]
    ppermute x1 -> x0, starting transfers between devices: 4.94 us -> none  [local(): across = lax.ppermute(total, 'seq', swap)]
    unnamed x8 -> x18, local copies, waits for them, and re-layouts: 0.02 us -> 4.45 us
    all_to_all x1, blocking collectives: 25.8 us -> 28.1 us  [local(): parts = lax.all_to_all(summed, 'dp', 0, 0, tiled=True)]
    all_to_all x1, waiting for transfers between devices: 1.8 us -> 0.41 us  [local(): lax.all_to_all(piece, 'dp', 0, 0, tiled=True).reshape(shards * block, half)]
  transfers between devices with their start and end apart: 6 -> 6, of which waited for: 4 -> 5; matrix products, arithmetic and copies ran while one was open for 0% -> 0% of each run, Pallas kernels for 5% -> 4%
where the time goes in v9:
time: 113 us; the launch traced here: 112 us
  blocking collectives  36.5 us (32%)
  starting transfers between devices  36.4 us (32%)
  waiting for transfers between devices  18.7 us (17%)
  Pallas kernels  14.9 us (13%)
  local copies, waits for them, and re-layouts  4.45 us (4%)
    all_to_all x1, blocking collectives, local(): parts = lax.all_to_all(summed, 'dp', 0, 0, tiled=True)  28.1 us
    all_to_all x1, starting transfers between devices, local(): lax.all_to_all(piece, 'dp', 0, 0, tiled=True).reshape(shards * block, half)  14.3 us
    ppermute x1, waiting for transfers between devices, local(): outer = lax.ppermute(outer, 'seq', facing)  9.17 us
    all_to_all x1, blocking collectives, local(): lax.all_to_all(add_up(parts, 1.0, members // 4, BF16), 'seq', 0, 0, axis_...  8.47 us
    all_to_all x1, starting transfers between devices, local(): lax.all_to_all(add_up(spread, 1.0, 4, F32), 'seq', 0, 0, axis_index_group...  7.74 us
    pallas_call x1, Pallas kernels, backward(): pl.pallas_call(functools.partial(step_kernel, dims), out_shape=(jax.Shape...  6.34 us
    all_to_all x1, waiting for transfers between devices, local(): lax.all_to_all(add_up(spread, 1.0, 4, F32), 'seq', 0, 0, axis_index_group...  6.17 us
    ppermute x1, starting transfers between devices, local(): other = lax.ppermute(own, 'seq', swap)  4.72 us
  transfers between devices with their start and end apart: 6, of which 5 were waited for; matrix products, arithmetic and copies ran while one was open for 0% of the time, Pallas kernels for 4%

profile of v9, /device:TPU:1, one launch (start us, length us, event | category | flops | bytes accessed | tf_op | source)
XLA Modules:
  0.0 112.1 jit_solution(16568226462399921334)
XLA Ops:
  0.7 2.1 %pack.1 = (bf16[32,24,512]{2,1,0:T(8,128)(2,1)}, s32[1,128]{1,0:T(1,128)}, s32[1,128]{1,0:T(1,128)}) custom-call(s32[1]{0:T(128)} %bitcast.core_ref, s32[1,1536]{1,0:T(1,128)} %bases_ref.1, bf16[15,4,24]{2,1,0:T(4,128)(2,1)} %embed_hbm.1, bf16[1,24]{1,0:T(2,128)(2,1)} %bitcast.18, bf16[1,24]{1,0:T(2,128)(2,1)} %bitcast.19, bf16[24,896]{1,0:T(8,128)(2,1)} %proj_hbm.1, ...), custom_call_target="tpu_custom_call" | custom-call | tf_op jit(solution)/shard_map/pack/pallas_call | solution.py:350
  2.8 14.3 %all-to-all-start = ((bf16[32,24,512]{2,1,0:T(8,128)(2,1)}), bf16[32,24,512]{2,1,0:T(8,128)(2,1)S(1)}, u32[]{:S(2)}, u32[]{:S(2)}) async-start(bf16[32,24,512]{2,1,0:T(8,128)(2,1)} %get-tuple-element.24), calls=%async_computation | async-start | bytes 1572864 | tf_op jit(solution)/shard_map/all_to_all | solution.py:366
  17.1 2.8 %collective-permute-start = (s32[1,128]{1,0:T(1,128)S(1)}, s32[1,128]{1,0:T(1,128)S(1)}, u32[]{:S(2)}, u32[]{:S(2)}) collective-permute-start(s32[1,128]{1,0:T(1,128)S(1)} %copy-done.8), channel_id=1, source_target_pairs={{0,1},{1,0},{2,3},{3,2},{4,5},{5,4},{6,7},{7,6},{8,9},{9,8},{10,11... | collective-permute-start | bytes 1544 | tf_op jit(solution)/shard_map/ppermute | solution.py:364
  19.9 4.7 %collective-permute-start.1 = (s32[1,128]{1,0:T(1,128)S(1)}, s32[1,128]{1,0:T(1,128)S(1)}, u32[]{:S(2)}, u32[]{:S(2)}) collective-permute-start(s32[1,128]{1,0:T(1,128)S(1)} %copy-done.7), channel_id=1, source_target_pairs={{1,2},{2,1},{3,4},{4,3},{5,6},{6,5},{7,8},{8,7},{9,10},{10,9},{11,... | collective-permute-start | bytes 1544 | tf_op jit(solution)/shard_map/ppermute | solution.py:365
  24.6 9.2 %collective-permute-done.1.outer_ref = s32[1,128]{1,0:T(1,128)S(1)} collective-permute-done((s32[1,128]{1,0:T(1,128)S(1)}, s32[1,128]{1,0:T(1,128)S(1)}, u32[]{:S(2)}, u32[]{:S(2)}) %collective-permute-start.1) | collective-permute-done | bytes 544 | tf_op jit(solution)/shard_map/ppermute | solution.py:365
  33.7 1.9 %features.1 = (bf16[128,1536]{1,0:T(8,128)(2,1)S(1)}, f32[32,128]{1,0:T(8,128)S(1)}) custom-call(s32[1]{0:T(128)} %bitcast.core_ref, s32[1,128]{1,0:T(1,128)S(1)} %collective-permute-done.inner_ref, s32[1,1536]{1,0:T(1,128)S(1)} %copy-done.2, s32[1,128]{1,0:T(1,128)S(1)} %collective-permute-done.1.outer_ref, bf16[768,896]{1,0:T(8,128)(2,1)S(1)} %bitcast.11), custom_call_target="tpu_custom_call" | custom-call | flops 603979776 | bytes 2097152 | tf_op jit(solution)/shard_map/features/pallas_call | solution.py:196
  35.6 0.8 copy-done.3
  36.4 0.6 copy-done.5
  37.4 4.7 %collective-permute-start.2 = (bf16[768,512]{1,0:T(8,128)(2,1)S(1)}, bf16[768,512]{1,0:T(8,128)(2,1)S(1)}, u32[]{:S(2)}, u32[]{:S(2)}) collective-permute-start(bf16[768,512]{1,0:T(8,128)(2,1)S(1)} %bitcast.14), channel_id=1, source_target_pairs={{0,1},{1,0},{2,3},{3,2},{4,5},{5,4},{6,7},{7,6},{8,9},{9,8},{10,11... | collective-permute-start | bytes 2359304 | tf_op jit(solution)/shard_map/ppermute | solution.py:369
  42.1 1.9 %collective-permute-done.2.other_ref = bf16[768,512]{1,0:T(8,128)(2,1)S(1)} collective-permute-done((bf16[768,512]{1,0:T(8,128)(2,1)S(1)}, bf16[768,512]{1,0:T(8,128)(2,1)S(1)}, u32[]{:S(2)}, u32[]{:S(2)}) %collective-permute-start.2) | collective-permute-done | bytes 786464 | tf_op jit(solution)/shard_map/ppermute | solution.py:369
  44.0 1.3 %copy-done.1 = bf16[1,768,896]{2,1,0:T(8,128)(2,1)S(1)} copy-done((bf16[1,768,896]{2,1,0:T(8,128)(2,1)S(1)}, bf16[1,768,896]{2,1,0:T(8,128)(2,1)}, u32[]{:S(2)}) %copy-start.1) | copy-done | bytes 1376280
  45.4 1.0 copy-done.4
  46.4 0.7 copy-done.6
  47.1 6.3 %backward.1 = (bf16[768,512]{1,0:T(8,128)(2,1)S(1)}, bf16[768,768]{1,0:T(8,128)(2,1)S(1)}, f32[768,128]{1,0:T(8,128)S(1)}, f32[1,896]{1,0:T(1,128)S(1)}, bf16[768,1024]{1,0:T(8,128)(2,1)S(1)}) custom-call(s32[1]{0:T(128)} %bitcast.core_ref, bf16[128,1536]{1,0:T(8,128)(2,1)S(1)} %copy-done.4, f32[32,128]{1,0:T(8,128)S(1)} %copy-done.6, ...), custom_call_target="tpu_custom_call" | custom-call | flops 3170893824 | bytes 6291456 | tf_op jit(solution)/shard_map/backward/pallas_call | solution.py:213
  53.4 2.2 %collective-permute-start.3 = (bf16[768,512]{1,0:T(8,128)(2,1)S(1)}, bf16[768,512]{1,0:T(8,128)(2,1)S(1)}, u32[]{:S(2)}, u32[]{:S(2)}) collective-permute-start(bf16[768,512]{1,0:T(8,128)(2,1)S(1)} %get-tuple-element.36), channel_id=1, source_target_pairs={{0,1},{1,0},{2,3},{3,2},{4,5},{5,4},{6,7},{7,6},{8,9},{9,8},{10,11... | collective-permute-start | bytes 2359304 | tf_op jit(solution)/shard_map/ppermute | solution.py:373
  55.7 0.8 keep_half.1
  56.5 1.1 collective-permute-done.3
  57.9 28.1 %all_to_all.20.in_ref = bf16[32,24,512]{2,1,0:T(8,128)(2,1)S(1)} all-to-all(bf16[32,24,512]{2,1,0:T(8,128)(2,1)S(1)} %bitcast.16), channel_id=1, replica_groups=mesh['dp'=32,'seq'=16] {'dp'}, dimensions={0} | all-to-all | bytes 1572864 | tf_op jit(solution)/shard_map/all_to_all | solution.py:377
  86.0 8.5 %all_to_all.21.in_ref = bf16[4,24,512]{2,1,0:T(8,128)(2,1)S(1)} all-to-all(bf16[4,24,512]{2,1,0:T(8,128)(2,1)S(1)} %add_up.2), channel_id=1, replica_groups={{0,4,8,12},{1,5,9,13},{2,6,10,14},{3,7,11,15},{16,20,24,28},{17,21,25,2..., dimensions={0} | all-to-all | bytes 196608 | tf_op jit(solution)/shard_map/all_to_all | solution.py:391
  94.5 0.7 add_up.3
  95.2 7.7 %all-to-all-start.3 = ((f32[4,24,512]{2,1,0:T(8,128)}), f32[4,24,512]{2,1,0:T(8,128)S(1)}, u32[]{:S(2)}, u32[]{:S(2)}) async-start(f32[4,24,512]{2,1,0:T(8,128)} %add_up.3), calls=%async_computation.3 | async-start | bytes 393216 | tf_op jit(solution)/shard_map/all_to_all | solution.py:392
  102.9 2.2 %pool.1 = bf16[768,896]{1,0:T(8,128)(2,1)} custom-call(bf16[768,768]{1,0:T(8,128)(2,1)S(1)} %get-tuple-element.32.s_ref, bf16[768,1024]{1,0:T(8,128)(2,1)S(1)} %get-tuple-element.33.w_ref, f32[1,896]{1,0:T(1,128)S(1)} %get-tuple-element.34.bias_ref), custom_call_target="tpu_custom_call" | custom-call | flops 1056964608 | bytes 4194304 | tf_op jit(solution)/shard_map/pool/pallas_call | solution.py:255
  105.2 6.2 %all-to-all-done.3.parts_ref = f32[4,24,512]{2,1,0:T(8,128)S(1)} async-done(((f32[4,24,512]{2,1,0:T(8,128)}), f32[4,24,512]{2,1,0:T(8,128)S(1)}, u32[]{:S(2)}, u32[]{:S(2)}) %all-to-all-start.3) | async-done | bytes 196640 | tf_op jit(solution)/shard_map/all_to_all | solution.py:392
  111.3 0.7 unpack.1
  (17 shorter events, 0.8 us)
Async XLA Ops:
  0.6 33.1 %copy-start.2 = (s32[1,1536]{1,0:T(1,128)S(1)}, s32[1,1536]{1,0:T(1,128)}, u32[]{:S(2)}) copy-start(s32[1,1536]{1,0:T(1,128)} %bases_ref.1) | copy-start | bytes 18436
  0.6 33.1 %copy-start = (bf16[1,768,896]{2,1,0:T(8,128)(2,1)S(1)}, bf16[1,768,896]{2,1,0:T(8,128)(2,1)}, u32[]{:S(2)}) copy-start(bf16[1,768,896]{2,1,0:T(8,128)(2,1)} %param.13) | copy-start | bytes 4128772
  2.7 14.3 %copy-start.8 = (s32[1,128]{1,0:T(1,128)S(1)}, s32[1,128]{1,0:T(1,128)}, u32[]{:S(2)}) copy-start(s32[1,128]{1,0:T(1,128)} %get-tuple-element.25) | copy-start | bytes 1540
  2.7 17.1 %copy-start.7 = (s32[1,128]{1,0:T(1,128)S(1)}, s32[1,128]{1,0:T(1,128)}, u32[]{:S(2)}) copy-start(s32[1,128]{1,0:T(1,128)} %get-tuple-element.26) | copy-start | bytes 1540
  2.8 34.7 %all-to-all-start = ((bf16[32,24,512]{2,1,0:T(8,128)(2,1)}), bf16[32,24,512]{2,1,0:T(8,128)(2,1)S(1)}, u32[]{:S(2)}, u32[]{:S(2)}) async-start(bf16[32,24,512]{2,1,0:T(8,128)(2,1)} %get-tuple-element.24), calls=%async_computation | async-start | bytes 1572864 | tf_op jit(solution)/shard_map/all_to_all | solution.py:366
  17.1 7.5 %collective-permute-start = (s32[1,128]{1,0:T(1,128)S(1)}, s32[1,128]{1,0:T(1,128)S(1)}, u32[]{:S(2)}, u32[]{:S(2)}) collective-permute-start(s32[1,128]{1,0:T(1,128)S(1)} %copy-done.8), channel_id=1, source_target_pairs={{0,1},{1,0},{2,3},{3,2},{4,5},{5,4},{6,7},{7,6},{8,9},{9,8},{10,11... | collective-permute-start | bytes 1544 | tf_op jit(solution)/shard_map/ppermute | solution.py:364
  19.9 13.8 %collective-permute-start.1 = (s32[1,128]{1,0:T(1,128)S(1)}, s32[1,128]{1,0:T(1,128)S(1)}, u32[]{:S(2)}, u32[]{:S(2)}) collective-permute-start(s32[1,128]{1,0:T(1,128)S(1)} %copy-done.7), channel_id=1, source_target_pairs={{1,2},{2,1},{3,4},{4,3},{5,6},{6,5},{7,8},{8,7},{9,10},{10,9},{11,... | collective-permute-start | bytes 1544 | tf_op jit(solution)/shard_map/ppermute | solution.py:365
  35.6 0.8 copy-start.3
  36.4 0.6 copy-start.5
  37.4 6.6 %collective-permute-start.2 = (bf16[768,512]{1,0:T(8,128)(2,1)S(1)}, bf16[768,512]{1,0:T(8,128)(2,1)S(1)}, u32[]{:S(2)}, u32[]{:S(2)}) collective-permute-start(bf16[768,512]{1,0:T(8,128)(2,1)S(1)} %bitcast.14), channel_id=1, source_target_pairs={{0,1},{1,0},{2,3},{3,2},{4,5},{5,4},{6,7},{7,6},{8,9},{9,8},{10,11... | collective-permute-start | bytes 2359304 | tf_op jit(solution)/shard_map/ppermute | solution.py:369
  44.0 1.3 %copy-start.1 = (bf16[1,768,896]{2,1,0:T(8,128)(2,1)S(1)}, bf16[1,768,896]{2,1,0:T(8,128)(2,1)}, u32[]{:S(2)}) copy-start(bf16[1,768,896]{2,1,0:T(8,128)(2,1)} %param.13) | copy-start | bytes 4128772
  45.4 1.0 copy-start.4
  46.4 0.7 copy-start.6
  53.4 4.2 %collective-permute-start.3 = (bf16[768,512]{1,0:T(8,128)(2,1)S(1)}, bf16[768,512]{1,0:T(8,128)(2,1)S(1)}, u32[]{:S(2)}, u32[]{:S(2)}) collective-permute-start(bf16[768,512]{1,0:T(8,128)(2,1)S(1)} %get-tuple-element.36), channel_id=1, source_target_pairs={{0,1},{1,0},{2,3},{3,2},{4,5},{5,4},{6,7},{7,6},{8,9},{9,8},{10,11... | collective-permute-start | bytes 2359304 | tf_op jit(solution)/shard_map/ppermute | solution.py:373
  95.2 16.1 %all-to-all-start.3 = ((f32[4,24,512]{2,1,0:T(8,128)}), f32[4,24,512]{2,1,0:T(8,128)S(1)}, u32[]{:S(2)}, u32[]{:S(2)}) async-start(f32[4,24,512]{2,1,0:T(8,128)} %add_up.3), calls=%async_computation.3 | async-start | bytes 393216 | tf_op jit(solution)/shard_map/all_to_all | solution.py:392

commit v10 on v8

--- a/solution.py
+++ b/solution.py
@@ -396,7 +396,7 @@
             name="add_up",
         )(parts)
 
-    groups = [[i for i in range(members) if i % 2 == c] for c in range(2)]
+    groups = [[i + high for high in (0, 2) for i in range(c, members, 4)] for c in range(2)]
     spread = lax.all_to_all(add_up(parts, 1.0, members // 2, BF16), "seq", 0, 0, axis_index_groups=groups, tiled=True)
     total = add_up(spread, 0.125 / (cotangent.shape[1] * members * shards), 1, F32)[0]
     across = lax.ppermute(total, "seq", swap)

time: 107 us -> 106 us (level)
  no operation moved by 1% of the time
where the time goes in v10:
time: 106 us
  blocking collectives  43.2 us (41%)
  starting transfers between devices  33.6 us (32%)
  Pallas kernels  14.1 us (13%)
  waiting for transfers between devices  14 us (13%)
    all_to_all x1, blocking collectives, local(): parts = lax.all_to_all(summed, 'dp', 0, 0, tiled=True)  25.8 us
    all_to_all x1, blocking collectives, local(): lax.all_to_all(add_up(parts, 1.0, members // 2, BF16), 'seq', 0, 0, axis_...  17.4 us
    all_to_all x1, starting transfers between devices, local(): lax.all_to_all(piece, 'dp', 0, 0, tiled=True).reshape(shards * block, half)  14.3 us
    ppermute x1, waiting for transfers between devices, local(): outer = lax.ppermute(outer, 'seq', facing)  9.17 us
    pallas_call x1, Pallas kernels, backward(): pl.pallas_call(functools.partial(step_kernel, dims), out_shape=(jax.Shape...  6.21 us
    ppermute x1, starting transfers between devices, local(): across = lax.ppermute(total, 'seq', swap)  4.94 us
    ppermute x1, starting transfers between devices, local(): other = lax.ppermute(own, 'seq', swap)  4.72 us
    ppermute x1, starting transfers between devices, local(): outer = lax.ppermute(outer, 'seq', facing)  4.65 us
  transfers between devices with their start and end apart: 6, of which 4 were waited for; matrix products, arithmetic and copies ran while one was open for 0% of the time, Pallas kernels for 5%

profile of v10, /device:TPU:1, one launch (start us, length us, event | category | flops | bytes accessed | tf_op | source)
XLA Modules:
  0.0 106.0 jit_solution(3815694530561856454)
XLA Ops:
  0.7 2.1 %pack.1 = (bf16[32,24,512]{2,1,0:T(8,128)(2,1)}, s32[1,128]{1,0:T(1,128)}, s32[1,128]{1,0:T(1,128)}) custom-call(s32[1]{0:T(128)} %bitcast.core_ref, s32[1,1536]{1,0:T(1,128)} %bases_ref.1, bf16[15,4,24]{2,1,0:T(4,128)(2,1)} %embed_hbm.1, bf16[1,24]{1,0:T(2,128)(2,1)} %bitcast.21, bf16[1,24]{1,0:T(2,128)(2,1)} %bitcast.22, bf16[24,896]{1,0:T(8,128)(2,1)} %proj_hbm.1, ...), custom_call_target="tpu_custom_call" | custom-call | tf_op jit(solution)/shard_map/pack/pallas_call | solution.py:360
  2.7 0.0 copy-start.3
  2.7 0.0 copy-start.2
  2.8 14.3 %all-to-all-start = ((bf16[32,24,512]{2,1,0:T(8,128)(2,1)}), bf16[32,24,512]{2,1,0:T(8,128)(2,1)S(1)}, u32[]{:S(2)}, u32[]{:S(2)}) async-start(bf16[32,24,512]{2,1,0:T(8,128)(2,1)} %get-tuple-element.24), calls=%async_computation | async-start | bytes 1572864 | tf_op jit(solution)/shard_map/all_to_all | solution.py:376
  17.1 2.8 %collective-permute-start = (s32[1,128]{1,0:T(1,128)S(1)}, s32[1,128]{1,0:T(1,128)S(1)}, u32[]{:S(2)}, u32[]{:S(2)}) collective-permute-start(s32[1,128]{1,0:T(1,128)S(1)} %copy-done.3), channel_id=1, source_target_pairs={{0,1},{1,0},{2,3},{3,2},{4,5},{5,4},{6,7},{7,6},{8,9},{9,8},{10,11... | collective-permute-start | bytes 1544 | tf_op jit(solution)/shard_map/ppermute | solution.py:374
  19.9 4.7 %collective-permute-start.1 = (s32[1,128]{1,0:T(1,128)S(1)}, s32[1,128]{1,0:T(1,128)S(1)}, u32[]{:S(2)}, u32[]{:S(2)}) collective-permute-start(s32[1,128]{1,0:T(1,128)S(1)} %copy-done.2), channel_id=1, source_target_pairs={{1,2},{2,1},{3,4},{4,3},{5,6},{6,5},{7,8},{8,7},{9,10},{10,9},{11,... | collective-permute-start | bytes 1544 | tf_op jit(solution)/shard_map/ppermute | solution.py:375
  24.5 0.0 collective-permute-done.inner_ref
  24.6 9.2 %collective-permute-done.1.outer_ref = s32[1,128]{1,0:T(1,128)S(1)} collective-permute-done((s32[1,128]{1,0:T(1,128)S(1)}, s32[1,128]{1,0:T(1,128)S(1)}, u32[]{:S(2)}, u32[]{:S(2)}) %collective-permute-start.1) | collective-permute-done | bytes 544 | tf_op jit(solution)/shard_map/ppermute | solution.py:375
  33.7 1.9 %features.1 = (bf16[128,1536]{1,0:T(8,128)(2,1)S(1)}, f32[32,128]{1,0:T(8,128)S(1)}) custom-call(s32[1]{0:T(128)} %bitcast.core_ref, s32[1,128]{1,0:T(1,128)S(1)} %collective-permute-done.inner_ref, s32[1,1536]{1,0:T(1,128)S(1)} %copy-done.1, s32[1,128]{1,0:T(1,128)S(1)} %collective-permute-done.1.outer_ref, bf16[768,896]{1,0:T(8,128)(2,1)S(1)} %bitcast.12), custom_call_target="tpu_custom_call" | custom-call | flops 603979776 | bytes 2097152 | tf_op jit(solution)/shard_map/features/pallas_call | solution.py:196
  35.6 1.8 %all-to-all-done = bf16[32,24,512]{2,1,0:T(8,128)(2,1)S(1)} async-done(((bf16[32,24,512]{2,1,0:T(8,128)(2,1)}), bf16[32,24,512]{2,1,0:T(8,128)(2,1)S(1)}, u32[]{:S(2)}, u32[]{:S(2)}) %all-to-all-start) | async-done | bytes 786464 | tf_op jit(solution)/shard_map/all_to_all | solution.py:376
  37.4 4.7 %collective-permute-start.2 = (bf16[768,512]{1,0:T(8,128)(2,1)S(1)}, bf16[768,512]{1,0:T(8,128)(2,1)S(1)}, u32[]{:S(2)}, u32[]{:S(2)}) collective-permute-start(bf16[768,512]{1,0:T(8,128)(2,1)S(1)} %bitcast.15), channel_id=1, source_target_pairs={{0,1},{1,0},{2,3},{3,2},{4,5},{5,4},{6,7},{7,6},{8,9},{9,8},{10,11... | collective-permute-start | bytes 2359304 | tf_op jit(solution)/shard_map/ppermute | solution.py:379
  42.1 1.9 %collective-permute-done.2.other_ref = bf16[768,512]{1,0:T(8,128)(2,1)S(1)} collective-permute-done((bf16[768,512]{1,0:T(8,128)(2,1)S(1)}, bf16[768,512]{1,0:T(8,128)(2,1)S(1)}, u32[]{:S(2)}, u32[]{:S(2)}) %collective-permute-start.2) | collective-permute-done | bytes 786464 | tf_op jit(solution)/shard_map/ppermute | solution.py:379
  44.0 6.2 %backward.1 = (bf16[768,512]{1,0:T(8,128)(2,1)S(1)}, bf16[768,768]{1,0:T(8,128)(2,1)S(1)}, f32[768,128]{1,0:T(8,128)S(1)}, f32[1,896]{1,0:T(1,128)S(1)}, bf16[768,1024]{1,0:T(8,128)(2,1)S(1)}) custom-call(s32[1]{0:T(128)} %bitcast.core_ref, bf16[128,1536]{1,0:T(8,128)(2,1)S(1)} %get-tuple-element.29.feat_ref, f32[32,128]{1,0:T(8,128)S(1)} %get-tuple-element.30.sums_ref, ...), custom_call_target="tpu_custom_call" | custom-call | flops 3170893824 | bytes 6291456 | tf_op jit(solution)/shard_map/backward/pallas_call | solution.py:213
  50.2 2.2 %collective-permute-start.3 = (bf16[768,512]{1,0:T(8,128)(2,1)S(1)}, bf16[768,512]{1,0:T(8,128)(2,1)S(1)}, u32[]{:S(2)}, u32[]{:S(2)}) collective-permute-start(bf16[768,512]{1,0:T(8,128)(2,1)S(1)} %get-tuple-element.36), channel_id=1, source_target_pairs={{0,1},{1,0},{2,3},{3,2},{4,5},{5,4},{6,7},{7,6},{8,9},{9,8},{10,11... | collective-permute-start | bytes 2359304 | tf_op jit(solution)/shard_map/ppermute | solution.py:383
  52.5 0.8 keep_half.1
  53.3 1.1 %collective-permute-done.3 = bf16[768,512]{1,0:T(8,128)(2,1)S(1)} collective-permute-done((bf16[768,512]{1,0:T(8,128)(2,1)S(1)}, bf16[768,512]{1,0:T(8,128)(2,1)S(1)}, u32[]{:S(2)}, u32[]{:S(2)}) %collective-permute-start.3) | collective-permute-done | bytes 786464 | tf_op jit(solution)/shard_map/ppermute | solution.py:383
  54.4 0.3 add_convert_fusion
  54.7 25.8 %all_to_all.15.in_ref = bf16[32,24,512]{2,1,0:T(8,128)(2,1)S(1)} all-to-all(bf16[32,24,512]{2,1,0:T(8,128)(2,1)S(1)} %bitcast.19), channel_id=1, replica_groups=mesh['dp'=32,'seq'=16] {'dp'}, dimensions={0} | all-to-all | bytes 1572864 | tf_op jit(solution)/shard_map/all_to_all | solution.py:387
  80.5 0.1 add_up.2
  80.6 17.4 %all_to_all.16.in_ref = bf16[8,24,512]{2,1,0:T(8,128)(2,1)S(1)} all-to-all(bf16[8,24,512]{2,1,0:T(8,128)(2,1)S(1)} %add_up.2), channel_id=1, replica_groups={{0,4,8,12,2,6,10,14},{1,5,9,13,3,7,11,15},{16,20,24,28,18,22,26,30},{17..., dimensions={0} | all-to-all | bytes 393216 | tf_op jit(solution)/shard_map/all_to_all | solution.py:400
  98.0 4.9 %collective-permute-start.4 = (f32[24,512]{1,0:T(8,128)S(1)}, f32[24,512]{1,0:T(8,128)S(1)}, u32[]{:S(2)}, u32[]{:S(2)}) collective-permute-start(f32[24,512]{1,0:T(8,128)S(1)} %bitcast.17), channel_id=1, source_target_pairs={{0,1},{1,0},{2,3},{3,2},{4,5},{5,4},{6,7},{7,6},{8,9},{9,8},{10,11... | collective-permute-start | bytes 147464 | tf_op jit(solution)/shard_map/ppermute | solution.py:402
  103.0 2.2 %pool.1 = bf16[768,896]{1,0:T(8,128)(2,1)} custom-call(bf16[768,768]{1,0:T(8,128)(2,1)S(1)} %get-tuple-element.32.s_ref, bf16[768,1024]{1,0:T(8,128)(2,1)S(1)} %get-tuple-element.33.w_ref, f32[1,896]{1,0:T(1,128)S(1)} %get-tuple-element.34.bias_ref), custom_call_target="tpu_custom_call" | custom-call | flops 1056964608 | bytes 4194304 | tf_op jit(solution)/shard_map/pool/pallas_call | solution.py:255
  105.2 0.0 collective-permute-done.4.across_ref
  105.2 0.8 unpack.1
  (7 shorter events, 0.0 us)
Async XLA Ops:
  0.6 33.1 %copy-start.1 = (s32[1,1536]{1,0:T(1,128)S(1)}, s32[1,1536]{1,0:T(1,128)}, u32[]{:S(2)}) copy-start(s32[1,1536]{1,0:T(1,128)} %bases_ref.1) | copy-start | bytes 18436
  0.6 33.1 %copy-start = (bf16[1,768,896]{2,1,0:T(8,128)(2,1)S(1)}, bf16[1,768,896]{2,1,0:T(8,128)(2,1)}, u32[]{:S(2)}) copy-start(bf16[1,768,896]{2,1,0:T(8,128)(2,1)} %param.13) | copy-start | bytes 4128772
  2.7 14.3 %copy-start.3 = (s32[1,128]{1,0:T(1,128)S(1)}, s32[1,128]{1,0:T(1,128)}, u32[]{:S(2)}) copy-start(s32[1,128]{1,0:T(1,128)} %get-tuple-element.25) | copy-start | bytes 1540
  2.7 17.1 %copy-start.2 = (s32[1,128]{1,0:T(1,128)S(1)}, s32[1,128]{1,0:T(1,128)}, u32[]{:S(2)}) copy-start(s32[1,128]{1,0:T(1,128)} %get-tuple-element.26) | copy-start | bytes 1540
  2.8 34.7 %all-to-all-start = ((bf16[32,24,512]{2,1,0:T(8,128)(2,1)}), bf16[32,24,512]{2,1,0:T(8,128)(2,1)S(1)}, u32[]{:S(2)}, u32[]{:S(2)}) async-start(bf16[32,24,512]{2,1,0:T(8,128)(2,1)} %get-tuple-element.24), calls=%async_computation | async-start | bytes 1572864 | tf_op jit(solution)/shard_map/all_to_all | solution.py:376
  17.1 7.5 %collective-permute-start = (s32[1,128]{1,0:T(1,128)S(1)}, s32[1,128]{1,0:T(1,128)S(1)}, u32[]{:S(2)}, u32[]{:S(2)}) collective-permute-start(s32[1,128]{1,0:T(1,128)S(1)} %copy-done.3), channel_id=1, source_target_pairs={{0,1},{1,0},{2,3},{3,2},{4,5},{5,4},{6,7},{7,6},{8,9},{9,8},{10,11... | collective-permute-start | bytes 1544 | tf_op jit(solution)/shard_map/ppermute | solution.py:374
  19.9 13.8 %collective-permute-start.1 = (s32[1,128]{1,0:T(1,128)S(1)}, s32[1,128]{1,0:T(1,128)S(1)}, u32[]{:S(2)}, u32[]{:S(2)}) collective-permute-start(s32[1,128]{1,0:T(1,128)S(1)} %copy-done.2), channel_id=1, source_target_pairs={{1,2},{2,1},{3,4},{4,3},{5,6},{6,5},{7,8},{8,7},{9,10},{10,9},{11,... | collective-permute-start | bytes 1544 | tf_op jit(solution)/shard_map/ppermute | solution.py:375
  37.4 6.6 %collective-permute-start.2 = (bf16[768,512]{1,0:T(8,128)(2,1)S(1)}, bf16[768,512]{1,0:T(8,128)(2,1)S(1)}, u32[]{:S(2)}, u32[]{:S(2)}) collective-permute-start(bf16[768,512]{1,0:T(8,128)(2,1)S(1)} %bitcast.15), channel_id=1, source_target_pairs={{0,1},{1,0},{2,3},{3,2},{4,5},{5,4},{6,7},{7,6},{8,9},{9,8},{10,11... | collective-permute-start | bytes 2359304 | tf_op jit(solution)/shard_map/ppermute | solution.py:379
  50.2 4.2 %collective-permute-start.3 = (bf16[768,512]{1,0:T(8,128)(2,1)S(1)}, bf16[768,512]{1,0:T(8,128)(2,1)S(1)}, u32[]{:S(2)}, u32[]{:S(2)}) collective-permute-start(bf16[768,512]{1,0:T(8,128)(2,1)S(1)} %get-tuple-element.36), channel_id=1, source_target_pairs={{0,1},{1,0},{2,3},{3,2},{4,5},{5,4},{6,7},{7,6},{8,9},{9,8},{10,11... | collective-permute-start | bytes 2359304 | tf_op jit(solution)/shard_map/ppermute | solution.py:383
  98.0 7.2 %collective-permute-start.4 = (f32[24,512]{1,0:T(8,128)S(1)}, f32[24,512]{1,0:T(8,128)S(1)}, u32[]{:S(2)}, u32[]{:S(2)}) collective-permute-start(f32[24,512]{1,0:T(8,128)S(1)} %bitcast.17), channel_id=1, source_target_pairs={{0,1},{1,0},{2,3},{3,2},{4,5},{5,4},{6,7},{7,6},{8,9},{9,8},{10,11... | collective-permute-start | bytes 147464 | tf_op jit(solution)/shard_map/ppermute | solution.py:402
